TPU v7x, 128 devices: a whole 4x4x4 slice. The times are simulated.
128 devices in a mesh: ctx: 32 (over y, z, core), head: 4 (over x).
Axes of the slice: x: 4, y: 4, z: 4, core: 2. Of those that a mesh axis runs over, the one named last changes fastest.
Arguments:
- stream: bfloat16 [16384, 2048], P(('ctx', 'head')), may hold values from -6 to 6
- moe_gain: float32 [2048], replicated, may hold values from 0.5 to 1.5
- router: bfloat16 [2048, 256], replicated, may hold values from -0.125 to 0.125
- expert_ids: int32 [16384, 10], P(('ctx', 'head')), may hold values from 0 to 255, all different within a row; in each aligned block of 128 rows (0 to 127, 128 to 255, ...) at most 6 rows name the same one
- expert_gate: bfloat16 [256, 2048, 512], P(('ctx', 'head')), may hold values from -0.125 to 0.125
- expert_up: bfloat16 [256, 2048, 512], P(('ctx', 'head')), may hold values from -0.125 to 0.125
- expert_down: bfloat16 [256, 512, 2048], P(('ctx', 'head')), may hold values from -1 to 1
- mixer_gain: float32 [2048], replicated, may hold values from 0.5 to 1.5
- query_weight: bfloat16 [2048, 1024], P(None, 'head'), may hold values from -0.125 to 0.125
- key_weight: bfloat16 [2048, 1024], P(None, 'head'), may hold values from -0.125 to 0.125
- value_weight: bfloat16 [2048, 2048], P(None, 'head'), may hold values from -0.125 to 0.125
- output_gate: bfloat16 [2048, 2048], P(None, 'head'), may hold values from -0.125 to 0.125
- beta_weight: bfloat16 [2048, 16], P(None, 'head'), may hold values from -0.125 to 0.125
- decay_weight: bfloat16 [2048, 16], P(None, 'head'), may hold values from -0.5 to 0.5
- query_conv: float32 [4, 1024], P(None, 'head'), may hold values from -3 to 3
- key_conv: float32 [4, 1024], P(None, 'head'), may hold values from -3 to 3
- value_conv: float32 [4, 2048], P(None, 'head'), may hold values from -3 to 3
- decay_log: float32 [16], P('head'), may hold values from -12 to -2.5
- decay_bias: float32 [16], P('head'), may hold values from -2 to 1
- head_gain: float32 [128], replicated, may hold values from 0.5 to 1.5
- out_weight: bfloat16 [2048, 2048], P('head'), may hold values from -0.125 to 0.125
Outputs:
- moe_out: bfloat16 [16384, 2048], P(('ctx', 'head'))
- mixer_out: bfloat16 [16384, 2048], P(('ctx', 'head'))
Inputs may be any that keep to these rules, and one draw needn't show every extreme that they name: `expert_ids`: each row names 10 different experts; in each aligned block of 128 rows (the rows of one device) no expert is named by more than 6 rows, a bound that some block reaches.
All inputs are finite; a program needn't handle non-finite values.
Results may differ from a plain program's by a relative error of at most 0.017.
Values may be sent and summed in bfloat16 or wider, within the bound.
A program may use at most 128 MiB of HBM per device.

v0:
```python
import math

import jax
import jax.numpy as jnp
from jax import lax
from jax.sharding import PartitionSpec as P

DK = 128


epsilon = 1e-06
exact_precision = lax.Precision.HIGHEST


def passed_along(value, axis, steps):
    count = lax.axis_size(axis)
    first, last = (max(0, -steps), min(count, count - steps))
    return lax.ppermute(value, axis, [(source, source + steps) for source in range(first, last)])


def prefix(array, axis, combine, identity):
    peers, place = (lax.axis_size(axis), lax.axis_index(axis))
    everything = jax.tree.map(
        lambda part, kind: lax.all_gather(part.astype(kind), axis),
        array,
        (jnp.bfloat16, jnp.bfloat16),
    )
    start = jax.tree.map(
        lambda part, zero: jnp.broadcast_to(jnp.asarray(zero, part.dtype), part.shape),
        array,
        identity,
    )

    def step(k, before):
        reached = k < place
        new = combine(
            before, jax.tree.map(lambda part, own: part[k].astype(own.dtype), everything, array)
        )
        return jax.tree.map(lambda a, b: jnp.where(reached, a, b), new, before)

    return lax.fori_loop(0, peers, step, start)


def rms_rows(values, gain):
    values = values.astype(jnp.float32)
    scale = lax.rsqrt(jnp.mean(values * values, axis=-1, keepdims=True) + epsilon)
    return values * scale * gain


def block_terms(queries, key_rows, values, strength, decays):
    length = queries.shape[0]
    cumulative = jnp.cumsum(decays)
    spread = cumulative[:, None] - cumulative[None, :]
    positions = jnp.arange(length, dtype=jnp.int32)
    strict = positions[:, None] > positions[None, :]
    inclusive = positions[:, None] >= positions[None, :]
    fall_strict = jnp.where(strict, jnp.exp(jnp.where(strict, spread, 0.0)), 0.0)
    fall_inclusive = jnp.where(inclusive, jnp.exp(jnp.where(inclusive, spread, 0.0)), 0.0)
    key_dots = jnp.dot(key_rows, key_rows.T, precision=exact_precision)
    strict_part = strength[:, None] * fall_strict * key_dots
    system = jnp.eye(length, dtype=jnp.float32) + strict_part
    targets = strength[:, None] * jnp.concatenate(
        [values, jnp.exp(cumulative)[:, None] * key_rows], axis=1
    )
    solved = jax.scipy.linalg.solve_triangular(system, targets, lower=True, unit_diagonal=True)
    value_width = values.shape[1]
    w_values = solved[:, :value_width]
    w_keys = solved[:, value_width:]
    mixing = fall_inclusive * jnp.dot(queries, key_rows.T, precision=exact_precision)
    q_decayed = jnp.exp(cumulative)[:, None] * queries
    k_decayed = jnp.exp(cumulative[-1] - cumulative)[:, None] * key_rows
    closing = jnp.exp(cumulative[-1])
    return (w_values, w_keys, mixing, q_decayed, k_decayed, closing)


def local_pass(queries, key_rows, values, strength, decays):
    length = queries.shape[0]
    block_len = math.gcd(length, 64)
    block_count = length // block_len

    def split_blocks(array):
        return array.reshape((block_count, block_len) + array.shape[1:])

    terms = jax.vmap(block_terms)(
        split_blocks(queries),
        split_blocks(key_rows),
        split_blocks(values),
        split_blocks(strength),
        split_blocks(decays),
    )

    def advance(carried_pair, block_term):
        state_now, transfer = carried_pair
        w_values, w_keys, mixing, q_decayed, k_decayed, closing = block_term
        update = w_values - jnp.dot(w_keys, state_now, precision=exact_precision)
        result = jnp.dot(q_decayed, state_now, precision=exact_precision) + jnp.dot(
            mixing, update, precision=exact_precision
        )
        moved_rows = jnp.dot(w_keys, transfer, precision=exact_precision)
        reading = jnp.dot(q_decayed, transfer, precision=exact_precision) - jnp.dot(
            mixing, moved_rows, precision=exact_precision
        )
        state_now = closing * state_now + jnp.dot(k_decayed.T, update, precision=exact_precision)
        transfer = closing * transfer - jnp.dot(k_decayed.T, moved_rows, precision=exact_precision)
        return ((state_now, transfer), (result, reading))

    key_width = key_rows.shape[1]
    initial = (
        jnp.zeros((key_width, values.shape[1]), jnp.float32),
        jnp.eye(key_width, dtype=jnp.float32),
    )
    (state_now, transfer), (results, read_values) = lax.scan(advance, initial, terms)
    return (results.reshape(length, -1), read_values.reshape(length, -1), transfer, state_now)


def unit_heads(array, heads):
    reshaped_rows = array.reshape(array.shape[0], heads, -1)
    return reshaped_rows * lax.rsqrt(
        jnp.sum(reshaped_rows * reshaped_rows, axis=-1, keepdims=True) + epsilon
    )


def on_device(
    stream,
    moe_gain,
    router,
    expert_ids,
    expert_gate,
    expert_up,
    expert_down,
    mixer_gain,
    query_weight,
    key_weight,
    value_weight,
    output_gate,
    beta_weight,
    decay_weight,
    query_conv,
    key_conv,
    value_conv,
    decay_log,
    decay_bias,
    head_gain,
    out_weight,
):
    ctx_count = lax.axis_size("ctx")
    head_count = lax.axis_size("head")
    sources = ctx_count * head_count
    tok_rows, model_width = stream.shape
    top_count = expert_ids.shape[1]
    local_experts = expert_gate.shape[0]
    experts_all = local_experts * sources
    capacity = (11 * tok_rows * top_count + 10 * experts_all - 1) // (10 * experts_all)
    normed = rms_rows(stream, moe_gain).astype(jnp.bfloat16)
    logits = jnp.dot(normed, router, preferred_element_type=jnp.float32)
    chosen = jnp.take_along_axis(logits, expert_ids, axis=1)
    raised = jnp.exp(chosen)
    weights = raised / jnp.sum(raised, axis=1, keepdims=True)
    flat_ids = expert_ids.reshape(-1)
    matches = (flat_ids[:, None] == jnp.arange(experts_all, dtype=jnp.int32)[None, :]).astype(
        jnp.int32
    )
    slot_index = jnp.sum((jnp.cumsum(matches, axis=0) - 1) * matches, axis=1)
    places = flat_ids * capacity + slot_index
    token_rows = jnp.arange(tok_rows * top_count, dtype=jnp.int32) // top_count
    outgoing = (
        jnp.zeros((experts_all * capacity, model_width), jnp.bfloat16)
        .at[places]
        .set(normed[token_rows])
    )
    outgoing = outgoing.reshape(sources, local_experts, capacity, model_width)
    received = lax.all_to_all(outgoing, ("ctx", "head"), split_axis=0, concat_axis=0, tiled=True)
    gate_part = jnp.einsum(
        "nesd,edh->nesh", received, expert_gate, preferred_element_type=jnp.float32
    )
    up_part = jnp.einsum("nesd,edh->nesh", received, expert_up, preferred_element_type=jnp.float32)
    hidden = (jax.nn.silu(gate_part) * up_part).astype(jnp.bfloat16)
    returned = lax.all_to_all(
        jnp.einsum(
            "nesh,ehd->nesd", hidden, expert_down, preferred_element_type=jnp.float32
        ).astype(jnp.bfloat16),
        ("ctx", "head"),
        split_axis=0,
        concat_axis=0,
        tiled=True,
    )
    gathered_rows = returned.reshape(experts_all * capacity, model_width)[places].reshape(
        tok_rows, top_count, model_width
    )
    moe_out = jnp.sum(weights[:, :, None] * gathered_rows.astype(jnp.float32), axis=1).astype(
        jnp.bfloat16
    )
    mixer_in = rms_rows(
        stream.astype(jnp.float32) + moe_out.astype(jnp.float32), mixer_gain
    ).astype(jnp.bfloat16)
    weight_list = (query_weight, key_weight, value_weight, output_gate, beta_weight, decay_weight)
    piece_rows = lax.all_gather(mixer_in, "head", axis=0, tiled=True)
    projected = jnp.concatenate(
        [jnp.dot(piece_rows, matrix, preferred_element_type=jnp.float32) for matrix in weight_list],
        axis=1,
    )
    row_count = projected.shape[0]
    key_cols = query_weight.shape[1]
    value_cols = value_weight.shape[1]
    head_cols = beta_weight.shape[1]
    conv_cols = 2 * key_cols + value_cols
    qkv_raw = projected[:, :conv_cols].astype(jnp.bfloat16)
    gate_raw = projected[:, conv_cols : conv_cols + value_cols].astype(jnp.bfloat16)
    beta_raw = projected[:, conv_cols + value_cols : conv_cols + value_cols + head_cols]
    decay_raw = projected[:, conv_cols + value_cols + head_cols :]
    taps = jnp.concatenate([query_conv, key_conv, value_conv], axis=1)
    rim_len = taps.shape[0] - 1
    rim_cells = passed_along(qkv_raw[row_count - rim_len :], "ctx", 1)
    extended = jnp.concatenate([rim_cells.astype(jnp.float32), qkv_raw.astype(jnp.float32)], axis=0)
    summed = jnp.zeros((row_count, conv_cols), jnp.float32)
    for shift_index in range(rim_len + 1):
        summed = (
            summed + taps[shift_index][None, :] * extended[shift_index : shift_index + row_count]
        )
    convolved = jax.nn.silu(summed)
    key_width = DK
    key_heads = key_cols // key_width
    group_size = head_cols // key_heads
    queries = unit_heads(convolved[:, :key_cols], key_heads) * key_width ** (-0.5)
    key_rows = unit_heads(convolved[:, key_cols : 2 * key_cols], key_heads)
    values = convolved[:, 2 * key_cols :].reshape(row_count, head_cols, -1)
    strength = jax.nn.sigmoid(beta_raw)
    decays = -jnp.exp(decay_log)[None, :] * jax.nn.softplus(decay_raw + decay_bias[None, :])
    query_heads = jnp.repeat(queries, group_size, axis=1).transpose(1, 0, 2)
    key_head_rows = jnp.repeat(key_rows, group_size, axis=1).transpose(1, 0, 2)
    output_list, read_values, transfer, offset = jax.vmap(local_pass)(
        query_heads, key_head_rows, values.transpose(1, 0, 2), strength.T, decays.T
    )

    def compose(earlier, later):
        joined = jnp.einsum("hij,hjk->hik", later[0], earlier[0], precision=exact_precision)
        shifted = (
            jnp.einsum("hij,hjk->hik", later[0], earlier[1], precision=exact_precision) + later[1]
        )
        return (joined, shifted)

    identity = (
        jnp.broadcast_to(jnp.eye(transfer.shape[1], dtype=jnp.float32), transfer.shape),
        jnp.zeros_like(offset),
    )
    incoming_rows = prefix((transfer, offset), "ctx", compose, identity)[1]
    delta_core_output = output_list + jnp.einsum(
        "wnc,wcg->wng", read_values, incoming_rows, precision=exact_precision
    )
    delta_core_output = delta_core_output.transpose(1, 0, 2)
    normal = (
        delta_core_output
        * lax.rsqrt(
            jnp.mean(delta_core_output * delta_core_output, axis=-1, keepdims=True) + epsilon
        )
        * head_gain
    )
    gate_values = gate_raw.astype(jnp.float32).reshape(row_count, head_cols, -1)
    gated_out = (
        (normal * jax.nn.silu(gate_values)).astype(jnp.bfloat16).reshape(row_count, value_cols)
    )
    mixer_out = lax.psum_scatter(
        jnp.dot(gated_out, out_weight, preferred_element_type=jnp.float32).astype(jnp.bfloat16),
        "head",
        scatter_dimension=0,
        tiled=True,
    )
    return (moe_out, mixer_out)


def solution(mesh):
    return jax.shard_map(
        on_device,
        mesh=mesh,
        in_specs=(
            P(("ctx", "head"), None),
            P(),
            P(),
            P(("ctx", "head"), None),
            P(("ctx", "head"), None, None),
            P(("ctx", "head"), None, None),
            P(("ctx", "head"), None, None),
            P(),
            P(None, "head"),
            P(None, "head"),
            P(None, "head"),
            P(None, "head"),
            P(None, "head"),
            P(None, "head"),
            P(None, "head"),
            P(None, "head"),
            P(None, "head"),
            P("head"),
            P("head"),
            P(),
            P("head", None),
        ),
        out_specs=(P(("ctx", "head"), None), P(("ctx", "head"), None)),
        check_vma=False,
    )
```

profile of v0, /device:TPU:1, one launch (start us, length us, event | category | flops | bytes accessed | tf_op | source)
XLA Modules:
  0.0 852.3 jit_solution(13656351736903203024)
XLA Ops:
  17.1 34.2 %scatter_custom_fusion = bf16[1536,2048]{1,0:T(8,128)(2,1)} fusion(s32[1280]{0:T(1024)S(1)} %fusion.111, bf16[128,2048]{1,0:T(8,128)(2,1)S(1)} %fusion.102, s32[2048]{0:T(1024)S(1)} %pad_clamp_fusion.1, bf16[]{:T(256)} %constant.111.clone.1), kind=kCustom, calls=%fused_computation.65 | custom fusion | bytes 6291458 | tf_op jit(solution)/shard_map/scatter | solution.py:169
  51.3 11.0 %reshape.241 = bf16[128,2,6,2048]{3,2,1,0:T(8,128)(2,1)} reshape(bf16[1536,2048]{1,0:T(8,128)(2,1)} %scatter_custom_fusion) | data formatting | bytes 12582912 | tf_op jit(solution)/shard_map/reshape | solution.py:171
  62.3 9.6 %copy.131 = bf16[128,2,6,2048]{3,1,2,0:T(2,128)(2,1)S(1)} copy(bf16[128,2,6,2048]{3,2,1,0:T(8,128)(2,1)} %reshape.241) | data formatting | bytes 12582912 | tf_op jit(solution)/shard_map/reshape | solution.py:171
  72.0 87.2 %all_to_all.10 = bf16[128,2,6,2048]{3,1,2,0:T(2,128)(2,1)S(1)} all-to-all(bf16[128,2,6,2048]{3,1,2,0:T(2,128)(2,1)S(1)} %copy.131), channel_id=1, replica_groups=mesh['ctx'=32,'head'=4] {'ctx','head'}, dimensions={0} | all-to-all | bytes 12582912 | tf_op jit(solution)/shard_map/all_to_all | solution.py:172
  161.9 8.6 %fusion.48 = f32[2,128,6,512]{3,1,2,0:T(8,128)} fusion(bf16[128,2,6,2048]{3,1,2,0:T(2,128)(2,1)S(1)} %all_to_all.10, bf16[2,2048,512]{2,1,0:T(8,128)(2,1)S(1)} %copy-done.22), kind=kOutput, calls=%fused_computation.61 | convolution fusion | flops 3221225472 | bytes 13631488 | tf_op jit(solution)/shard_map/nesd,edh->nesh/dot_general | solution.py:176
  170.4 19.9 %convert_bitcast_fusion = bf16[128,2,6,2048]{3,0,2,1:T(8,128)(2,1)} fusion(bf16[2,512,2048]{2,1,0:T(8,128)(2,1)} %param.31, f32[2,128,6,512]{3,1,2,0:T(8,128)} %fusion.48, bf16[2,2048,512]{2,1,0:T(8,128)(2,1)} %param.29, bf16[128,2,6,2048]{3,1,2,0:T(2,128)(2,1)} %copy-done.7), kind=kOutput, calls=%fused_computation.60 | convolution fusion | flops 6450315264 | bytes 24117248 | tf_op jit(solution)/shard_map/nesh,ehd->nesd/dot_general | solution.py:179
  190.3 12.8 %copy.134 = bf16[128,2,6,2048]{3,1,2,0:T(2,128)(2,1)} copy(bf16[128,2,6,2048]{3,0,2,1:T(8,128)(2,1)} %convert_bitcast_fusion) | data formatting | bytes 12582912 | tf_op jit(solution)/shard_map/convert_element_type | solution.py:181
  203.1 4.9 all-to-all-start.1
  209.9 10.3 %gather_fusion.1 = f32[1280]{0:T(1024)S(1)} fusion(f32[128,256]{1,0:T(8,128)S(1)} %fusion.119, s32[1280]{0:T(1024)S(1)} %reshape.277), kind=kCustom, calls=%fused_computation.2 | custom fusion | bytes 20480 | tf_op jit(solution)/shard_map/jit(take_along_axis)/gather | solution.py:156
  220.6 64.5 %all-to-all-done.1 = bf16[128,2,6,2048]{3,1,2,0:T(2,128)(2,1)} async-done(((bf16[128,2,6,2048]{3,1,2,0:T(2,128)(2,1)}), bf16[128,2,6,2048]{3,1,2,0:T(2,128)(2,1)}, u32[]{:S(2)}, u32[]{:S(2)}) %all-to-all-start.1) | async-done | bytes 6291488 | tf_op jit(solution)/shard_map/all_to_all | solution.py:178
  285.0 10.4 %copy.135 = bf16[128,2,6,2048]{3,2,1,0:T(8,128)(2,1)} copy(bf16[128,2,6,2048]{3,1,2,0:T(2,128)(2,1)} %all-to-all-done.1) | data formatting | bytes 12582912 | tf_op jit(solution)/shard_map/all_to_all | solution.py:178
  295.4 11.0 %reshape.242 = bf16[1536,2048]{1,0:T(8,128)(2,1)} reshape(bf16[128,2,6,2048]{3,2,1,0:T(8,128)(2,1)} %copy.135) | data formatting | bytes 12582912 | tf_op jit(solution)/shard_map/reshape | solution.py:187
  306.5 14.4 %gather_fusion = bf16[1280,2048]{1,0:T(8,128)(2,1)} fusion(bf16[1536,2048]{1,0:T(8,128)(2,1)} %reshape.242, s32[2048]{0:T(1024)S(1)} %pad_clamp_fusion), kind=kCustom, calls=%fused_computation.1 | custom fusion | bytes 10490880 | tf_op jit(solution)/shard_map/gather | solution.py:187
  320.9 10.5 %reshape.258 = f32[128,10,2048]{2,1,0:T(8,128)} reshape(bf16[1280,2048]{1,0:T(8,128)(2,1)} %gather_fusion) | data formatting | bytes 15728640 | tf_op jit(solution)/shard_map/convert_element_type | solution.py:190
  331.4 9.6 %multiply_reduce_fusion = bf16[128,2048]{1,0:T(8,128)(2,1)S(1)} fusion(f32[128,10,2048]{2,1,0:T(8,128)} %reshape.258, f32[128,10]{1,0:T(8,128)S(1)} %copy.125), kind=kLoop, calls=%fused_computation.59 | loop fusion | flops 4980736 | bytes 11015168 | tf_op jit(solution)/shard_map/reduce_sum | solution.py:190
  343.9 27.1 %all-gather.6.cloned.1.call-done = bf16[512,2048]{1,0:T(8,128)(2,1)} async-done(((bf16[128,2048]{1,0:T(8,128)(2,1)}), bf16[512,2048]{1,0:T(8,128)(2,1)}) %all-gather.6.cloned.1.call-update) | async-done | bytes 2097168 | tf_op jit(solution)/shard_map/all_gather | solution.py:197
  387.5 6.4 divide_multiply_fusion
  403.0 158.7 %custom-call.4 = f32[4,8,1,64,64]{3,4,2,1,0:T(8,128)} custom-call(f32[4,8,1,64,64]{4,3,2,1,0:T(8,128)} %fusion.88), custom_call_target="InvertDiagBlocksLowerTriangular" | custom-call | tf_op jit(solution)/shard_map/vmap(vmap(jit(_solve_triangular)))/triangular_solve | solution.py:65
  573.3 100.6 %while.31 = (s32[]{:T(128)}, f32[4,128,128]{2,1,0:T(8,128)S(1)}, f32[4,128,128]{2,1,0:T(8,128)S(1)}, f32[8,4,64,128]{3,2,0,1:T(8,128)}, f32[8,4,64,128]{3,2,0,1:...) while((s32[]{:T(128)}, f32[4,128,128]{2,1,0:T(8,128)S(1)}, ...), condition=%wide.region_12.13_spmd.clone, body=%wide.region_11.12_spmd.clone.sunk | while | flops 352878592 | bytes 4855501 | solution.py:112
  675.7 4.3 convolution_convert_fusion.1
  681.6 39.2 %all-gather.8.cloned.1.call-done = bf16[128,128,128]{2,1,0:T(8,128)(2,1)} async-done(((bf16[4,128,128]{2,1,0:T(8,128)(2,1)}), bf16[128,128,128]{2,1,0:T(8,128)(2,1)}) %all-gather.8.cloned.1.call-update) | async-done | bytes 4194320 | tf_op jit(solution)/shard_map/all_gather | solution.py:24
  720.8 48.0 %all-gather.10.cloned.1.call-done = bf16[128,128,128]{2,1,0:T(8,128)(2,1)} async-done(((bf16[4,128,128]{2,1,0:T(8,128)(2,1)}), bf16[128,128,128]{2,1,0:T(8,128)(2,1)}) %all-gather.10.cloned.1.call-update) | async-done | bytes 4194320 | tf_op jit(solution)/shard_map/all_gather | solution.py:24
  768.8 42.3 %while.32 = (s32[]{:T(128)}, f32[4,128,128]{2,1,0:T(8,128)S(1)}, s32[]{:T(128)}, bf16[32,4,128,128]{3,2,1,0:T(8,128)(2,1)}, bf16[32,4,128,128]{3,2,1,0:T(8,128)(2,1)}, /*index=5*/s32[]{:T(128)}, s32[]{:T(128)}) while((s32[]{:T(128)}, f32[4,128,128]{2,1,0:T(8,128)S(1)}, s32[]{:T(128)}, bf16[32,4,128,128]{3,2,1,0:T(8,128)(2,1)}, ...), condition=%wide.region_14.15_spmd.clone, body=%wide.region_13.14_spmd.clone.sunk | while | flops 100990976 | bytes 1575519 | solution.py:41
  816.6 28.7 %reduce-scatter.2.cloned.1.call-done = bf16[128,2048]{1,0:T(8,128)(2,1)} async-done(((bf16[512,2048]{1,0:T(8,128)(2,1)}), bf16[128,2048]{1,0:T(8,128)(2,1)}) %reduce-scatter.2.cloned.1.call-update) | async-done | bytes 524304 | tf_op jit(solution)/shard_map/reduce_scatter | solution.py:262
  (282 shorter events, 204.5 us)
Async XLA Ops:
  7.2 806.8 %copy-start = (bf16[512,2048]{1,0:T(8,128)(2,1)S(1)}, bf16[512,2048]{1,0:T(8,128)(2,1)}, u32[]{:S(2)}) copy-start(bf16[512,2048]{1,0:T(8,128)(2,1)} %param.45) | copy-start | bytes 6291460
  12.8 2.1 copy-start.6
  12.8 4.1 copy-start.15
  72.0 89.9 %copy-start.22 = (bf16[2,2048,512]{2,1,0:T(8,128)(2,1)S(1)}, bf16[2,2048,512]{2,1,0:T(8,128)(2,1)}, u32[]{:S(2)}) copy-start(bf16[2,2048,512]{2,1,0:T(8,128)(2,1)} %param.30) | copy-start | bytes 12582916
  159.2 2.6 copy-start.7
  203.1 5.0 copy-start.12
  203.1 82.0 %all-to-all-start.1 = ((bf16[128,2,6,2048]{3,1,2,0:T(2,128)(2,1)}), bf16[128,2,6,2048]{3,1,2,0:T(2,128)(2,1)}, u32[]{:S(2)}, u32[]{:S(2)}) async-start(bf16[128,2,6,2048]{3,1,2,0:T(2,128)(2,1)} %copy.134), calls=%async_computation.1 | async-start | bytes 12582912 | tf_op jit(solution)/shard_map/all_to_all | solution.py:178
  208.0 162.9 %all-gather.6.cloned.1.call-start = ((), (), s32[]{:S(2)}) async-start(), calls=%async_computation.3 | async-start | bytes 2621440 | tf_op jit(solution)/shard_map/all_gather | solution.py:197
  331.4 9.9 %copy-start.16 = (f32[2048]{0:T(1024)S(1)}, f32[2048]{0:T(1024)}, u32[]{:S(2)}) copy-start(f32[2048]{0:T(1024)} %param.32) | copy-start | bytes 24580
  341.0 33.6 %copy-start.8 = (bf16[128,2048]{1,0:T(8,128)(2,1)}, bf16[128,2048]{1,0:T(8,128)(2,1)S(1)}, u32[]{:S(2)}) copy-start(bf16[128,2048]{1,0:T(8,128)(2,1)S(1)} %multiply_reduce_fusion) | copy-start | bytes 1572868
  341.0 2.1 copy-start.25
  342.4 378.5 %all-gather.8.cloned.1.call-start = ((), (), s32[]{:S(2)}) async-start(), calls=%async_computation.5 | async-start | bytes 4325376 | tf_op jit(solution)/shard_map/all_gather | solution.py:24
  370.9 3.7 copy-start.5
  370.9 3.7 copy-start.23
  376.6 5.6 copy-start.13
  376.7 5.6 copy-start.21
  378.4 6.0 copy-start.14
  378.5 8.9 %collective-permute-start = (bf16[3,1024]{0,1:T(8,128)(2,1)S(1)}, bf16[3,1024]{0,1:T(8,128)(2,1)S(1)}, u32[]{:S(2)}, u32[]{:S(2)}) collective-permute-start(bf16[3,1024]{0,1:T(8,128)(2,1)S(1)} %slice.81), channel_id=1, source_target_pairs={{0,4},{4,8},{8,12},{12,16},{16,20},{20,24},{24,28},{28,32},{32,36}... | collective-permute-start | bytes 18440 | tf_op jit(solution)/shard_map/ppermute | solution.py:18
  397.2 164.4 %slice-start = ((f32[512,1024]{0,1:T(8,128)}), f32[512,512]{0,1:T(8,128)S(1)}, s32[]{:S(2)}) async-start(f32[512,1024]{0,1:T(8,128)} %copy-done.1), calls=%async_computation.7 | async-start | bytes 2097152 | tf_op jit(solution)/shard_map/slice | solution.py:226
  564.3 2.2 copy-start.10
  674.6 94.2 %all-gather.10.cloned.1.call-start = ((), (), s32[]{:S(2)}) async-start(), calls=%async_computation.6 | async-start | bytes 4325376 | tf_op jit(solution)/shard_map/all_gather | solution.py:24
  675.3 170.0 %reduce-scatter.2.cloned.1.call-start = ((), (), s32[]{:S(2)}) async-start(), calls=%async_computation.4 | async-start | bytes 2621440 | tf_op jit(solution)/shard_map/reduce_scatter | solution.py:262
  811.1 2.4 copy-start.11
  811.1 2.4 copy-start.20
  (9 other events, 12.4 us)
Sparse Core Ops, SparseCore 0:
  342.5 28.4 all-gather.5
  674.7 46.0 all-gather.7
  723.1 45.6 all-gather.9
  816.7 28.5 reduce-scatter.1
where the time goes:
time: 859 us; the launch traced here: 852 us
  waiting for transfers between devices  208 us (24%)
  matrix products  191 us (22%)
  other arithmetic  189 us (22%)
  local copies, waits for them, and re-layouts  152 us (18%)
  blocking collectives  87.2 us (10%)
  between operations  14.9 us (2%)
  starting transfers between devices  9.12 us (1%)
    another operation x2, other arithmetic, block_terms(): jax.scipy.linalg.solve_triangular(system, targets, lower=True, unit_diago...  159 us
    all_to_all x1, blocking collectives, on_device(): lax.all_to_all(outgoing, ('ctx', 'head'), split_axis=0, concat_axis=0, ti...  87.2 us
    all_gather x2, waiting for transfers between devices, prefix(): lax.all_gather(part.astype(kind), axis)  87.2 us
    all_to_all x1, waiting for transfers between devices, on_device(): lax.all_to_all(jnp.einsum('nesh,ehd->nesd', hidden, expert_down, preferre...  64.5 us
    dot_general x32, matrix products, compose(): jnp.einsum('hij,hjk->hik', later[0], earlier[1], precision=exact_precision)  40.5 us
    scatter x1, local copies, waits for them, and re-layouts, on_device(): outgoing = jnp.zeros((experts_all * capacity, model_width), jnp.bfloat16)...  34.2 us
    reduce_scatter x1, waiting for transfers between devices, on_device(): lax.psum_scatter(jnp.dot(gated_out, out_weight, preferred_element_type=jn...  28.7 us
    all_gather x1, waiting for transfers between devices, on_device(): piece_rows = lax.all_gather(mixer_in, 'head', axis=0, tiled=True)  27.1 us
  transfers between devices with their start and end apart: 6, of which 5 were waited for; matrix products, arithmetic and copies ran while one was open for 3% of the time, Pallas kernels for 0%

commit v1 on v0

--- a/solution.py
+++ b/solution.py
@@ -3,9 +3,105 @@
 import jax
 import jax.numpy as jnp
 from jax import lax
+from jax.experimental import pallas as pl
+from jax.experimental.pallas import tpu as pltpu
 from jax.sharding import PartitionSpec as P
 
 DK = 128
+HI = lax.Precision.HIGHEST
+CHUNK = 64
+
+
+def _mm(a, b):
+    return jnp.dot(a, b, precision=HI, preferred_element_type=jnp.float32)
+
+
+def _mm_nt(a, b):
+    return lax.dot_general(a, b, (((1,), (1,)), ((), ())), precision=HI,
+                           preferred_element_type=jnp.float32)
+
+
+def _mm_tn(a, b):
+    return lax.dot_general(a, b, (((0,), (0,)), ((), ())), precision=HI,
+                           preferred_element_type=jnp.float32)
+
+
+def delta_kernel(q_ref, k_ref, v_ref, b_ref, cc_ref, cr_ref, res_ref, read_ref, t_ref, o_ref):
+    length, kw = q_ref.shape[1], q_ref.shape[2]
+    vw = v_ref.shape[2]
+    n_chunks = length // CHUNK
+    row = lax.broadcasted_iota(jnp.int32, (CHUNK, CHUNK), 0)
+    col = lax.broadcasted_iota(jnp.int32, (CHUNK, CHUNK), 1)
+    strict = row > col
+    inclusive = row >= col
+    eye_c = jnp.where(row == col, 1.0, 0.0).astype(jnp.float32)
+    krow = lax.broadcasted_iota(jnp.int32, (kw, kw), 0)
+    kcol = lax.broadcasted_iota(jnp.int32, (kw, kw), 1)
+    eye_k = jnp.where(krow == kcol, 1.0, 0.0).astype(jnp.float32)
+
+    def body(c, carry):
+        state, transfer = carry
+        rows = pl.ds(pl.multiple_of(c * CHUNK, CHUNK), CHUNK)
+        q = q_ref[0, rows, :]
+        k = k_ref[0, rows, :]
+        v = v_ref[0, rows, :]
+        beta = b_ref[0, rows, :]
+        cum_c = cc_ref[0, rows, :]
+        cum_r = cr_ref[0, pl.ds(c, 1), :]
+        spread = cum_c - cum_r
+        fall_s = jnp.where(strict, jnp.exp(jnp.where(strict, spread, 0.0)), 0.0)
+        fall_i = jnp.where(inclusive, jnp.exp(jnp.where(inclusive, spread, 0.0)), 0.0)
+        a = beta * fall_s * _mm_nt(k, k)
+        inv = eye_c
+        size = 1
+        while size < CHUNK:
+            band = ((row // (2 * size)) == (col // (2 * size))) & ((row // size) != (col // size))
+            e = jnp.where(band, a, 0.0)
+            inv = inv - _mm(_mm(inv, e), inv)
+            size *= 2
+        ec = jnp.exp(cum_c)
+        w_values = _mm(inv, beta * v)
+        w_keys = _mm(inv, (beta * ec) * k)
+        mixing = fall_i * _mm_nt(q, k)
+        q_dec = ec * q
+        last = cum_r[:, CHUNK - 1:CHUNK]
+        k_dec = jnp.exp(last - cum_c) * k
+        closing = jnp.exp(last)
+        update = w_values - _mm(w_keys, state)
+        res_ref[0, rows, :] = _mm(q_dec, state) + _mm(mixing, update)
+        moved = _mm(w_keys, transfer)
+        read_ref[0, rows, :] = _mm(q_dec, transfer) - _mm(mixing, moved)
+        state = closing * state + _mm_tn(k_dec, update)
+        transfer = closing * transfer - _mm_tn(k_dec, moved)
+        return state, transfer
+
+    state0 = jnp.zeros((kw, vw), jnp.float32)
+    state, transfer = lax.fori_loop(0, n_chunks, body, (state0, eye_k))
+    t_ref[0] = transfer
+    o_ref[0] = state
+
+
+def local_delta(queries, key_rows, values, strength, decays):
+    heads, length, kw = queries.shape
+    vw = values.shape[2]
+    n_chunks = length // CHUNK
+    cum = jnp.cumsum(decays.reshape(heads, n_chunks, CHUNK), axis=-1)
+    cum_col = cum.reshape(heads, length, 1)
+    beta_col = strength.reshape(heads, length, 1)
+    seq = lambda w: pl.BlockSpec((1, length, w), lambda h: (h, 0, 0))
+    mat = pl.BlockSpec((1, kw, vw), lambda h: (h, 0, 0))
+    return pl.pallas_call(
+        delta_kernel,
+        grid=(heads,),
+        in_specs=[seq(kw), seq(kw), seq(vw), seq(1), seq(1),
+                  pl.BlockSpec((1, n_chunks, CHUNK), lambda h: (h, 0, 0))],
+        out_specs=[seq(vw), seq(vw), mat, mat],
+        out_shape=[jax.ShapeDtypeStruct((heads, length, vw), jnp.float32),
+                   jax.ShapeDtypeStruct((heads, length, vw), jnp.float32),
+                   jax.ShapeDtypeStruct((heads, kw, vw), jnp.float32),
+                   jax.ShapeDtypeStruct((heads, kw, vw), jnp.float32)],
+        name="delta_chunks",
+    )(queries, key_rows, values, beta_col, cum_col, cum)
 
 
 epsilon = 1e-06
@@ -18,99 +114,35 @@
     return lax.ppermute(value, axis, [(source, source + steps) for source in range(first, last)])
 
 
-def prefix(array, axis, combine, identity):
-    peers, place = (lax.axis_size(axis), lax.axis_index(axis))
-    everything = jax.tree.map(
-        lambda part, kind: lax.all_gather(part.astype(kind), axis),
-        array,
-        (jnp.bfloat16, jnp.bfloat16),
-    )
-    start = jax.tree.map(
-        lambda part, zero: jnp.broadcast_to(jnp.asarray(zero, part.dtype), part.shape),
-        array,
-        identity,
-    )
-
-    def step(k, before):
-        reached = k < place
-        new = combine(
-            before, jax.tree.map(lambda part, own: part[k].astype(own.dtype), everything, array)
-        )
-        return jax.tree.map(lambda a, b: jnp.where(reached, a, b), new, before)
-
-    return lax.fori_loop(0, peers, step, start)
+def shifted(value, axis, steps):
+    count = lax.axis_size(axis)
+    return lax.ppermute(value, axis, [(source, source + steps) for source in range(count - steps)])
+
+
+def batched_mm(a, b):
+    return jnp.einsum("hij,hjk->hik", a, b, precision=HI)
+
+
+def incoming_state(transfer, offset, axis):
+    count, place = lax.axis_size(axis), lax.axis_index(axis)
+    steps = 1
+    while steps < count:
+        far_offset = shifted(offset, axis, steps)
+        reached = place >= steps
+        if 2 * steps < count:
+            far_transfer = shifted(transfer, axis, steps)
+            offset = jnp.where(reached, offset + batched_mm(transfer, far_offset), offset)
+            transfer = jnp.where(reached, batched_mm(transfer, far_transfer), transfer)
+        else:
+            offset = jnp.where(reached, offset + batched_mm(transfer, far_offset), offset)
+        steps *= 2
+    return shifted(offset, axis, 1)
 
 
 def rms_rows(values, gain):
     values = values.astype(jnp.float32)
     scale = lax.rsqrt(jnp.mean(values * values, axis=-1, keepdims=True) + epsilon)
     return values * scale * gain
-
-
-def block_terms(queries, key_rows, values, strength, decays):
-    length = queries.shape[0]
-    cumulative = jnp.cumsum(decays)
-    spread = cumulative[:, None] - cumulative[None, :]
-    positions = jnp.arange(length, dtype=jnp.int32)
-    strict = positions[:, None] > positions[None, :]
-    inclusive = positions[:, None] >= positions[None, :]
-    fall_strict = jnp.where(strict, jnp.exp(jnp.where(strict, spread, 0.0)), 0.0)
-    fall_inclusive = jnp.where(inclusive, jnp.exp(jnp.where(inclusive, spread, 0.0)), 0.0)
-    key_dots = jnp.dot(key_rows, key_rows.T, precision=exact_precision)
-    strict_part = strength[:, None] * fall_strict * key_dots
-    system = jnp.eye(length, dtype=jnp.float32) + strict_part
-    targets = strength[:, None] * jnp.concatenate(
-        [values, jnp.exp(cumulative)[:, None] * key_rows], axis=1
-    )
-    solved = jax.scipy.linalg.solve_triangular(system, targets, lower=True, unit_diagonal=True)
-    value_width = values.shape[1]
-    w_values = solved[:, :value_width]
-    w_keys = solved[:, value_width:]
-    mixing = fall_inclusive * jnp.dot(queries, key_rows.T, precision=exact_precision)
-    q_decayed = jnp.exp(cumulative)[:, None] * queries
-    k_decayed = jnp.exp(cumulative[-1] - cumulative)[:, None] * key_rows
-    closing = jnp.exp(cumulative[-1])
-    return (w_values, w_keys, mixing, q_decayed, k_decayed, closing)
-
-
-def local_pass(queries, key_rows, values, strength, decays):
-    length = queries.shape[0]
-    block_len = math.gcd(length, 64)
-    block_count = length // block_len
-
-    def split_blocks(array):
-        return array.reshape((block_count, block_len) + array.shape[1:])
-
-    terms = jax.vmap(block_terms)(
-        split_blocks(queries),
-        split_blocks(key_rows),
-        split_blocks(values),
-        split_blocks(strength),
-        split_blocks(decays),
-    )
-
-    def advance(carried_pair, block_term):
-        state_now, transfer = carried_pair
-        w_values, w_keys, mixing, q_decayed, k_decayed, closing = block_term
-        update = w_values - jnp.dot(w_keys, state_now, precision=exact_precision)
-        result = jnp.dot(q_decayed, state_now, precision=exact_precision) + jnp.dot(
-            mixing, update, precision=exact_precision
-        )
-        moved_rows = jnp.dot(w_keys, transfer, precision=exact_precision)
-        reading = jnp.dot(q_decayed, transfer, precision=exact_precision) - jnp.dot(
-            mixing, moved_rows, precision=exact_precision
-        )
-        state_now = closing * state_now + jnp.dot(k_decayed.T, update, precision=exact_precision)
-        transfer = closing * transfer - jnp.dot(k_decayed.T, moved_rows, precision=exact_precision)
-        return ((state_now, transfer), (result, reading))
-
-    key_width = key_rows.shape[1]
-    initial = (
-        jnp.zeros((key_width, values.shape[1]), jnp.float32),
-        jnp.eye(key_width, dtype=jnp.float32),
-    )
-    (state_now, transfer), (results, read_values) = lax.scan(advance, initial, terms)
-    return (results.reshape(length, -1), read_values.reshape(length, -1), transfer, state_now)
 
 
 def unit_heads(array, heads):
@@ -228,22 +260,10 @@
     decays = -jnp.exp(decay_log)[None, :] * jax.nn.softplus(decay_raw + decay_bias[None, :])
     query_heads = jnp.repeat(queries, group_size, axis=1).transpose(1, 0, 2)
     key_head_rows = jnp.repeat(key_rows, group_size, axis=1).transpose(1, 0, 2)
-    output_list, read_values, transfer, offset = jax.vmap(local_pass)(
+    output_list, read_values, transfer, offset = local_delta(
         query_heads, key_head_rows, values.transpose(1, 0, 2), strength.T, decays.T
     )
-
-    def compose(earlier, later):
-        joined = jnp.einsum("hij,hjk->hik", later[0], earlier[0], precision=exact_precision)
-        shifted = (
-            jnp.einsum("hij,hjk->hik", later[0], earlier[1], precision=exact_precision) + later[1]
-        )
-        return (joined, shifted)
-
-    identity = (
-        jnp.broadcast_to(jnp.eye(transfer.shape[1], dtype=jnp.float32), transfer.shape),
-        jnp.zeros_like(offset),
-    )
-    incoming_rows = prefix((transfer, offset), "ctx", compose, identity)[1]
+    incoming_rows = incoming_state(transfer, offset, "ctx")
     delta_core_output = output_list + jnp.einsum(
         "wnc,wcg->wng", read_values, incoming_rows, precision=exact_precision
     )

time: 859 us -> 618 us (0.72)
  other arithmetic: 189 us -> 28.8 us
  matrix products: 191 us -> 53.5 us
  Pallas kernels: 0 us -> 99.5 us
  waiting for transfers between devices: 208 us -> 129 us
  starting transfers between devices: 9.12 us -> 56 us
    another operation x7 -> x3, other arithmetic: 160 us -> 1.49 us  [the longest x1 1.12 us: local_delta(): cum = jnp.cumsum(decays.reshape(heads, n_chunks, CHUNK), axis=-1)]
    dot_general x98 -> x9, matrix products: 141 us -> 7.53 us  [batched_mm(): return jnp.einsum('hij,hjk->hik', a, b, precision=HI)]
    pallas_call x0 -> x1, Pallas kernels: none -> 99.5 us  [local_delta(): pl.pallas_call(delta_kernel, grid=(heads,), in_specs=[seq(kw), seq(kw), s...]
    all_gather x2 -> x0, waiting for transfers between devices: 87.2 us -> none  [prefix(): lax.all_gather(part.astype(kind), axis)]
    ppermute x0 -> x10, starting transfers between devices: none -> 47.3 us  [shifted(): lax.ppermute(value, axis, [(source, source + steps) for source in range(c...]
  transfers between devices with their start and end apart: 6 -> 14, of which waited for: 5 -> 4; matrix products, arithmetic and copies ran while one was open for 3% -> 5% of each run, Pallas kernels for 0% -> 0%
where the time goes in v1:
time: 618 us; the launch traced here: 613 us
  local copies, waits for them, and re-layouts  144 us (23%)
  waiting for transfers between devices  129 us (21%)
  Pallas kernels  99.5 us (16%)
  blocking collectives  87.2 us (14%)
  starting transfers between devices  56 us (9%)
  matrix products  53.5 us (9%)
  other arithmetic  28.8 us (5%)
  between operations  15.1 us (2%)
    pallas_call x1, Pallas kernels, local_delta(): pl.pallas_call(delta_kernel, grid=(heads,), in_specs=[seq(kw), seq(kw), s...  99.5 us
    all_to_all x1, blocking collectives, on_device(): lax.all_to_all(outgoing, ('ctx', 'head'), split_axis=0, concat_axis=0, ti...  87.2 us
    all_to_all x1, waiting for transfers between devices, on_device(): lax.all_to_all(jnp.einsum('nesh,ehd->nesd', hidden, expert_down, preferre...  64.5 us
    ppermute x10, starting transfers between devices, shifted(): lax.ppermute(value, axis, [(source, source + steps) for source in range(c...  47.3 us
    scatter x1, local copies, waits for them, and re-layouts, on_device(): outgoing = jnp.zeros((experts_all * capacity, model_width), jnp.bfloat16)...  34.1 us
    reduce_scatter x1, waiting for transfers between devices, on_device(): lax.psum_scatter(jnp.dot(gated_out, out_weight, preferred_element_type=jn...  30.1 us
    all_gather x1, waiting for transfers between devices, on_device(): piece_rows = lax.all_gather(mixer_in, 'head', axis=0, tiled=True)  28.4 us
    reshape x2, local copies, waits for them, and re-layouts, on_device(): outgoing = outgoing.reshape(sources, local_experts, capacity, model_width)  20.6 us
  transfers between devices with their start and end apart: 14, of which 4 were waited for; matrix products, arithmetic and copies ran while one was open for 5% of the time, Pallas kernels for 0%

profile of v1, /device:TPU:1, one launch (start us, length us, event | category | flops | bytes accessed | tf_op | source)
XLA Modules:
  0.0 612.9 jit_solution(805912479068068179)
XLA Ops:
  16.0 34.1 %scatter_custom_fusion = bf16[1536,2048]{1,0:T(8,128)(2,1)} fusion(s32[1280]{0:T(1024)S(1)} %fusion.50, bf16[128,2048]{1,0:T(8,128)(2,1)S(1)} %fusion.47, s32[2048]{0:T(1024)S(1)} %pad_clamp_fusion.1, bf16[]{:T(256)} %constant.41.clone.1), kind=kCustom, calls=%fused_computation.10 | custom fusion | bytes 6291458 | tf_op jit(solution)/shard_map/scatter | solution.py:201
  50.1 11.0 %reshape.202 = bf16[128,2,6,2048]{3,2,1,0:T(8,128)(2,1)} reshape(bf16[1536,2048]{1,0:T(8,128)(2,1)} %scatter_custom_fusion) | data formatting | bytes 12582912 | tf_op jit(solution)/shard_map/reshape | solution.py:203
  61.1 9.6 %copy.106 = bf16[128,2,6,2048]{3,1,2,0:T(2,128)(2,1)S(1)} copy(bf16[128,2,6,2048]{3,2,1,0:T(8,128)(2,1)} %reshape.202) | data formatting | bytes 12582912 | tf_op jit(solution)/shard_map/reshape | solution.py:203
  70.8 87.2 %all_to_all.10 = bf16[128,2,6,2048]{3,1,2,0:T(2,128)(2,1)S(1)} all-to-all(bf16[128,2,6,2048]{3,1,2,0:T(2,128)(2,1)S(1)} %copy.106), channel_id=1, replica_groups=mesh['ctx'=32,'head'=4] {'ctx','head'}, dimensions={0} | all-to-all | bytes 12582912 | tf_op jit(solution)/shard_map/all_to_all | solution.py:204
  160.7 8.6 %fusion = f32[2,128,6,512]{3,1,2,0:T(8,128)} fusion(bf16[128,2,6,2048]{3,1,2,0:T(2,128)(2,1)S(1)} %all_to_all.10, bf16[2,2048,512]{2,1,0:T(8,128)(2,1)S(1)} %copy-done.18), kind=kOutput, calls=%fused_computation.6 | convolution fusion | flops 3221225472 | bytes 13631488 | tf_op jit(solution)/shard_map/nesd,edh->nesh/dot_general | solution.py:208
  169.3 19.8 %convert_bitcast_fusion = bf16[128,2,6,2048]{3,0,2,1:T(8,128)(2,1)} fusion(bf16[2,512,2048]{2,1,0:T(8,128)(2,1)} %param.27, f32[2,128,6,512]{3,1,2,0:T(8,128)} %fusion, bf16[2,2048,512]{2,1,0:T(8,128)(2,1)} %param.25, bf16[128,2,6,2048]{3,1,2,0:T(2,128)(2,1)} %copy-done.5), kind=kOutput, calls=%fused_computation.5 | convolution fusion | flops 6450315264 | bytes 24117248 | tf_op jit(solution)/shard_map/nesh,ehd->nesd/dot_general | solution.py:211
  189.1 12.7 %copy.109 = bf16[128,2,6,2048]{3,1,2,0:T(2,128)(2,1)} copy(bf16[128,2,6,2048]{3,0,2,1:T(8,128)(2,1)} %convert_bitcast_fusion) | data formatting | bytes 12582912 | tf_op jit(solution)/shard_map/convert_element_type | solution.py:213
  201.8 4.9 all-to-all-start.1
  208.6 10.3 %gather_fusion.1 = f32[1280]{0:T(1024)S(1)} fusion(f32[128,256]{1,0:T(8,128)S(1)} %fusion.56, s32[1280]{0:T(1024)S(1)} %reshape.234), kind=kCustom, calls=%fused_computation.2 | custom fusion | bytes 20480 | tf_op jit(solution)/shard_map/jit(take_along_axis)/gather | solution.py:188
  219.3 64.5 %all-to-all-done.1 = bf16[128,2,6,2048]{3,1,2,0:T(2,128)(2,1)} async-done(((bf16[128,2,6,2048]{3,1,2,0:T(2,128)(2,1)}), bf16[128,2,6,2048]{3,1,2,0:T(2,128)(2,1)}, u32[]{:S(2)}, u32[]{:S(2)}) %all-to-all-start.1) | async-done | bytes 6291488 | tf_op jit(solution)/shard_map/all_to_all | solution.py:210
  283.8 10.4 %copy.110 = bf16[128,2,6,2048]{3,2,1,0:T(8,128)(2,1)} copy(bf16[128,2,6,2048]{3,1,2,0:T(2,128)(2,1)} %all-to-all-done.1) | data formatting | bytes 12582912 | tf_op jit(solution)/shard_map/all_to_all | solution.py:210
  294.2 11.1 %reshape.203 = bf16[1536,2048]{1,0:T(8,128)(2,1)} reshape(bf16[128,2,6,2048]{3,2,1,0:T(8,128)(2,1)} %copy.110) | data formatting | bytes 12582912 | tf_op jit(solution)/shard_map/reshape | solution.py:219
  305.2 14.4 %gather_fusion = bf16[1280,2048]{1,0:T(8,128)(2,1)} fusion(bf16[1536,2048]{1,0:T(8,128)(2,1)} %reshape.203, s32[2048]{0:T(1024)S(1)} %pad_clamp_fusion), kind=kCustom, calls=%fused_computation.1 | custom fusion | bytes 10490880 | tf_op jit(solution)/shard_map/gather | solution.py:219
  319.6 10.5 %reshape.215 = f32[128,10,2048]{2,1,0:T(8,128)} reshape(bf16[1280,2048]{1,0:T(8,128)(2,1)} %gather_fusion) | data formatting | bytes 15728640 | tf_op jit(solution)/shard_map/convert_element_type | solution.py:222
  330.2 9.6 %multiply_reduce_fusion = bf16[128,2048]{1,0:T(8,128)(2,1)S(1)} fusion(f32[128,10,2048]{2,1,0:T(8,128)} %reshape.215, f32[128,10]{1,0:T(8,128)S(1)} %copy.100), kind=kLoop, calls=%fused_computation.4 | loop fusion | flops 4980736 | bytes 11015168 | tf_op jit(solution)/shard_map/reduce_sum | solution.py:222
  341.3 28.4 %all-gather.2.cloned.1.call-done = bf16[512,2048]{1,0:T(8,128)(2,1)} async-done(((bf16[128,2048]{1,0:T(8,128)(2,1)}), bf16[512,2048]{1,0:T(8,128)(2,1)}) %all-gather.2.cloned.1.call-update) | async-done | bytes 2097168 | tf_op jit(solution)/shard_map/all_gather | solution.py:229
  387.0 6.6 %divide_multiply_fusion = f32[512,1024]{0,1:T(8,128)S(1)} fusion(f32[512,1024]{0,1:T(8,128)} %get-tuple-element.15, f32[3,1024]{0,1:T(8,128)S(1)} %convert_element_type.64, f32[1024]{0:T(1024)S(1)} %bitcast.131, f32[1024]{0:T(1024)S(1)} %bitcast.132, f32[1024]{0:T(1024)S(1)} %bitcast.133, f32[1024]{0:T(1024)S(1)} %bitcast.130), kind=kLoop, calls=%fused_computation.37 | loop fusion | flops 7340032 | bytes 4222976 | tf_op jit(solution)/shard_map/jit(silu)/mul | solution.py:252
  402.1 99.5 %delta_chunks.1 = (f32[4,512,128]{2,1,0:T(8,128)}, f32[4,512,128]{2,1,0:T(8,128)}, f32[4,128,128]{2,1,0:T(8,128)}, f32[4,128,128]{2,1,0:T(8,128)}) custom-call(f32[4,512,128]{2,1,0:T(8,128)} %bitcast.125, f32[4,512,128]{2,1,0:T(8,128)} %bitcast.124, f32[4,512,128]{2,1,0:T(8,128)} %bitcast.123, f32[4,512,1]{2,1,0:T(8,128)} %copy.114.b_ref, ...), custom_call_target="tpu_custom_call" | custom-call | tf_op jit(solution)/shard_map/delta_chunks/pallas_call | solution.py:93
  516.5 8.3 %collective-permute-start.5 = (f32[4,128,128]{2,1,0:T(8,128)S(1)}, f32[4,128,128]{2,1,0:T(8,128)}, u32[]{:S(2)}, u32[]{:S(2)}) collective-permute-start(f32[4,128,128]{2,1,0:T(8,128)S(1)} %fusion.38), channel_id=1, source_target_pairs={{0,16},{4,20},{8,24},{12,28},{16,32},{20,36},{24,40},{28,44},{32,4... | collective-permute-start | bytes 786440 | tf_op jit(solution)/shard_map/ppermute | solution.py:119
  531.0 4.9 collective-permute-start.7
  540.6 4.6 collective-permute-start.9
  545.7 5.4 collective-permute-done.9
  551.5 10.5 %collective-permute-start.10 = (f32[4,128,128]{2,1,0:T(8,128)S(1)}, f32[4,128,128]{2,1,0:T(8,128)}, u32[]{:S(2)}, u32[]{:S(2)}) collective-permute-start(f32[4,128,128]{2,1,0:T(8,128)S(1)} %fusion.35), channel_id=1, source_target_pairs={{0,4},{4,8},{8,12},{12,16},{16,20},{20,24},{24,28},{28,32},{32,36}... | collective-permute-start | bytes 786440 | tf_op jit(solution)/shard_map/ppermute | solution.py:119
  575.6 30.1 %reduce-scatter.2.cloned.1.call-done = bf16[128,2048]{1,0:T(8,128)(2,1)} async-done(((bf16[512,2048]{1,0:T(8,128)(2,1)}), bf16[128,2048]{1,0:T(8,128)(2,1)}) %reduce-scatter.2.cloned.1.call-update) | async-done | bytes 524304 | tf_op jit(solution)/shard_map/reduce_scatter | solution.py:282
  (139 shorter events, 80.7 us)
Async XLA Ops:
  7.2 565.8 %copy-start = (bf16[512,2048]{1,0:T(8,128)(2,1)S(1)}, bf16[512,2048]{1,0:T(8,128)(2,1)}, u32[]{:S(2)}) copy-start(bf16[512,2048]{1,0:T(8,128)(2,1)} %param.41) | copy-start | bytes 6291460
  70.8 89.9 %copy-start.18 = (bf16[2,2048,512]{2,1,0:T(8,128)(2,1)S(1)}, bf16[2,2048,512]{2,1,0:T(8,128)(2,1)}, u32[]{:S(2)}) copy-start(bf16[2,2048,512]{2,1,0:T(8,128)(2,1)} %param.26) | copy-start | bytes 12582916
  201.8 5.0 copy-start.7
  201.8 82.0 %all-to-all-start.1 = ((bf16[128,2,6,2048]{3,1,2,0:T(2,128)(2,1)}), bf16[128,2,6,2048]{3,1,2,0:T(2,128)(2,1)}, u32[]{:S(2)}, u32[]{:S(2)}) async-start(bf16[128,2,6,2048]{3,1,2,0:T(2,128)(2,1)} %copy.109), calls=%async_computation.1 | async-start | bytes 12582912 | tf_op jit(solution)/shard_map/all_to_all | solution.py:210
  206.7 163.0 %all-gather.2.cloned.1.call-start = ((), (), s32[]{:S(2)}) async-start(), calls=%async_computation.3 | async-start | bytes 2621440 | tf_op jit(solution)/shard_map/all_gather | solution.py:229
  330.2 9.9 %copy-start.12 = (f32[2048]{0:T(1024)S(1)}, f32[2048]{0:T(1024)}, u32[]{:S(2)}) copy-start(f32[2048]{0:T(1024)} %param.28) | copy-start | bytes 24580
  339.8 32.7 %copy-start.6 = (bf16[128,2048]{1,0:T(8,128)(2,1)}, bf16[128,2048]{1,0:T(8,128)(2,1)S(1)}, u32[]{:S(2)}) copy-start(bf16[128,2048]{1,0:T(8,128)(2,1)S(1)} %multiply_reduce_fusion) | copy-start | bytes 1572868
  341.2 264.6 %reduce-scatter.2.cloned.1.call-start = ((), (), s32[]{:S(2)}) async-start(), calls=%async_computation.4 | async-start | bytes 2621440 | tf_op jit(solution)/shard_map/reduce_scatter | solution.py:282
  375.4 5.6 copy-start.9
  375.4 5.6 copy-start.16
  377.1 4.6 copy-start.10
  377.2 9.7 %collective-permute-start = (bf16[3,1024]{0,1:T(8,128)(2,1)S(1)}, bf16[3,1024]{0,1:T(8,128)(2,1)S(1)}, u32[]{:S(2)}, u32[]{:S(2)}) collective-permute-start(bf16[3,1024]{0,1:T(8,128)(2,1)S(1)} %slice.61), channel_id=1, source_target_pairs={{0,4},{4,8},{8,12},{12,16},{16,20},{20,24},{24,28},{28,32},{32,36}... | collective-permute-start | bytes 18440 | tf_op jit(solution)/shard_map/ppermute | solution.py:114
  384.9 8.7 %copy-start.8 = (f32[4,8,64]{2,1,0:T(8,128)}, f32[4,8,64]{2,1,0:T(8,128)S(1)}, u32[]{:S(2)}) copy-start(f32[4,8,64]{2,1,0:T(8,128)S(1)} %reduce_window_sum.25.cr_ref) | copy-start | bytes 24580
  501.6 5.5 collective-permute-start.1
  503.5 8.2 %collective-permute-start.2 = (f32[4,128,128]{2,1,0:T(8,128)}, f32[4,128,128]{2,1,0:T(8,128)S(1)}, u32[]{:S(2)}, u32[]{:S(2)}) collective-permute-start(f32[4,128,128]{2,1,0:T(8,128)} %get-tuple-element.9), channel_id=1, source_target_pairs={{0,4},{4,8},{8,12},{12,16},{16,20},{20,24},{24,28},{28,32},{32,36}... | collective-permute-start | bytes 786440 | tf_op jit(solution)/shard_map/ppermute | solution.py:119
  508.6 7.6 %collective-permute-start.3 = (f32[4,128,128]{2,1,0:T(8,128)S(1)}, f32[4,128,128]{2,1,0:T(8,128)S(1)}, u32[]{:S(2)}, u32[]{:S(2)}) collective-permute-start(f32[4,128,128]{2,1,0:T(8,128)S(1)} %fusion.39), channel_id=1, source_target_pairs={{0,8},{4,12},{8,16},{12,20},{16,24},{20,28},{24,32},{28,36},{32,40... | collective-permute-start | bytes 786440 | tf_op jit(solution)/shard_map/ppermute | solution.py:119
  513.2 11.6 %collective-permute-start.4 = (f32[4,128,128]{2,1,0:T(8,128)S(1)}, f32[4,128,128]{2,1,0:T(8,128)S(1)}, u32[]{:S(2)}, u32[]{:S(2)}) collective-permute-start(f32[4,128,128]{2,1,0:T(8,128)S(1)} %convolution_select_fusion.3), channel_id=1, source_target_pairs={{0,8},{4,12},{8,16},{12,20},{16,24},{20,28},{24,32},{28,36},{32,40... | collective-permute-start | bytes 786440 | tf_op jit(solution)/shard_map/ppermute | solution.py:119
  516.5 13.1 %collective-permute-start.5 = (f32[4,128,128]{2,1,0:T(8,128)S(1)}, f32[4,128,128]{2,1,0:T(8,128)}, u32[]{:S(2)}, u32[]{:S(2)}) collective-permute-start(f32[4,128,128]{2,1,0:T(8,128)S(1)} %fusion.38), channel_id=1, source_target_pairs={{0,16},{4,20},{8,24},{12,28},{16,32},{20,36},{24,40},{28,44},{32,4... | collective-permute-start | bytes 786440 | tf_op jit(solution)/shard_map/ppermute | solution.py:119
  525.3 10.6 %collective-permute-start.6 = (f32[4,128,128]{2,1,0:T(8,128)S(1)}, f32[4,128,128]{2,1,0:T(8,128)S(1)}, u32[]{:S(2)}, u32[]{:S(2)}) collective-permute-start(f32[4,128,128]{2,1,0:T(8,128)S(1)} %convolution_select_fusion.2), channel_id=1, source_target_pairs={{0,16},{4,20},{8,24},{12,28},{16,32},{20,36},{24,40},{28,44},{32,4... | collective-permute-start | bytes 786440 | tf_op jit(solution)/shard_map/ppermute | solution.py:119
  531.0 8.3 %collective-permute-start.7 = (f32[4,128,128]{2,1,0:T(8,128)S(1)}, f32[4,128,128]{2,1,0:T(8,128)}, u32[]{:S(2)}, u32[]{:S(2)}) collective-permute-start(f32[4,128,128]{2,1,0:T(8,128)S(1)} %fusion.37), channel_id=1, source_target_pairs={{0,32},{4,36},{8,40},{12,44},{16,48},{20,52},{24,56},{28,60},{32,6... | collective-permute-start | bytes 786440 | tf_op jit(solution)/shard_map/ppermute | solution.py:119
  536.3 9.0 %collective-permute-start.8 = (f32[4,128,128]{2,1,0:T(8,128)S(1)}, f32[4,128,128]{2,1,0:T(8,128)S(1)}, u32[]{:S(2)}, u32[]{:S(2)}) collective-permute-start(f32[4,128,128]{2,1,0:T(8,128)S(1)} %convolution_select_fusion.1), channel_id=1, source_target_pairs={{0,32},{4,36},{8,40},{12,44},{16,48},{20,52},{24,56},{28,60},{32,6... | collective-permute-start | bytes 786440 | tf_op jit(solution)/shard_map/ppermute | solution.py:119
  540.6 10.5 %collective-permute-start.9 = (f32[4,128,128]{2,1,0:T(8,128)S(1)}, f32[4,128,128]{2,1,0:T(8,128)S(1)}, u32[]{:S(2)}, u32[]{:S(2)}) collective-permute-start(f32[4,128,128]{2,1,0:T(8,128)S(1)} %fusion.36), channel_id=1, source_target_pairs={{0,64},{4,68},{8,72},{12,76},{16,80},{20,84},{24,88},{28,92},{32,9... | collective-permute-start | bytes 786440 | tf_op jit(solution)/shard_map/ppermute | solution.py:119
  551.5 16.1 %collective-permute-start.10 = (f32[4,128,128]{2,1,0:T(8,128)S(1)}, f32[4,128,128]{2,1,0:T(8,128)}, u32[]{:S(2)}, u32[]{:S(2)}) collective-permute-start(f32[4,128,128]{2,1,0:T(8,128)S(1)} %fusion.35), channel_id=1, source_target_pairs={{0,4},{4,8},{8,12},{12,16},{16,20},{20,24},{24,28},{28,32},{32,36}... | collective-permute-start | bytes 786440 | tf_op jit(solution)/shard_map/ppermute | solution.py:119
  567.6 3.0 copy-start.17
  (12 other events, 20.2 us)
Sparse Core Ops, SparseCore 0:
  341.3 28.4 all-gather.1
  575.7 29.9 reduce-scatter.1

commit v2 on v1

--- a/solution.py
+++ b/solution.py
@@ -10,6 +10,8 @@
 DK = 128
 HI = lax.Precision.HIGHEST
 CHUNK = 64
+UNROLL = 2
+epsilon = 1e-06
 
 
 def _mm(a, b):
@@ -26,7 +28,7 @@
                            preferred_element_type=jnp.float32)
 
 
-def delta_kernel(q_ref, k_ref, v_ref, b_ref, cc_ref, cr_ref, res_ref, read_ref, t_ref, o_ref):
+def delta_kernel(q_ref, k_ref, v_ref, b_ref, cc_ref, cr_ref, out_ref, carry_ref):
     length, kw = q_ref.shape[1], q_ref.shape[2]
     vw = v_ref.shape[2]
     n_chunks = length // CHUNK
@@ -35,12 +37,13 @@
     strict = row > col
     inclusive = row >= col
     eye_c = jnp.where(row == col, 1.0, 0.0).astype(jnp.float32)
-    krow = lax.broadcasted_iota(jnp.int32, (kw, kw), 0)
-    kcol = lax.broadcasted_iota(jnp.int32, (kw, kw), 1)
-    eye_k = jnp.where(krow == kcol, 1.0, 0.0).astype(jnp.float32)
+    lane = lax.broadcasted_iota(jnp.int32, (CHUNK, vw + kw), 1)
+    value_lanes = lane < vw
+    krow = lax.broadcasted_iota(jnp.int32, (kw, vw + kw), 0)
+    kcol = lax.broadcasted_iota(jnp.int32, (kw, vw + kw), 1)
+    carry0 = jnp.where(kcol - vw == krow, 1.0, 0.0).astype(jnp.float32)
 
     def body(c, carry):
-        state, transfer = carry
         rows = pl.ds(pl.multiple_of(c * CHUNK, CHUNK), CHUNK)
         q = q_ref[0, rows, :]
         k = k_ref[0, rows, :]
@@ -60,25 +63,19 @@
             inv = inv - _mm(_mm(inv, e), inv)
             size *= 2
         ec = jnp.exp(cum_c)
-        w_values = _mm(inv, beta * v)
-        w_keys = _mm(inv, (beta * ec) * k)
+        solved = _mm(inv, jnp.concatenate([beta * v, (beta * ec) * k], axis=1))
+        w_values = jnp.where(value_lanes, solved, 0.0)
+        w_keys = solved[:, vw:]
         mixing = fall_i * _mm_nt(q, k)
         q_dec = ec * q
         last = cum_r[:, CHUNK - 1:CHUNK]
         k_dec = jnp.exp(last - cum_c) * k
         closing = jnp.exp(last)
-        update = w_values - _mm(w_keys, state)
-        res_ref[0, rows, :] = _mm(q_dec, state) + _mm(mixing, update)
-        moved = _mm(w_keys, transfer)
-        read_ref[0, rows, :] = _mm(q_dec, transfer) - _mm(mixing, moved)
-        state = closing * state + _mm_tn(k_dec, update)
-        transfer = closing * transfer - _mm_tn(k_dec, moved)
-        return state, transfer
-
-    state0 = jnp.zeros((kw, vw), jnp.float32)
-    state, transfer = lax.fori_loop(0, n_chunks, body, (state0, eye_k))
-    t_ref[0] = transfer
-    o_ref[0] = state
+        change = w_values - _mm(w_keys, carry)
+        out_ref[0, rows, :] = _mm(q_dec, carry) + _mm(mixing, change)
+        return closing * carry + _mm_tn(k_dec, change)
+
+    carry_ref[0] = lax.fori_loop(0, n_chunks, body, carry0, unroll=UNROLL)
 
 
 def local_delta(queries, key_rows, values, strength, decays):
@@ -89,23 +86,17 @@
     cum_col = cum.reshape(heads, length, 1)
     beta_col = strength.reshape(heads, length, 1)
     seq = lambda w: pl.BlockSpec((1, length, w), lambda h: (h, 0, 0))
-    mat = pl.BlockSpec((1, kw, vw), lambda h: (h, 0, 0))
-    return pl.pallas_call(
+    out, carry = pl.pallas_call(
         delta_kernel,
         grid=(heads,),
         in_specs=[seq(kw), seq(kw), seq(vw), seq(1), seq(1),
                   pl.BlockSpec((1, n_chunks, CHUNK), lambda h: (h, 0, 0))],
-        out_specs=[seq(vw), seq(vw), mat, mat],
-        out_shape=[jax.ShapeDtypeStruct((heads, length, vw), jnp.float32),
-                   jax.ShapeDtypeStruct((heads, length, vw), jnp.float32),
-                   jax.ShapeDtypeStruct((heads, kw, vw), jnp.float32),
-                   jax.ShapeDtypeStruct((heads, kw, vw), jnp.float32)],
+        out_specs=[seq(vw + kw), pl.BlockSpec((1, kw, vw + kw), lambda h: (h, 0, 0))],
+        out_shape=[jax.ShapeDtypeStruct((heads, length, vw + kw), jnp.float32),
+                   jax.ShapeDtypeStruct((heads, kw, vw + kw), jnp.float32)],
         name="delta_chunks",
     )(queries, key_rows, values, beta_col, cum_col, cum)
-
-
-epsilon = 1e-06
-exact_precision = lax.Precision.HIGHEST
+    return out, carry
 
 
 def passed_along(value, axis, steps):
@@ -123,18 +114,22 @@
     return jnp.einsum("hij,hjk->hik", a, b, precision=HI)
 
 
-def incoming_state(transfer, offset, axis):
+def incoming_state(pair, axis):
     count, place = lax.axis_size(axis), lax.axis_index(axis)
+    value_width = pair.shape[2] - pair.shape[1]
+    offset_lanes = lax.broadcasted_iota(jnp.int32, pair.shape, 2) < value_width
     steps = 1
     while steps < count:
-        far_offset = shifted(offset, axis, steps)
         reached = place >= steps
+        transfer = pair[..., value_width:]
         if 2 * steps < count:
-            far_transfer = shifted(transfer, axis, steps)
-            offset = jnp.where(reached, offset + batched_mm(transfer, far_offset), offset)
-            transfer = jnp.where(reached, batched_mm(transfer, far_transfer), transfer)
+            far = shifted(pair, axis, steps)
+            joined = batched_mm(transfer, far) + jnp.where(offset_lanes, pair, 0.0)
+            pair = jnp.where(reached, joined, pair)
         else:
-            offset = jnp.where(reached, offset + batched_mm(transfer, far_offset), offset)
+            far = shifted(pair[..., :value_width], axis, steps)
+            offset = pair[..., :value_width]
+            offset = jnp.where(reached, offset + batched_mm(transfer, far), offset)
         steps *= 2
     return shifted(offset, axis, 1)
 
@@ -185,7 +180,8 @@
     capacity = (11 * tok_rows * top_count + 10 * experts_all - 1) // (10 * experts_all)
     normed = rms_rows(stream, moe_gain).astype(jnp.bfloat16)
     logits = jnp.dot(normed, router, preferred_element_type=jnp.float32)
-    chosen = jnp.take_along_axis(logits, expert_ids, axis=1)
+    expert_hit = expert_ids[:, :, None] == jnp.arange(experts_all, dtype=jnp.int32)[None, None, :]
+    chosen = jnp.sum(jnp.where(expert_hit, logits[:, None, :], 0.0), axis=2)
     raised = jnp.exp(chosen)
     weights = raised / jnp.sum(raised, axis=1, keepdims=True)
     flat_ids = expert_ids.reshape(-1)
@@ -194,12 +190,13 @@
     )
     slot_index = jnp.sum((jnp.cumsum(matches, axis=0) - 1) * matches, axis=1)
     places = flat_ids * capacity + slot_index
-    token_rows = jnp.arange(tok_rows * top_count, dtype=jnp.int32) // top_count
-    outgoing = (
-        jnp.zeros((experts_all * capacity, model_width), jnp.bfloat16)
-        .at[places]
-        .set(normed[token_rows])
-    )
+    slot_count = experts_all * capacity
+    place_rows = places.reshape(tok_rows, top_count)
+    slot_ids = jnp.arange(slot_count, dtype=jnp.int32)
+    take = jnp.sum((place_rows[None, :, :] == slot_ids[:, None, None]).astype(jnp.float32), axis=2)
+    outgoing = jnp.dot(
+        take.astype(jnp.bfloat16), normed, preferred_element_type=jnp.float32
+    ).astype(jnp.bfloat16)
     outgoing = outgoing.reshape(sources, local_experts, capacity, model_width)
     received = lax.all_to_all(outgoing, ("ctx", "head"), split_axis=0, concat_axis=0, tiled=True)
     gate_part = jnp.einsum(
@@ -216,12 +213,12 @@
         concat_axis=0,
         tiled=True,
     )
-    gathered_rows = returned.reshape(experts_all * capacity, model_width)[places].reshape(
-        tok_rows, top_count, model_width
-    )
-    moe_out = jnp.sum(weights[:, :, None] * gathered_rows.astype(jnp.float32), axis=1).astype(
-        jnp.bfloat16
-    )
+    mix = jnp.sum(
+        jnp.where(place_rows[:, :, None] == slot_ids[None, None, :], weights[:, :, None], 0.0), axis=1
+    )
+    moe_out = jnp.dot(
+        mix, returned.reshape(slot_count, model_width).astype(jnp.float32), precision=HI
+    ).astype(jnp.bfloat16)
     mixer_in = rms_rows(
         stream.astype(jnp.float32) + moe_out.astype(jnp.float32), mixer_gain
     ).astype(jnp.bfloat16)
@@ -260,12 +257,13 @@
     decays = -jnp.exp(decay_log)[None, :] * jax.nn.softplus(decay_raw + decay_bias[None, :])
     query_heads = jnp.repeat(queries, group_size, axis=1).transpose(1, 0, 2)
     key_head_rows = jnp.repeat(key_rows, group_size, axis=1).transpose(1, 0, 2)
-    output_list, read_values, transfer, offset = local_delta(
+    core_parts, carry = local_delta(
         query_heads, key_head_rows, values.transpose(1, 0, 2), strength.T, decays.T
     )
-    incoming_rows = incoming_state(transfer, offset, "ctx")
-    delta_core_output = output_list + jnp.einsum(
-        "wnc,wcg->wng", read_values, incoming_rows, precision=exact_precision
+    incoming_rows = incoming_state(carry, "ctx")
+    value_width = values.shape[2]
+    delta_core_output = core_parts[..., :value_width] + jnp.einsum(
+        "wnc,wcg->wng", core_parts[..., value_width:], incoming_rows, precision=HI
     )
     delta_core_output = delta_core_output.transpose(1, 0, 2)
     normal = (

time: 618 us -> 577 us (0.934)
  local copies, waits for them, and re-layouts: 144 us -> 78.5 us
  waiting for transfers between devices: 129 us -> 171 us
  starting transfers between devices: 56 us -> 40.1 us
  matrix products: 53.5 us -> 64.2 us
  other arithmetic: 28.8 us -> 18.4 us
    scatter x1 -> x0, local copies, waits for them, and re-layouts: 34.1 us -> none  [on_device(): outgoing = jnp.zeros((experts_all * capacity, model_width), jnp.bfloat16)...]
    ppermute x10 -> x6, waiting for transfers between devices: 5.44 us -> 37.9 us  [shifted(): lax.ppermute(value, axis, [(source, source + steps) for source in range(c...]
    gather x6 -> x0, local copies, waits for them, and re-layouts: 25.2 us -> none  [the longest x1 14.4 us: on_device(): returned.reshape(experts_all * capacity, model_width)[places]]
    ppermute x10 -> x6, starting transfers between devices: 47.3 us -> 31.3 us  [shifted(): lax.ppermute(value, axis, [(source, source + steps) for source in range(c...]
    convert_element_type x1 -> x0, local copies, waits for them, and re-layouts: 10.5 us -> none  [on_device(): gathered_rows.astype(jnp.float32)]
    dot_general x1 -> x3, matrix products: 2.95 us -> 13.1 us  [the longest x1 5.61 us: on_device(): jnp.dot(mix, returned.reshape(slot_count, model_width).astype(jnp.float32...]
    all_to_all x1, waiting for transfers between devices: 64.5 us -> 73.5 us  [on_device(): lax.all_to_all(jnp.einsum('nesh,ehd->nesd', hidden, expert_down, preferre...]
    reduce_sum x1 -> x3, other arithmetic: 9.59 us -> 2.76 us  [the longest x1 1.39 us: on_device(): jnp.sum(jnp.where(place_rows[:, :, None] == slot_ids[None, None, :], weig...]
  transfers between devices with their start and end apart: 14 -> 10, of which waited for: 4 -> 8; matrix products, arithmetic and copies ran while one was open for 5% -> 3% of each run, Pallas kernels for 0% -> 0%
where the time goes in v2:
time: 577 us; the launch traced here: 570 us
  waiting for transfers between devices  171 us (30%)
  Pallas kernels  95.5 us (17%)
  blocking collectives  87.7 us (15%)
  local copies, waits for them, and re-layouts  78.5 us (14%)
  matrix products  64.2 us (11%)
  starting transfers between devices  40.1 us (7%)
  other arithmetic  18.4 us (3%)
  between operations  15.1 us (3%)
    pallas_call x1, Pallas kernels, local_delta(): pl.pallas_call(delta_kernel, grid=(heads,), in_specs=[seq(kw), seq(kw), s...  95.5 us
    all_to_all x1, blocking collectives, on_device(): lax.all_to_all(outgoing, ('ctx', 'head'), split_axis=0, concat_axis=0, ti...  87.7 us
    all_to_all x1, waiting for transfers between devices, on_device(): lax.all_to_all(jnp.einsum('nesh,ehd->nesd', hidden, expert_down, preferre...  73.5 us
    ppermute x6, waiting for transfers between devices, shifted(): lax.ppermute(value, axis, [(source, source + steps) for source in range(c...  37.9 us
    ppermute x6, starting transfers between devices, shifted(): lax.ppermute(value, axis, [(source, source + steps) for source in range(c...  31.3 us
    reduce_scatter x1, waiting for transfers between devices, on_device(): lax.psum_scatter(jnp.dot(gated_out, out_weight, preferred_element_type=jn...  30.7 us
    all_gather x1, waiting for transfers between devices, on_device(): piece_rows = lax.all_gather(mixer_in, 'head', axis=0, tiled=True)  28.4 us
    reshape x2, local copies, waits for them, and re-layouts, on_device(): outgoing = outgoing.reshape(sources, local_experts, capacity, model_width)  20.6 us
  transfers between devices with their start and end apart: 10, of which 8 were waited for; matrix products, arithmetic and copies ran while one was open for 3% of the time, Pallas kernels for 0%

profile of v2, /device:TPU:1, one launch (start us, length us, event | category | flops | bytes accessed | tf_op | source)
XLA Modules:
  0.0 570.2 jit_solution(3210708204180775235)
XLA Ops:
  14.7 4.6 convolution_convert_fusion
  19.3 11.0 %reshape.139 = bf16[128,2,6,2048]{3,2,1,0:T(8,128)(2,1)} reshape(bf16[1536,2048]{1,0:T(8,128)(2,1)} %convolution_convert_fusion) | data formatting | bytes 12582912 | tf_op jit(solution)/shard_map/reshape | solution.py:200
  30.3 9.6 %copy.120 = bf16[128,2,6,2048]{3,1,2,0:T(2,128)(2,1)S(1)} copy(bf16[128,2,6,2048]{3,2,1,0:T(8,128)(2,1)} %reshape.139) | data formatting | bytes 12582912 | tf_op jit(solution)/shard_map/reshape | solution.py:200
  39.9 87.7 %all_to_all.10 = bf16[128,2,6,2048]{3,1,2,0:T(2,128)(2,1)S(1)} all-to-all(bf16[128,2,6,2048]{3,1,2,0:T(2,128)(2,1)S(1)} %copy.120), channel_id=1, replica_groups=mesh['ctx'=32,'head'=4] {'ctx','head'}, dimensions={0} | all-to-all | bytes 12582912 | tf_op jit(solution)/shard_map/all_to_all | solution.py:201
  130.3 8.6 %fusion = f32[2,128,6,512]{3,1,2,0:T(8,128)} fusion(bf16[128,2,6,2048]{3,1,2,0:T(2,128)(2,1)S(1)} %all_to_all.10, bf16[2,2048,512]{2,1,0:T(8,128)(2,1)S(1)} %copy-done.19), kind=kOutput, calls=%fused_computation.6 | convolution fusion | flops 3221225472 | bytes 13631488 | tf_op jit(solution)/shard_map/nesd,edh->nesh/dot_general | solution.py:205
  138.9 19.6 %convert_bitcast_fusion = bf16[128,2,6,2048]{3,0,2,1:T(8,128)(2,1)} fusion(bf16[2,512,2048]{2,1,0:T(8,128)(2,1)} %param.27, f32[2,128,6,512]{3,1,2,0:T(8,128)} %fusion, bf16[2,2048,512]{2,1,0:T(8,128)(2,1)} %param.25, bf16[128,2,6,2048]{3,1,2,0:T(2,128)(2,1)} %copy-done.5), kind=kOutput, calls=%fused_computation.5 | convolution fusion | flops 6450315264 | bytes 24117248 | tf_op jit(solution)/shard_map/nesh,ehd->nesd/dot_general | solution.py:208
  158.5 12.8 %copy.123 = bf16[128,2,6,2048]{3,1,2,0:T(2,128)(2,1)} copy(bf16[128,2,6,2048]{3,0,2,1:T(8,128)(2,1)} %convert_bitcast_fusion) | data formatting | bytes 12582912 | tf_op jit(solution)/shard_map/convert_element_type | solution.py:210
  171.3 4.8 all-to-all-start.1
  179.6 73.5 %all-to-all-done.1 = bf16[128,2,6,2048]{3,1,2,0:T(2,128)(2,1)} async-done(((bf16[128,2,6,2048]{3,1,2,0:T(2,128)(2,1)}), bf16[128,2,6,2048]{3,1,2,0:T(2,128)(2,1)}, u32[]{:S(2)}, u32[]{:S(2)}) %all-to-all-start.1) | async-done | bytes 6291488 | tf_op jit(solution)/shard_map/all_to_all | solution.py:207
  253.1 10.4 %copy.124 = bf16[128,2,6,2048]{3,2,1,0:T(8,128)(2,1)} copy(bf16[128,2,6,2048]{3,1,2,0:T(2,128)(2,1)} %all-to-all-done.1) | data formatting | bytes 12582912 | tf_op jit(solution)/shard_map/all_to_all | solution.py:207
  263.5 11.0 %reshape.140 = bf16[1536,2048]{1,0:T(8,128)(2,1)} reshape(bf16[128,2,6,2048]{3,2,1,0:T(8,128)(2,1)} %copy.124) | data formatting | bytes 12582912 | tf_op jit(solution)/shard_map/reshape | solution.py:220
  274.5 5.6 multiply_reduce_fusion.1
  282.1 28.4 %all-gather.2.cloned.1.call-done = bf16[512,2048]{1,0:T(8,128)(2,1)} async-done(((bf16[128,2048]{1,0:T(8,128)(2,1)}), bf16[512,2048]{1,0:T(8,128)(2,1)}) %all-gather.2.cloned.1.call-update) | async-done | bytes 2097168 | tf_op jit(solution)/shard_map/all_gather | solution.py:226
  327.8 6.5 %divide_multiply_fusion = f32[512,1024]{0,1:T(8,128)S(1)} fusion(f32[512,1024]{0,1:T(8,128)} %get-tuple-element.11, f32[3,1024]{0,1:T(8,128)S(1)} %convert_element_type.69, f32[1024]{0:T(1024)S(1)} %bitcast.114, f32[1024]{0:T(1024)S(1)} %bitcast.115, f32[1024]{0:T(1024)S(1)} %bitcast.116, f32[1024]{0:T(1024)S(1)} %bitcast.113), kind=kLoop, calls=%fused_computation.35 | loop fusion | flops 7340032 | bytes 4222976 | tf_op jit(solution)/shard_map/jit(silu)/mul | solution.py:249
  345.9 95.5 %delta_chunks.1 = (f32[4,512,256]{2,1,0:T(8,128)}, f32[4,128,256]{2,1,0:T(8,128)}) custom-call(f32[4,512,128]{2,1,0:T(8,128)} %bitcast.108, f32[4,512,128]{2,1,0:T(8,128)} %bitcast.109, f32[4,512,128]{2,1,0:T(8,128)} %bitcast.107, f32[4,512,1]{2,1,0:T(8,128)} %copy.128.b_ref, f32[4,512,1]{2,1,0:T(8,128)} %reshape.157.cc_ref, f32[4,8,64]{2,1,0:T(8,128)} %copy-done.8), custom_call_target="tpu_custom_call" | custom-call | tf_op jit(solution)/shard_map/delta_chunks/pallas_call | solution.py:89
  443.3 6.4 %collective-permute-done.1 = f32[4,128,256]{2,1,0:T(8,128)S(1)} collective-permute-done((f32[4,128,256]{2,1,0:T(8,128)}, f32[4,128,256]{2,1,0:T(8,128)S(1)}, u32[]{:S(2)}, u32[]{:S(2)}) %collective-permute-start.1) | collective-permute-done | bytes 524320 | tf_op jit(solution)/shard_map/ppermute | solution.py:110
  455.5 9.2 %collective-permute-done.2 = f32[4,128,256]{2,1,0:T(8,128)} collective-permute-done((f32[4,128,256]{2,1,0:T(8,128)S(1)}, f32[4,128,256]{2,1,0:T(8,128)}, u32[]{:S(2)}, u32[]{:S(2)}) %collective-permute-start.2) | collective-permute-done | bytes 524320 | tf_op jit(solution)/shard_map/ppermute | solution.py:110
  466.3 7.7 %collective-permute-start.3 = (f32[4,128,256]{2,1,0:T(8,128)S(1)}, f32[4,128,256]{2,1,0:T(8,128)S(1)}, u32[]{:S(2)}, u32[]{:S(2)}) collective-permute-start(f32[4,128,256]{2,1,0:T(8,128)S(1)} %fusion.34), channel_id=1, source_target_pairs={{0,16},{4,20},{8,24},{12,28},{16,32},{20,36},{24,40},{28,44},{32,4... | collective-permute-start | bytes 1572872 | tf_op jit(solution)/shard_map/ppermute | solution.py:110
  474.1 10.7 %collective-permute-done.3 = f32[4,128,256]{2,1,0:T(8,128)S(1)} collective-permute-done((f32[4,128,256]{2,1,0:T(8,128)S(1)}, f32[4,128,256]{2,1,0:T(8,128)S(1)}, u32[]{:S(2)}, u32[]{:S(2)}) %collective-permute-start.3) | collective-permute-done | bytes 524320 | tf_op jit(solution)/shard_map/ppermute | solution.py:110
  490.5 8.3 %collective-permute-done.4 = f32[4,128,256]{2,1,0:T(8,128)} collective-permute-done((f32[4,128,256]{2,1,0:T(8,128)S(1)}, f32[4,128,256]{2,1,0:T(8,128)}, u32[]{:S(2)}, u32[]{:S(2)}) %collective-permute-start.4) | collective-permute-done | bytes 524320 | tf_op jit(solution)/shard_map/ppermute | solution.py:110
  500.5 4.3 collective-permute-start.5
  509.2 9.5 %collective-permute-start.6 = (f32[4,128,128]{2,1,0:T(8,128)}, f32[4,128,128]{2,1,0:T(8,128)S(1)}, u32[]{:S(2)}, u32[]{:S(2)}) collective-permute-start(f32[4,128,128]{2,1,0:T(8,128)} %fusion.36), channel_id=1, source_target_pairs={{0,4},{4,8},{8,12},{12,16},{16,20},{20,24},{24,28},{28,32},{32,36}... | collective-permute-start | bytes 786440 | tf_op jit(solution)/shard_map/ppermute | solution.py:110
  518.6 4.3 convolution_convert_fusion.3
  532.2 30.7 %reduce-scatter.2.cloned.1.call-done = bf16[128,2048]{1,0:T(8,128)(2,1)} async-done(((bf16[512,2048]{1,0:T(8,128)(2,1)}), bf16[128,2048]{1,0:T(8,128)(2,1)}) %reduce-scatter.2.cloned.1.call-update) | async-done | bytes 524304 | tf_op jit(solution)/shard_map/reduce_scatter | solution.py:280
  (120 shorter events, 74.3 us)
Async XLA Ops:
  7.2 522.4 %copy-start = (bf16[512,2048]{1,0:T(8,128)(2,1)S(1)}, bf16[512,2048]{1,0:T(8,128)(2,1)}, u32[]{:S(2)}) copy-start(bf16[512,2048]{1,0:T(8,128)(2,1)} %param.41) | copy-start | bytes 6291460
  12.1 2.6 copy-start.12
  39.9 90.4 %copy-start.19 = (bf16[2,2048,512]{2,1,0:T(8,128)(2,1)S(1)}, bf16[2,2048,512]{2,1,0:T(8,128)(2,1)}, u32[]{:S(2)}) copy-start(bf16[2,2048,512]{2,1,0:T(8,128)(2,1)} %param.26) | copy-start | bytes 12582916
  127.7 2.6 copy-start.5
  171.3 81.8 %all-to-all-start.1 = ((bf16[128,2,6,2048]{3,1,2,0:T(2,128)(2,1)}), bf16[128,2,6,2048]{3,1,2,0:T(2,128)(2,1)}, u32[]{:S(2)}, u32[]{:S(2)}) async-start(bf16[128,2,6,2048]{3,1,2,0:T(2,128)(2,1)} %copy.123), calls=%async_computation.1 | async-start | bytes 12582912 | tf_op jit(solution)/shard_map/all_to_all | solution.py:207
  176.1 134.5 %all-gather.2.cloned.1.call-start = ((), (), s32[]{:S(2)}) async-start(), calls=%async_computation.3 | async-start | bytes 2621440 | tf_op jit(solution)/shard_map/all_gather | solution.py:226
  274.5 6.4 %copy-start.13 = (f32[2048]{0:T(1024)S(1)}, f32[2048]{0:T(1024)}, u32[]{:S(2)}) copy-start(f32[2048]{0:T(1024)} %param.28) | copy-start | bytes 24580
  282.0 280.9 %reduce-scatter.2.cloned.1.call-start = ((), (), s32[]{:S(2)}) async-start(), calls=%async_computation.4 | async-start | bytes 2621440 | tf_op jit(solution)/shard_map/reduce_scatter | solution.py:280
  310.6 3.7 copy-start.4
  310.6 3.7 copy-start.20
  316.3 5.8 %copy-start.10 = (bf16[2048,4]{0,1:T(4,128)(2,1)S(1)}, bf16[2048,4]{0,1:T(4,128)(2,1)}, u32[]{:S(2)}) copy-start(bf16[2048,4]{0,1:T(4,128)(2,1)} %param.34) | copy-start | bytes 49156
  316.3 5.8 %copy-start.17 = (f32[4]{0:T(128)S(1)}, f32[4]{0:T(128)}, u32[]{:S(2)}) copy-start(f32[4]{0:T(128)} %param.39) | copy-start | bytes 52
  317.9 4.9 copy-start.11
  318.1 9.7 %collective-permute-start = (bf16[3,1024]{0,1:T(8,128)(2,1)S(1)}, bf16[3,1024]{0,1:T(8,128)(2,1)S(1)}, u32[]{:S(2)}, u32[]{:S(2)}) collective-permute-start(bf16[3,1024]{0,1:T(8,128)(2,1)S(1)} %slice.88), channel_id=1, source_target_pairs={{0,4},{4,8},{8,12},{12,16},{16,20},{20,24},{24,28},{28,32},{32,36}... | collective-permute-start | bytes 18440 | tf_op jit(solution)/shard_map/ppermute | solution.py:105
  324.4 10.0 %copy-start.8 = (f32[4,8,64]{2,1,0:T(8,128)}, f32[4,8,64]{2,1,0:T(8,128)S(1)}, u32[]{:S(2)}) copy-start(f32[4,8,64]{2,1,0:T(8,128)S(1)} %reduce_window_sum.25.cr_ref) | copy-start | bytes 24580
  336.1 4.2 slice-start
  441.4 8.3 %collective-permute-start.1 = (f32[4,128,256]{2,1,0:T(8,128)}, f32[4,128,256]{2,1,0:T(8,128)S(1)}, u32[]{:S(2)}, u32[]{:S(2)}) collective-permute-start(f32[4,128,256]{2,1,0:T(8,128)} %get-tuple-element.5), channel_id=1, source_target_pairs={{0,4},{4,8},{8,12},{12,16},{16,20},{20,24},{24,28},{28,32},{32,36}... | collective-permute-start | bytes 1572872 | tf_op jit(solution)/shard_map/ppermute | solution.py:110
  451.5 13.2 %collective-permute-start.2 = (f32[4,128,256]{2,1,0:T(8,128)S(1)}, f32[4,128,256]{2,1,0:T(8,128)}, u32[]{:S(2)}, u32[]{:S(2)}) collective-permute-start(f32[4,128,256]{2,1,0:T(8,128)S(1)} %fusion.35), channel_id=1, source_target_pairs={{0,8},{4,12},{8,16},{12,20},{16,24},{20,28},{24,32},{28,36},{32,40... | collective-permute-start | bytes 1572872 | tf_op jit(solution)/shard_map/ppermute | solution.py:110
  466.3 7.8 %copy-start.7 = (f32[4,128,256]{2,1,0:T(8,128)}, f32[4,128,256]{2,1,0:T(8,128)S(1)}, u32[]{:S(2)}) copy-start(f32[4,128,256]{2,1,0:T(8,128)S(1)} %fusion.34) | copy-start | bytes 1572868
  466.3 18.5 %collective-permute-start.3 = (f32[4,128,256]{2,1,0:T(8,128)S(1)}, f32[4,128,256]{2,1,0:T(8,128)S(1)}, u32[]{:S(2)}, u32[]{:S(2)}) collective-permute-start(f32[4,128,256]{2,1,0:T(8,128)S(1)} %fusion.34), channel_id=1, source_target_pairs={{0,16},{4,20},{8,24},{12,28},{16,32},{20,36},{24,40},{28,44},{32,4... | collective-permute-start | bytes 1572872 | tf_op jit(solution)/shard_map/ppermute | solution.py:110
  486.6 12.2 %collective-permute-start.4 = (f32[4,128,256]{2,1,0:T(8,128)S(1)}, f32[4,128,256]{2,1,0:T(8,128)}, u32[]{:S(2)}, u32[]{:S(2)}) collective-permute-start(f32[4,128,256]{2,1,0:T(8,128)S(1)} %fusion.33), channel_id=1, source_target_pairs={{0,32},{4,36},{8,40},{12,44},{16,48},{20,52},{24,56},{28,60},{32,6... | collective-permute-start | bytes 1572872 | tf_op jit(solution)/shard_map/ppermute | solution.py:110
  500.5 7.6 %collective-permute-start.5 = (f32[4,128,128]{2,1,0:T(8,128)S(1)}, f32[4,128,128]{2,1,0:T(8,128)S(1)}, u32[]{:S(2)}, u32[]{:S(2)}) collective-permute-start(f32[4,128,128]{2,1,0:T(8,128)S(1)} %slice.102), channel_id=1, source_target_pairs={{0,64},{4,68},{8,72},{12,76},{16,80},{20,84},{24,88},{28,92},{32,9... | collective-permute-start | bytes 786440 | tf_op jit(solution)/shard_map/ppermute | solution.py:110
  509.2 15.0 %collective-permute-start.6 = (f32[4,128,128]{2,1,0:T(8,128)}, f32[4,128,128]{2,1,0:T(8,128)S(1)}, u32[]{:S(2)}, u32[]{:S(2)}) collective-permute-start(f32[4,128,128]{2,1,0:T(8,128)} %fusion.36), channel_id=1, source_target_pairs={{0,4},{4,8},{8,12},{12,16},{16,20},{20,24},{24,28},{28,32},{32,36}... | collective-permute-start | bytes 786440 | tf_op jit(solution)/shard_map/ppermute | solution.py:110
  522.9 4.2 copy-start.18
  (10 other events, 16.5 us)
Sparse Core Ops, SparseCore 0:
  282.1 28.4 all-gather.1
  532.3 30.5 reduce-scatter.1

commit v3 on v2

--- a/solution.py
+++ b/solution.py
@@ -10,7 +10,6 @@
 DK = 128
 HI = lax.Precision.HIGHEST
 CHUNK = 64
-UNROLL = 2
 epsilon = 1e-06
 
 
@@ -29,7 +28,7 @@
 
 
 def delta_kernel(q_ref, k_ref, v_ref, b_ref, cc_ref, cr_ref, out_ref, carry_ref):
-    length, kw = q_ref.shape[1], q_ref.shape[2]
+    heads, length, kw = q_ref.shape
     vw = v_ref.shape[2]
     n_chunks = length // CHUNK
     row = lax.broadcasted_iota(jnp.int32, (CHUNK, CHUNK), 0)
@@ -37,26 +36,27 @@
     strict = row > col
     inclusive = row >= col
     eye_c = jnp.where(row == col, 1.0, 0.0).astype(jnp.float32)
+    pairs = ((row // 2) == (col // 2)) & (row != col)
     lane = lax.broadcasted_iota(jnp.int32, (CHUNK, vw + kw), 1)
     value_lanes = lane < vw
     krow = lax.broadcasted_iota(jnp.int32, (kw, vw + kw), 0)
     kcol = lax.broadcasted_iota(jnp.int32, (kw, vw + kw), 1)
     carry0 = jnp.where(kcol - vw == krow, 1.0, 0.0).astype(jnp.float32)
 
-    def body(c, carry):
+    def one_head(h, c, carry):
         rows = pl.ds(pl.multiple_of(c * CHUNK, CHUNK), CHUNK)
-        q = q_ref[0, rows, :]
-        k = k_ref[0, rows, :]
-        v = v_ref[0, rows, :]
-        beta = b_ref[0, rows, :]
-        cum_c = cc_ref[0, rows, :]
-        cum_r = cr_ref[0, pl.ds(c, 1), :]
+        q = q_ref[h, rows, :]
+        k = k_ref[h, rows, :]
+        v = v_ref[h, rows, :]
+        beta = b_ref[h, rows, :]
+        cum_c = cc_ref[h, rows, :]
+        cum_r = cr_ref[h, pl.ds(c, 1), :]
         spread = cum_c - cum_r
         fall_s = jnp.where(strict, jnp.exp(jnp.where(strict, spread, 0.0)), 0.0)
         fall_i = jnp.where(inclusive, jnp.exp(jnp.where(inclusive, spread, 0.0)), 0.0)
         a = beta * fall_s * _mm_nt(k, k)
-        inv = eye_c
-        size = 1
+        inv = eye_c - jnp.where(pairs, a, 0.0)
+        size = 2
         while size < CHUNK:
             band = ((row // (2 * size)) == (col // (2 * size))) & ((row // size) != (col // size))
             e = jnp.where(band, a, 0.0)
@@ -72,10 +72,15 @@
         k_dec = jnp.exp(last - cum_c) * k
         closing = jnp.exp(last)
         change = w_values - _mm(w_keys, carry)
-        out_ref[0, rows, :] = _mm(q_dec, carry) + _mm(mixing, change)
+        out_ref[h, rows, :] = _mm(q_dec, carry) + _mm(mixing, change)
         return closing * carry + _mm_tn(k_dec, change)
 
-    carry_ref[0] = lax.fori_loop(0, n_chunks, body, carry0, unroll=UNROLL)
+    def body(c, carries):
+        return tuple(one_head(h, c, carries[h]) for h in range(heads))
+
+    carries = lax.fori_loop(0, n_chunks, body, (carry0,) * heads)
+    for h in range(heads):
+        carry_ref[h] = carries[h]
 
 
 def local_delta(queries, key_rows, values, strength, decays):
@@ -85,18 +90,17 @@
     cum = jnp.cumsum(decays.reshape(heads, n_chunks, CHUNK), axis=-1)
     cum_col = cum.reshape(heads, length, 1)
     beta_col = strength.reshape(heads, length, 1)
-    seq = lambda w: pl.BlockSpec((1, length, w), lambda h: (h, 0, 0))
-    out, carry = pl.pallas_call(
+    whole = lambda *shape: pl.BlockSpec(shape, lambda i: (0,) * len(shape))
+    return pl.pallas_call(
         delta_kernel,
-        grid=(heads,),
-        in_specs=[seq(kw), seq(kw), seq(vw), seq(1), seq(1),
-                  pl.BlockSpec((1, n_chunks, CHUNK), lambda h: (h, 0, 0))],
-        out_specs=[seq(vw + kw), pl.BlockSpec((1, kw, vw + kw), lambda h: (h, 0, 0))],
+        grid=(1,),
+        in_specs=[whole(heads, length, kw), whole(heads, length, kw), whole(heads, length, vw),
+                  whole(heads, length, 1), whole(heads, length, 1), whole(heads, n_chunks, CHUNK)],
+        out_specs=[whole(heads, length, vw + kw), whole(heads, kw, vw + kw)],
         out_shape=[jax.ShapeDtypeStruct((heads, length, vw + kw), jnp.float32),
                    jax.ShapeDtypeStruct((heads, kw, vw + kw), jnp.float32)],
         name="delta_chunks",
     )(queries, key_rows, values, beta_col, cum_col, cum)
-    return out, carry
 
 
 def passed_along(value, axis, steps):

time: 577 us -> 567 us (0.983)
  Pallas kernels: 95.5 us -> 86.5 us
    pallas_call x1, Pallas kernels: 95.5 us -> 86.5 us  [local_delta(): pl.pallas_call(delta_kernel, grid=(1,), in_specs=[whole(heads, length, kw...]
where the time goes in v3:
time: 567 us; the launch traced here: 560 us
  waiting for transfers between devices  170 us (30%)
  blocking collectives  87.7 us (15%)
  Pallas kernels  86.5 us (15%)
  local copies, waits for them, and re-layouts  78.5 us (14%)
  matrix products  64.2 us (11%)
  starting transfers between devices  39.9 us (7%)
  other arithmetic  18.5 us (3%)
  between operations  14.8 us (3%)
    all_to_all x1, blocking collectives, on_device(): lax.all_to_all(outgoing, ('ctx', 'head'), split_axis=0, concat_axis=0, ti...  87.7 us
    pallas_call x1, Pallas kernels, local_delta(): pl.pallas_call(delta_kernel, grid=(1,), in_specs=[whole(heads, length, kw...  86.5 us
    all_to_all x1, waiting for transfers between devices, on_device(): lax.all_to_all(jnp.einsum('nesh,ehd->nesd', hidden, expert_down, preferre...  73.5 us
    ppermute x6, waiting for transfers between devices, shifted(): lax.ppermute(value, axis, [(source, source + steps) for source in range(c...  37.4 us
    ppermute x6, starting transfers between devices, shifted(): lax.ppermute(value, axis, [(source, source + steps) for source in range(c...  30.9 us
    reduce_scatter x1, waiting for transfers between devices, on_device(): lax.psum_scatter(jnp.dot(gated_out, out_weight, preferred_element_type=jn...  30.8 us
    all_gather x1, waiting for transfers between devices, on_device(): piece_rows = lax.all_gather(mixer_in, 'head', axis=0, tiled=True)  28.4 us
    reshape x2, local copies, waits for them, and re-layouts, on_device(): outgoing = outgoing.reshape(sources, local_experts, capacity, model_width)  20.6 us
  transfers between devices with their start and end apart: 10, of which 8 were waited for; matrix products, arithmetic and copies ran while one was open for 3% of the time, Pallas kernels for 0%

profile of v3, /device:TPU:1, one launch (start us, length us, event | category | flops | bytes accessed | tf_op | source)
XLA Modules:
  0.0 560.3 jit_solution(15817495479098274115)
XLA Ops:
  14.7 4.6 convolution_convert_fusion
  19.3 11.0 %reshape.139 = bf16[128,2,6,2048]{3,2,1,0:T(8,128)(2,1)} reshape(bf16[1536,2048]{1,0:T(8,128)(2,1)} %convolution_convert_fusion) | data formatting | bytes 12582912 | tf_op jit(solution)/shard_map/reshape | solution.py:204
  30.3 9.6 %copy.120 = bf16[128,2,6,2048]{3,1,2,0:T(2,128)(2,1)S(1)} copy(bf16[128,2,6,2048]{3,2,1,0:T(8,128)(2,1)} %reshape.139) | data formatting | bytes 12582912 | tf_op jit(solution)/shard_map/reshape | solution.py:204
  39.9 87.7 %all_to_all.10 = bf16[128,2,6,2048]{3,1,2,0:T(2,128)(2,1)S(1)} all-to-all(bf16[128,2,6,2048]{3,1,2,0:T(2,128)(2,1)S(1)} %copy.120), channel_id=1, replica_groups=mesh['ctx'=32,'head'=4] {'ctx','head'}, dimensions={0} | all-to-all | bytes 12582912 | tf_op jit(solution)/shard_map/all_to_all | solution.py:205
  130.3 8.6 %fusion = f32[2,128,6,512]{3,1,2,0:T(8,128)} fusion(bf16[128,2,6,2048]{3,1,2,0:T(2,128)(2,1)S(1)} %all_to_all.10, bf16[2,2048,512]{2,1,0:T(8,128)(2,1)S(1)} %copy-done.19), kind=kOutput, calls=%fused_computation.6 | convolution fusion | flops 3221225472 | bytes 13631488 | tf_op jit(solution)/shard_map/nesd,edh->nesh/dot_general | solution.py:209
  138.9 19.6 %convert_bitcast_fusion = bf16[128,2,6,2048]{3,0,2,1:T(8,128)(2,1)} fusion(bf16[2,512,2048]{2,1,0:T(8,128)(2,1)} %param.27, f32[2,128,6,512]{3,1,2,0:T(8,128)} %fusion, bf16[2,2048,512]{2,1,0:T(8,128)(2,1)} %param.25, bf16[128,2,6,2048]{3,1,2,0:T(2,128)(2,1)} %copy-done.5), kind=kOutput, calls=%fused_computation.5 | convolution fusion | flops 6450315264 | bytes 24117248 | tf_op jit(solution)/shard_map/nesh,ehd->nesd/dot_general | solution.py:212
  158.5 12.8 %copy.123 = bf16[128,2,6,2048]{3,1,2,0:T(2,128)(2,1)} copy(bf16[128,2,6,2048]{3,0,2,1:T(8,128)(2,1)} %convert_bitcast_fusion) | data formatting | bytes 12582912 | tf_op jit(solution)/shard_map/convert_element_type | solution.py:214
  171.3 4.8 all-to-all-start.1
  179.6 73.5 %all-to-all-done.1 = bf16[128,2,6,2048]{3,1,2,0:T(2,128)(2,1)} async-done(((bf16[128,2,6,2048]{3,1,2,0:T(2,128)(2,1)}), bf16[128,2,6,2048]{3,1,2,0:T(2,128)(2,1)}, u32[]{:S(2)}, u32[]{:S(2)}) %all-to-all-start.1) | async-done | bytes 6291488 | tf_op jit(solution)/shard_map/all_to_all | solution.py:211
  253.1 10.4 %copy.124 = bf16[128,2,6,2048]{3,2,1,0:T(8,128)(2,1)} copy(bf16[128,2,6,2048]{3,1,2,0:T(2,128)(2,1)} %all-to-all-done.1) | data formatting | bytes 12582912 | tf_op jit(solution)/shard_map/all_to_all | solution.py:211
  263.5 11.0 %reshape.140 = bf16[1536,2048]{1,0:T(8,128)(2,1)} reshape(bf16[128,2,6,2048]{3,2,1,0:T(8,128)(2,1)} %copy.124) | data formatting | bytes 12582912 | tf_op jit(solution)/shard_map/reshape | solution.py:224
  274.5 5.6 %multiply_reduce_fusion.1 = (f32[128]{0:T(128)S(1)}, bf16[128,2048]{1,0:T(8,128)(2,1)S(1)}) fusion(bf16[128,2048]{1,0:T(8,128)(2,1)S(1)} %copy-done.3, f32[128,1536]{1,0:T(8,128)S(1)} %select_reduce_fusion, bf16[1536,2048]{1,0:T(8,128)(2,1)} %reshape.140), kind=kOutput, calls=%fused_computation.80 | convolution fusion | flops 4833411072 | bytes 8126976 | tf_op jit(solution)/shard_map/dot_general | solution.py:223
  282.1 28.4 %all-gather.2.cloned.1.call-done = bf16[512,2048]{1,0:T(8,128)(2,1)} async-done(((bf16[128,2048]{1,0:T(8,128)(2,1)}), bf16[512,2048]{1,0:T(8,128)(2,1)}) %all-gather.2.cloned.1.call-update) | async-done | bytes 2097168 | tf_op jit(solution)/shard_map/all_gather | solution.py:230
  328.0 6.5 %divide_multiply_fusion = f32[512,1024]{0,1:T(8,128)S(1)} fusion(f32[512,1024]{0,1:T(8,128)} %get-tuple-element.11, f32[3,1024]{0,1:T(8,128)S(1)} %convert_element_type.69, f32[1024]{0:T(1024)S(1)} %bitcast.114, f32[1024]{0:T(1024)S(1)} %bitcast.115, f32[1024]{0:T(1024)S(1)} %bitcast.116, f32[1024]{0:T(1024)S(1)} %bitcast.113), kind=kLoop, calls=%fused_computation.35 | loop fusion | flops 7340032 | bytes 4222976 | tf_op jit(solution)/shard_map/jit(silu)/mul | solution.py:253
  346.0 86.5 %delta_chunks.1 = (f32[4,512,256]{2,1,0:T(8,128)}, f32[4,128,256]{2,1,0:T(8,128)}) custom-call(f32[4,512,128]{2,1,0:T(8,128)} %bitcast.108, f32[4,512,128]{2,1,0:T(8,128)} %bitcast.109, f32[4,512,128]{2,1,0:T(8,128)} %bitcast.107, f32[4,512,1]{2,1,0:T(8,128)} %copy.128.b_ref, f32[4,512,1]{2,1,0:T(8,128)} %reshape.157.cc_ref, f32[4,8,64]{2,1,0:T(8,128)} %copy-done.8), custom_call_target="tpu_custom_call" | custom-call | tf_op jit(solution)/shard_map/delta_chunks/pallas_call | solution.py:94
  434.5 6.4 %collective-permute-done.1 = f32[4,128,256]{2,1,0:T(8,128)S(1)} collective-permute-done((f32[4,128,256]{2,1,0:T(8,128)}, f32[4,128,256]{2,1,0:T(8,128)S(1)}, u32[]{:S(2)}, u32[]{:S(2)}) %collective-permute-start.1) | collective-permute-done | bytes 524320 | tf_op jit(solution)/shard_map/ppermute | solution.py:114
  446.6 9.2 %collective-permute-done.2 = f32[4,128,256]{2,1,0:T(8,128)} collective-permute-done((f32[4,128,256]{2,1,0:T(8,128)S(1)}, f32[4,128,256]{2,1,0:T(8,128)}, u32[]{:S(2)}, u32[]{:S(2)}) %collective-permute-start.2) | collective-permute-done | bytes 524320 | tf_op jit(solution)/shard_map/ppermute | solution.py:114
  457.5 7.4 %collective-permute-start.3 = (f32[4,128,256]{2,1,0:T(8,128)S(1)}, f32[4,128,256]{2,1,0:T(8,128)S(1)}, u32[]{:S(2)}, u32[]{:S(2)}) collective-permute-start(f32[4,128,256]{2,1,0:T(8,128)S(1)} %fusion.34), channel_id=1, source_target_pairs={{0,16},{4,20},{8,24},{12,28},{16,32},{20,36},{24,40},{28,44},{32,4... | collective-permute-start | bytes 1572872 | tf_op jit(solution)/shard_map/ppermute | solution.py:114
  464.9 10.5 %collective-permute-done.3 = f32[4,128,256]{2,1,0:T(8,128)S(1)} collective-permute-done((f32[4,128,256]{2,1,0:T(8,128)S(1)}, f32[4,128,256]{2,1,0:T(8,128)S(1)}, u32[]{:S(2)}, u32[]{:S(2)}) %collective-permute-start.3) | collective-permute-done | bytes 524320 | tf_op jit(solution)/shard_map/ppermute | solution.py:114
  481.2 8.1 %collective-permute-done.4 = f32[4,128,256]{2,1,0:T(8,128)} collective-permute-done((f32[4,128,256]{2,1,0:T(8,128)S(1)}, f32[4,128,256]{2,1,0:T(8,128)}, u32[]{:S(2)}, u32[]{:S(2)}) %collective-permute-start.4) | collective-permute-done | bytes 524320 | tf_op jit(solution)/shard_map/ppermute | solution.py:114
  491.0 4.5 collective-permute-start.5
  499.7 9.2 %collective-permute-start.6 = (f32[4,128,128]{2,1,0:T(8,128)}, f32[4,128,128]{2,1,0:T(8,128)S(1)}, u32[]{:S(2)}, u32[]{:S(2)}) collective-permute-start(f32[4,128,128]{2,1,0:T(8,128)} %fusion.36), channel_id=1, source_target_pairs={{0,4},{4,8},{8,12},{12,16},{16,20},{20,24},{24,28},{28,32},{32,36}... | collective-permute-start | bytes 786440 | tf_op jit(solution)/shard_map/ppermute | solution.py:114
  508.9 4.3 convolution_convert_fusion.3
  522.4 30.8 %reduce-scatter.2.cloned.1.call-done = bf16[128,2048]{1,0:T(8,128)(2,1)} async-done(((bf16[512,2048]{1,0:T(8,128)(2,1)}), bf16[128,2048]{1,0:T(8,128)(2,1)}) %reduce-scatter.2.cloned.1.call-update) | async-done | bytes 524304 | tf_op jit(solution)/shard_map/reduce_scatter | solution.py:284
  (120 shorter events, 74.3 us)
Async XLA Ops:
  7.2 512.6 %copy-start = (bf16[512,2048]{1,0:T(8,128)(2,1)S(1)}, bf16[512,2048]{1,0:T(8,128)(2,1)}, u32[]{:S(2)}) copy-start(bf16[512,2048]{1,0:T(8,128)(2,1)} %param.41) | copy-start | bytes 6291460
  12.1 2.6 copy-start.12
  39.9 90.4 %copy-start.19 = (bf16[2,2048,512]{2,1,0:T(8,128)(2,1)S(1)}, bf16[2,2048,512]{2,1,0:T(8,128)(2,1)}, u32[]{:S(2)}) copy-start(bf16[2,2048,512]{2,1,0:T(8,128)(2,1)} %param.26) | copy-start | bytes 12582916
  127.7 2.6 copy-start.5
  171.3 81.8 %all-to-all-start.1 = ((bf16[128,2,6,2048]{3,1,2,0:T(2,128)(2,1)}), bf16[128,2,6,2048]{3,1,2,0:T(2,128)(2,1)}, u32[]{:S(2)}, u32[]{:S(2)}) async-start(bf16[128,2,6,2048]{3,1,2,0:T(2,128)(2,1)} %copy.123), calls=%async_computation.1 | async-start | bytes 12582912 | tf_op jit(solution)/shard_map/all_to_all | solution.py:211
  176.1 134.5 %all-gather.2.cloned.1.call-start = ((), (), s32[]{:S(2)}) async-start(), calls=%async_computation.3 | async-start | bytes 2621440 | tf_op jit(solution)/shard_map/all_gather | solution.py:230
  274.5 6.4 %copy-start.13 = (f32[2048]{0:T(1024)S(1)}, f32[2048]{0:T(1024)}, u32[]{:S(2)}) copy-start(f32[2048]{0:T(1024)} %param.28) | copy-start | bytes 24580
  282.0 271.3 %reduce-scatter.2.cloned.1.call-start = ((), (), s32[]{:S(2)}) async-start(), calls=%async_computation.4 | async-start | bytes 2621440 | tf_op jit(solution)/shard_map/reduce_scatter | solution.py:284
  310.6 3.7 copy-start.4
  310.6 3.7 copy-start.20
  316.3 6.0 %copy-start.10 = (bf16[2048,4]{0,1:T(4,128)(2,1)S(1)}, bf16[2048,4]{0,1:T(4,128)(2,1)}, u32[]{:S(2)}) copy-start(bf16[2048,4]{0,1:T(4,128)(2,1)} %param.34) | copy-start | bytes 49156
  316.3 6.0 %copy-start.17 = (f32[4]{0:T(128)S(1)}, f32[4]{0:T(128)}, u32[]{:S(2)}) copy-start(f32[4]{0:T(128)} %param.39) | copy-start | bytes 52
  317.9 5.0 copy-start.11
  318.1 9.9 %collective-permute-start = (bf16[3,1024]{0,1:T(8,128)(2,1)S(1)}, bf16[3,1024]{0,1:T(8,128)(2,1)S(1)}, u32[]{:S(2)}, u32[]{:S(2)}) collective-permute-start(bf16[3,1024]{0,1:T(8,128)(2,1)S(1)} %slice.88), channel_id=1, source_target_pairs={{0,4},{4,8},{8,12},{12,16},{16,20},{20,24},{24,28},{28,32},{32,36}... | collective-permute-start | bytes 18440 | tf_op jit(solution)/shard_map/ppermute | solution.py:109
  324.6 10.0 %copy-start.8 = (f32[4,8,64]{2,1,0:T(8,128)}, f32[4,8,64]{2,1,0:T(8,128)S(1)}, u32[]{:S(2)}) copy-start(f32[4,8,64]{2,1,0:T(8,128)S(1)} %reduce_window_sum.25.cr_ref) | copy-start | bytes 24580
  336.2 4.2 slice-start
  432.6 8.3 %collective-permute-start.1 = (f32[4,128,256]{2,1,0:T(8,128)}, f32[4,128,256]{2,1,0:T(8,128)S(1)}, u32[]{:S(2)}, u32[]{:S(2)}) collective-permute-start(f32[4,128,256]{2,1,0:T(8,128)} %get-tuple-element.5), channel_id=1, source_target_pairs={{0,4},{4,8},{8,12},{12,16},{16,20},{20,24},{24,28},{28,32},{32,36}... | collective-permute-start | bytes 1572872 | tf_op jit(solution)/shard_map/ppermute | solution.py:114
  442.7 13.2 %collective-permute-start.2 = (f32[4,128,256]{2,1,0:T(8,128)S(1)}, f32[4,128,256]{2,1,0:T(8,128)}, u32[]{:S(2)}, u32[]{:S(2)}) collective-permute-start(f32[4,128,256]{2,1,0:T(8,128)S(1)} %fusion.35), channel_id=1, source_target_pairs={{0,8},{4,12},{8,16},{12,20},{16,24},{20,28},{24,32},{28,36},{32,40... | collective-permute-start | bytes 1572872 | tf_op jit(solution)/shard_map/ppermute | solution.py:114
  457.5 7.4 %copy-start.7 = (f32[4,128,256]{2,1,0:T(8,128)}, f32[4,128,256]{2,1,0:T(8,128)S(1)}, u32[]{:S(2)}) copy-start(f32[4,128,256]{2,1,0:T(8,128)S(1)} %fusion.34) | copy-start | bytes 1572868
  457.5 18.0 %collective-permute-start.3 = (f32[4,128,256]{2,1,0:T(8,128)S(1)}, f32[4,128,256]{2,1,0:T(8,128)S(1)}, u32[]{:S(2)}, u32[]{:S(2)}) collective-permute-start(f32[4,128,256]{2,1,0:T(8,128)S(1)} %fusion.34), channel_id=1, source_target_pairs={{0,16},{4,20},{8,24},{12,28},{16,32},{20,36},{24,40},{28,44},{32,4... | collective-permute-start | bytes 1572872 | tf_op jit(solution)/shard_map/ppermute | solution.py:114
  477.2 12.1 %collective-permute-start.4 = (f32[4,128,256]{2,1,0:T(8,128)S(1)}, f32[4,128,256]{2,1,0:T(8,128)}, u32[]{:S(2)}, u32[]{:S(2)}) collective-permute-start(f32[4,128,256]{2,1,0:T(8,128)S(1)} %fusion.33), channel_id=1, source_target_pairs={{0,32},{4,36},{8,40},{12,44},{16,48},{20,52},{24,56},{28,60},{32,6... | collective-permute-start | bytes 1572872 | tf_op jit(solution)/shard_map/ppermute | solution.py:114
  491.0 7.6 %collective-permute-start.5 = (f32[4,128,128]{2,1,0:T(8,128)S(1)}, f32[4,128,128]{2,1,0:T(8,128)S(1)}, u32[]{:S(2)}, u32[]{:S(2)}) collective-permute-start(f32[4,128,128]{2,1,0:T(8,128)S(1)} %slice.102), channel_id=1, source_target_pairs={{0,64},{4,68},{8,72},{12,76},{16,80},{20,84},{24,88},{28,92},{32,9... | collective-permute-start | bytes 786440 | tf_op jit(solution)/shard_map/ppermute | solution.py:114
  499.7 14.8 %collective-permute-start.6 = (f32[4,128,128]{2,1,0:T(8,128)}, f32[4,128,128]{2,1,0:T(8,128)S(1)}, u32[]{:S(2)}, u32[]{:S(2)}) collective-permute-start(f32[4,128,128]{2,1,0:T(8,128)} %fusion.36), channel_id=1, source_target_pairs={{0,4},{4,8},{8,12},{12,16},{16,20},{20,24},{24,28},{28,32},{32,36}... | collective-permute-start | bytes 786440 | tf_op jit(solution)/shard_map/ppermute | solution.py:114
  513.2 4.2 copy-start.18
  (10 other events, 16.5 us)
Sparse Core Ops, SparseCore 0:
  282.1 28.4 all-gather.1
  522.6 30.6 reduce-scatter.1

commit v4 on v3

--- a/solution.py
+++ b/solution.py
@@ -198,10 +198,10 @@
     place_rows = places.reshape(tok_rows, top_count)
     slot_ids = jnp.arange(slot_count, dtype=jnp.int32)
     take = jnp.sum((place_rows[None, :, :] == slot_ids[:, None, None]).astype(jnp.float32), axis=2)
-    outgoing = jnp.dot(
-        take.astype(jnp.bfloat16), normed, preferred_element_type=jnp.float32
+    take = take.astype(jnp.bfloat16).reshape(sources, local_experts, capacity, tok_rows)
+    outgoing = jnp.einsum(
+        "nest,td->nesd", take, normed, preferred_element_type=jnp.float32
     ).astype(jnp.bfloat16)
-    outgoing = outgoing.reshape(sources, local_experts, capacity, model_width)
     received = lax.all_to_all(outgoing, ("ctx", "head"), split_axis=0, concat_axis=0, tiled=True)
     gate_part = jnp.einsum(
         "nesd,edh->nesh", received, expert_gate, preferred_element_type=jnp.float32
@@ -220,8 +220,9 @@
     mix = jnp.sum(
         jnp.where(place_rows[:, :, None] == slot_ids[None, None, :], weights[:, :, None], 0.0), axis=1
     )
-    moe_out = jnp.dot(
-        mix, returned.reshape(slot_count, model_width).astype(jnp.float32), precision=HI
+    mix = mix.reshape(tok_rows, sources, local_experts, capacity)
+    moe_out = jnp.einsum(
+        "tnes,nesd->td", mix, returned.astype(jnp.float32), precision=HI
     ).astype(jnp.bfloat16)
     mixer_in = rms_rows(
         stream.astype(jnp.float32) + moe_out.astype(jnp.float32), mixer_gain

time: 567 us -> 543 us (0.958)
  local copies, waits for them, and re-layouts: 78.5 us -> 52.1 us
  waiting for transfers between devices: 170 us -> 157 us
  other arithmetic: 18.5 us -> 29.1 us
    reshape x3 -> x1, local copies, waits for them, and re-layouts: 31.6 us -> 1.15 us  [on_device(): mix = mix.reshape(tok_rows, sources, local_experts, capacity)]
    all_to_all x1, waiting for transfers between devices: 73.5 us -> 60.3 us  [on_device(): lax.all_to_all(jnp.einsum('nesh,ehd->nesd', hidden, expert_down, preferre...]
    convert_element_type x0 -> x2, local copies, waits for them, and re-layouts: none -> 13.1 us  [the longest x1 13 us: on_device(): outgoing = jnp.einsum('nest,td->nesd', take, normed, preferred_element_ty...]
    reduce_sum x1, other arithmetic: 1.39 us -> 12.1 us  [on_device(): jnp.sum(jnp.where(place_rows[:, :, None] == slot_ids[None, None, :], weig...]
    all_to_all x1 -> x0, local copies, waits for them, and re-layouts: 10.4 us -> none  [on_device(): lax.all_to_all(jnp.einsum('nesh,ehd->nesd', hidden, expert_down, preferre...]
  transfers between devices with their start and end apart: 10 -> 10, of which waited for: 8 -> 8; matrix products, arithmetic and copies ran while one was open for 3% -> 5% of each run, Pallas kernels for 0% -> 0%
where the time goes in v4:
time: 543 us; the launch traced here: 537 us
  waiting for transfers between devices  157 us (29%)
  blocking collectives  87.4 us (16%)
  Pallas kernels  86.5 us (16%)
  matrix products  69.3 us (13%)
  local copies, waits for them, and re-layouts  52.1 us (10%)
  starting transfers between devices  40.3 us (7%)
  other arithmetic  29.1 us (5%)
  between operations  15.1 us (3%)
    all_to_all x1, blocking collectives, on_device(): lax.all_to_all(outgoing, ('ctx', 'head'), split_axis=0, concat_axis=0, ti...  87.4 us
    pallas_call x1, Pallas kernels, local_delta(): pl.pallas_call(delta_kernel, grid=(1,), in_specs=[whole(heads, length, kw...  86.5 us
    all_to_all x1, waiting for transfers between devices, on_device(): lax.all_to_all(jnp.einsum('nesh,ehd->nesd', hidden, expert_down, preferre...  60.3 us
    ppermute x6, waiting for transfers between devices, shifted(): lax.ppermute(value, axis, [(source, source + steps) for source in range(c...  37.7 us
    ppermute x6, starting transfers between devices, shifted(): lax.ppermute(value, axis, [(source, source + steps) for source in range(c...  31.3 us
    reduce_scatter x1, waiting for transfers between devices, on_device(): lax.psum_scatter(jnp.dot(gated_out, out_weight, preferred_element_type=jn...  30.7 us
    all_gather x1, waiting for transfers between devices, on_device(): piece_rows = lax.all_gather(mixer_in, 'head', axis=0, tiled=True)  28.4 us
    dot_general x1, matrix products, on_device(): jnp.einsum('nesh,ehd->nesd', hidden, expert_down, preferred_element_type=...  19.7 us
  transfers between devices with their start and end apart: 10, of which 8 were waited for; matrix products, arithmetic and copies ran while one was open for 5% of the time, Pallas kernels for 0%

profile of v4, /device:TPU:1, one launch (start us, length us, event | category | flops | bytes accessed | tf_op | source)
XLA Modules:
  0.0 536.9 jit_solution(7016240580669455272)
XLA Ops:
  17.4 13.0 %copy.130 = bf16[128,2,6,2048]{3,1,2,0:T(2,128)(2,1)S(1)} copy(bf16[128,2,6,2048]{3,0,2,1:T(8,128)(2,1)S(1)} %convolution_convert_fusion) | data formatting | bytes 12582912 | tf_op jit(solution)/shard_map/convert_element_type | solution.py:204
  30.4 87.4 %all_to_all.10 = bf16[128,2,6,2048]{3,1,2,0:T(2,128)(2,1)S(1)} all-to-all(bf16[128,2,6,2048]{3,1,2,0:T(2,128)(2,1)S(1)} %copy.130), channel_id=1, replica_groups=mesh['ctx'=32,'head'=4] {'ctx','head'}, dimensions={0} | all-to-all | bytes 12582912 | tf_op jit(solution)/shard_map/all_to_all | solution.py:205
  120.5 8.6 %fusion.2 = f32[2,128,6,512]{3,1,2,0:T(8,128)} fusion(bf16[128,2,6,2048]{3,1,2,0:T(2,128)(2,1)S(1)} %all_to_all.10, bf16[2,2048,512]{2,1,0:T(8,128)(2,1)S(1)} %copy-done.19), kind=kOutput, calls=%fused_computation.7 | convolution fusion | flops 3221225472 | bytes 13631488 | tf_op jit(solution)/shard_map/nesd,edh->nesh/dot_general | solution.py:209
  129.1 19.7 %convert_bitcast_fusion = bf16[128,2,6,2048]{3,0,2,1:T(8,128)(2,1)} fusion(bf16[2,512,2048]{2,1,0:T(8,128)(2,1)} %param.27, f32[2,128,6,512]{3,1,2,0:T(8,128)} %fusion.2, bf16[2,2048,512]{2,1,0:T(8,128)(2,1)} %param.25, bf16[128,2,6,2048]{3,1,2,0:T(2,128)(2,1)} %copy-done.4), kind=kOutput, calls=%fused_computation.6 | convolution fusion | flops 6450315264 | bytes 24117248 | tf_op jit(solution)/shard_map/nesh,ehd->nesd/dot_general | solution.py:212
  148.8 12.7 %copy.133 = bf16[128,2,6,2048]{3,1,2,0:T(2,128)(2,1)} copy(bf16[128,2,6,2048]{3,0,2,1:T(8,128)(2,1)} %convert_bitcast_fusion) | data formatting | bytes 12582912 | tf_op jit(solution)/shard_map/convert_element_type | solution.py:214
  161.5 4.9 all-to-all-start.1
  168.6 12.1 %select_reduce_fusion = f32[128,1536]{1,0:T(8,128)} fusion(f32[128,10]{0,1:T(8,128)S(1)} %exponential_divide_fusion, s32[128,10]{0,1:T(8,128)S(1)} %multiply_add_fusion), kind=kLoop, calls=%fused_computation.2 | loop fusion | flops 5701632 | bytes 796672 | tf_op jit(solution)/shard_map/reduce_sum | solution.py:220
  183.3 60.3 %all-to-all-done.1 = bf16[128,2,6,2048]{3,1,2,0:T(2,128)(2,1)} async-done(((bf16[128,2,6,2048]{3,1,2,0:T(2,128)(2,1)}), bf16[128,2,6,2048]{3,1,2,0:T(2,128)(2,1)}, u32[]{:S(2)}, u32[]{:S(2)}) %all-to-all-start.1) | async-done | bytes 6291488 | tf_op jit(solution)/shard_map/all_to_all | solution.py:211
  243.5 12.6 %multiply_reduce_fusion.1 = (f32[128]{0:T(128)S(1)}, bf16[128,2048]{1,0:T(8,128)(2,1)S(1)}) fusion(bf16[128,2048]{1,0:T(8,128)(2,1)S(1)} %copy-done.5, bf16[128,2,6,2048]{3,1,2,0:T(2,128)(2,1)} %all-to-all-done.1, f32[128,128,2,6]{0,3,2,1:T(8,128)} %reshape.139), kind=kOutput, calls=%fused_computation.83 | convolution fusion | flops 4833411072 | bytes 8126976 | tf_op jit(solution)/shard_map/tnes,nesd->td/dot_general | solution.py:224
  258.1 28.4 %all-gather.2.cloned.1.call-done = bf16[512,2048]{1,0:T(8,128)(2,1)} async-done(((bf16[128,2048]{1,0:T(8,128)(2,1)}), bf16[512,2048]{1,0:T(8,128)(2,1)}) %all-gather.2.cloned.1.call-update) | async-done | bytes 2097168 | tf_op jit(solution)/shard_map/all_gather | solution.py:231
  294.0 4.0 collective-permute-start
  303.7 6.5 %divide_multiply_fusion = f32[512,1024]{0,1:T(8,128)S(1)} fusion(f32[512,1024]{0,1:T(8,128)} %get-tuple-element.11, f32[3,1024]{0,1:T(8,128)S(1)} %convert_element_type.74, f32[1024]{0:T(1024)S(1)} %bitcast.124, f32[1024]{0:T(1024)S(1)} %bitcast.125, f32[1024]{0:T(1024)S(1)} %bitcast.126, f32[1024]{0:T(1024)S(1)} %bitcast.123), kind=kLoop, calls=%fused_computation.38 | loop fusion | flops 7340032 | bytes 4222976 | tf_op jit(solution)/shard_map/jit(silu)/mul | solution.py:254
  321.8 86.5 %delta_chunks.1 = (f32[4,512,256]{2,1,0:T(8,128)}, f32[4,128,256]{2,1,0:T(8,128)}) custom-call(f32[4,512,128]{2,1,0:T(8,128)} %bitcast.118, f32[4,512,128]{2,1,0:T(8,128)} %bitcast.119, f32[4,512,128]{2,1,0:T(8,128)} %bitcast.117, f32[4,512,1]{2,1,0:T(8,128)} %copy.139.b_ref, f32[4,512,1]{2,1,0:T(8,128)} %reshape.158.cc_ref, f32[4,8,64]{2,1,0:T(8,128)} %copy-done.8), custom_call_target="tpu_custom_call" | custom-call | tf_op jit(solution)/shard_map/delta_chunks/pallas_call | solution.py:94
  410.2 6.4 %collective-permute-done.1 = f32[4,128,256]{2,1,0:T(8,128)S(1)} collective-permute-done((f32[4,128,256]{2,1,0:T(8,128)}, f32[4,128,256]{2,1,0:T(8,128)S(1)}, u32[]{:S(2)}, u32[]{:S(2)}) %collective-permute-start.1) | collective-permute-done | bytes 524320 | tf_op jit(solution)/shard_map/ppermute | solution.py:114
  418.4 4.0 collective-permute-start.2
  422.4 9.2 %collective-permute-done.2 = f32[4,128,256]{2,1,0:T(8,128)} collective-permute-done((f32[4,128,256]{2,1,0:T(8,128)S(1)}, f32[4,128,256]{2,1,0:T(8,128)}, u32[]{:S(2)}, u32[]{:S(2)}) %collective-permute-start.2) | collective-permute-done | bytes 524320 | tf_op jit(solution)/shard_map/ppermute | solution.py:114
  433.2 7.8 %collective-permute-start.3 = (f32[4,128,256]{2,1,0:T(8,128)S(1)}, f32[4,128,256]{2,1,0:T(8,128)S(1)}, u32[]{:S(2)}, u32[]{:S(2)}) collective-permute-start(f32[4,128,256]{2,1,0:T(8,128)S(1)} %fusion.42), channel_id=1, source_target_pairs={{0,16},{4,20},{8,24},{12,28},{16,32},{20,36},{24,40},{28,44},{32,4... | collective-permute-start | bytes 1572872 | tf_op jit(solution)/shard_map/ppermute | solution.py:114
  441.0 10.7 %collective-permute-done.3 = f32[4,128,256]{2,1,0:T(8,128)S(1)} collective-permute-done((f32[4,128,256]{2,1,0:T(8,128)S(1)}, f32[4,128,256]{2,1,0:T(8,128)S(1)}, u32[]{:S(2)}, u32[]{:S(2)}) %collective-permute-start.3) | collective-permute-done | bytes 524320 | tf_op jit(solution)/shard_map/ppermute | solution.py:114
  453.5 4.0 collective-permute-start.4
  457.5 8.4 %collective-permute-done.4 = f32[4,128,256]{2,1,0:T(8,128)} collective-permute-done((f32[4,128,256]{2,1,0:T(8,128)S(1)}, f32[4,128,256]{2,1,0:T(8,128)}, u32[]{:S(2)}, u32[]{:S(2)}) %collective-permute-start.4) | collective-permute-done | bytes 524320 | tf_op jit(solution)/shard_map/ppermute | solution.py:114
  467.6 4.6 collective-permute-start.5
  476.3 9.1 %collective-permute-start.6 = (f32[4,128,128]{2,1,0:T(8,128)}, f32[4,128,128]{2,1,0:T(8,128)S(1)}, u32[]{:S(2)}, u32[]{:S(2)}) collective-permute-start(f32[4,128,128]{2,1,0:T(8,128)} %fusion.44), channel_id=1, source_target_pairs={{0,4},{4,8},{8,12},{12,16},{16,20},{20,24},{24,28},{28,32},{32,36}... | collective-permute-start | bytes 786440 | tf_op jit(solution)/shard_map/ppermute | solution.py:114
  485.4 4.3 convolution_convert_fusion.2
  499.0 30.7 %reduce-scatter.2.cloned.1.call-done = bf16[128,2048]{1,0:T(8,128)(2,1)} async-done(((bf16[512,2048]{1,0:T(8,128)(2,1)}), bf16[128,2048]{1,0:T(8,128)(2,1)}) %reduce-scatter.2.cloned.1.call-update) | async-done | bytes 524304 | tf_op jit(solution)/shard_map/reduce_scatter | solution.py:285
  (120 shorter events, 66.0 us)
Async XLA Ops:
  7.2 489.2 %copy-start = (bf16[512,2048]{1,0:T(8,128)(2,1)S(1)}, bf16[512,2048]{1,0:T(8,128)(2,1)}, u32[]{:S(2)}) copy-start(bf16[512,2048]{1,0:T(8,128)(2,1)} %param.41) | copy-start | bytes 6291460
  30.4 90.1 %copy-start.19 = (bf16[2,2048,512]{2,1,0:T(8,128)(2,1)S(1)}, bf16[2,2048,512]{2,1,0:T(8,128)(2,1)}, u32[]{:S(2)}) copy-start(bf16[2,2048,512]{2,1,0:T(8,128)(2,1)} %param.26) | copy-start | bytes 12582916
  117.8 2.7 copy-start.4
  161.5 5.0 copy-start.14
  161.5 82.0 %all-to-all-start.1 = ((bf16[128,2,6,2048]{3,1,2,0:T(2,128)(2,1)}), bf16[128,2,6,2048]{3,1,2,0:T(2,128)(2,1)}, u32[]{:S(2)}, u32[]{:S(2)}) async-start(bf16[128,2,6,2048]{3,1,2,0:T(2,128)(2,1)} %copy.133), calls=%async_computation.1 | async-start | bytes 12582912 | tf_op jit(solution)/shard_map/all_to_all | solution.py:211
  166.5 120.0 %all-gather.2.cloned.1.call-start = ((), (), s32[]{:S(2)}) async-start(), calls=%async_computation.3 | async-start | bytes 2621440 | tf_op jit(solution)/shard_map/all_gather | solution.py:231
  183.2 73.6 %copy-start.12 = (f32[2048]{0:T(1024)S(1)}, f32[2048]{0:T(1024)}, u32[]{:S(2)}) copy-start(f32[2048]{0:T(1024)} %param.28) | copy-start | bytes 24580
  257.9 271.7 %reduce-scatter.2.cloned.1.call-start = ((), (), s32[]{:S(2)}) async-start(), calls=%async_computation.4 | async-start | bytes 2621440 | tf_op jit(solution)/shard_map/reduce_scatter | solution.py:285
  286.5 3.7 copy-start.3
  286.5 3.7 copy-start.20
  292.2 5.8 %copy-start.10 = (bf16[2048,4]{0,1:T(4,128)(2,1)S(1)}, bf16[2048,4]{0,1:T(4,128)(2,1)}, u32[]{:S(2)}) copy-start(bf16[2048,4]{0,1:T(4,128)(2,1)} %param.34) | copy-start | bytes 49156
  292.2 5.8 %copy-start.17 = (f32[4]{0:T(128)S(1)}, f32[4]{0:T(128)}, u32[]{:S(2)}) copy-start(f32[4]{0:T(128)} %param.39) | copy-start | bytes 52
  293.9 4.8 copy-start.11
  294.0 9.7 %collective-permute-start = (bf16[3,1024]{0,1:T(8,128)(2,1)S(1)}, bf16[3,1024]{0,1:T(8,128)(2,1)S(1)}, u32[]{:S(2)}, u32[]{:S(2)}) collective-permute-start(bf16[3,1024]{0,1:T(8,128)(2,1)S(1)} %slice.88), channel_id=1, source_target_pairs={{0,4},{4,8},{8,12},{12,16},{16,20},{20,24},{24,28},{28,32},{32,36}... | collective-permute-start | bytes 18440 | tf_op jit(solution)/shard_map/ppermute | solution.py:109
  300.3 10.0 %copy-start.8 = (f32[4,8,64]{2,1,0:T(8,128)}, f32[4,8,64]{2,1,0:T(8,128)S(1)}, u32[]{:S(2)}) copy-start(f32[4,8,64]{2,1,0:T(8,128)S(1)} %reduce_window_sum.25.cr_ref) | copy-start | bytes 24580
  311.9 4.2 slice-start
  408.3 8.3 %collective-permute-start.1 = (f32[4,128,256]{2,1,0:T(8,128)}, f32[4,128,256]{2,1,0:T(8,128)S(1)}, u32[]{:S(2)}, u32[]{:S(2)}) collective-permute-start(f32[4,128,256]{2,1,0:T(8,128)} %get-tuple-element.5), channel_id=1, source_target_pairs={{0,4},{4,8},{8,12},{12,16},{16,20},{20,24},{24,28},{28,32},{32,36}... | collective-permute-start | bytes 1572872 | tf_op jit(solution)/shard_map/ppermute | solution.py:114
  418.4 13.2 %collective-permute-start.2 = (f32[4,128,256]{2,1,0:T(8,128)S(1)}, f32[4,128,256]{2,1,0:T(8,128)}, u32[]{:S(2)}, u32[]{:S(2)}) collective-permute-start(f32[4,128,256]{2,1,0:T(8,128)S(1)} %fusion.43), channel_id=1, source_target_pairs={{0,8},{4,12},{8,16},{12,20},{16,24},{20,28},{24,32},{28,36},{32,40... | collective-permute-start | bytes 1572872 | tf_op jit(solution)/shard_map/ppermute | solution.py:114
  433.2 7.8 %copy-start.6 = (f32[4,128,256]{2,1,0:T(8,128)}, f32[4,128,256]{2,1,0:T(8,128)S(1)}, u32[]{:S(2)}) copy-start(f32[4,128,256]{2,1,0:T(8,128)S(1)} %fusion.42) | copy-start | bytes 1572868
  433.2 18.5 %collective-permute-start.3 = (f32[4,128,256]{2,1,0:T(8,128)S(1)}, f32[4,128,256]{2,1,0:T(8,128)S(1)}, u32[]{:S(2)}, u32[]{:S(2)}) collective-permute-start(f32[4,128,256]{2,1,0:T(8,128)S(1)} %fusion.42), channel_id=1, source_target_pairs={{0,16},{4,20},{8,24},{12,28},{16,32},{20,36},{24,40},{28,44},{32,4... | collective-permute-start | bytes 1572872 | tf_op jit(solution)/shard_map/ppermute | solution.py:114
  453.5 12.3 %collective-permute-start.4 = (f32[4,128,256]{2,1,0:T(8,128)S(1)}, f32[4,128,256]{2,1,0:T(8,128)}, u32[]{:S(2)}, u32[]{:S(2)}) collective-permute-start(f32[4,128,256]{2,1,0:T(8,128)S(1)} %fusion.41), channel_id=1, source_target_pairs={{0,32},{4,36},{8,40},{12,44},{16,48},{20,52},{24,56},{28,60},{32,6... | collective-permute-start | bytes 1572872 | tf_op jit(solution)/shard_map/ppermute | solution.py:114
  467.6 7.6 %collective-permute-start.5 = (f32[4,128,128]{2,1,0:T(8,128)S(1)}, f32[4,128,128]{2,1,0:T(8,128)S(1)}, u32[]{:S(2)}, u32[]{:S(2)}) collective-permute-start(f32[4,128,128]{2,1,0:T(8,128)S(1)} %slice.102), channel_id=1, source_target_pairs={{0,64},{4,68},{8,72},{12,76},{16,80},{20,84},{24,88},{28,92},{32,9... | collective-permute-start | bytes 786440 | tf_op jit(solution)/shard_map/ppermute | solution.py:114
  476.3 14.7 %collective-permute-start.6 = (f32[4,128,128]{2,1,0:T(8,128)}, f32[4,128,128]{2,1,0:T(8,128)S(1)}, u32[]{:S(2)}, u32[]{:S(2)}) collective-permute-start(f32[4,128,128]{2,1,0:T(8,128)} %fusion.44), channel_id=1, source_target_pairs={{0,4},{4,8},{8,12},{12,16},{16,20},{20,24},{24,28},{28,32},{32,36}... | collective-permute-start | bytes 786440 | tf_op jit(solution)/shard_map/ppermute | solution.py:114
  489.7 4.2 copy-start.18
  (10 other events, 15.8 us)
Sparse Core Ops, SparseCore 0:
  258.0 28.4 all-gather.1
  499.1 30.4 reduce-scatter.1

commit v5 on v4

--- a/solution.py
+++ b/solution.py
@@ -9,21 +9,22 @@
 
 DK = 128
 HI = lax.Precision.HIGHEST
+KERNEL_PRECISION = lax.Precision.HIGH
 CHUNK = 64
 epsilon = 1e-06
 
 
 def _mm(a, b):
-    return jnp.dot(a, b, precision=HI, preferred_element_type=jnp.float32)
+    return jnp.dot(a, b, precision=KERNEL_PRECISION, preferred_element_type=jnp.float32)
 
 
 def _mm_nt(a, b):
-    return lax.dot_general(a, b, (((1,), (1,)), ((), ())), precision=HI,
+    return lax.dot_general(a, b, (((1,), (1,)), ((), ())), precision=KERNEL_PRECISION,
                            preferred_element_type=jnp.float32)
 
 
 def _mm_tn(a, b):
-    return lax.dot_general(a, b, (((0,), (0,)), ((), ())), precision=HI,
+    return lax.dot_general(a, b, (((0,), (0,)), ((), ())), precision=KERNEL_PRECISION,
                            preferred_element_type=jnp.float32)
 
 

time: 543 us -> 525 us (0.967)
  Pallas kernels: 86.5 us -> 68.3 us
  waiting for transfers between devices: 157 us -> 167 us
  other arithmetic: 29.1 us -> 19.4 us
    pallas_call x1, Pallas kernels: 86.5 us -> 68.3 us  [local_delta(): pl.pallas_call(delta_kernel, grid=(1,), in_specs=[whole(heads, length, kw...]
    all_to_all x1, waiting for transfers between devices: 60.3 us -> 70 us  [on_device(): lax.all_to_all(jnp.einsum('nesh,ehd->nesd', hidden, expert_down, preferre...]
    reduce_sum x1, other arithmetic: 12.1 us -> 2.34 us  [on_device(): jnp.sum(jnp.where(place_rows[:, :, None] == slot_ids[None, None, :], weig...]
  transfers between devices with their start and end apart: 10 -> 10, of which waited for: 8 -> 8; matrix products, arithmetic and copies ran while one was open for 5% -> 4% of each run, Pallas kernels for 0% -> 0%
where the time goes in v5:
time: 525 us; the launch traced here: 519 us
  waiting for transfers between devices  167 us (32%)
  blocking collectives  87.7 us (17%)
  matrix products  69.1 us (13%)
  Pallas kernels  68.3 us (13%)
  local copies, waits for them, and re-layouts  52.1 us (10%)
  starting transfers between devices  40.1 us (8%)
  other arithmetic  19.4 us (4%)
  between operations  14.8 us (3%)
    all_to_all x1, blocking collectives, on_device(): lax.all_to_all(outgoing, ('ctx', 'head'), split_axis=0, concat_axis=0, ti...  87.7 us
    all_to_all x1, waiting for transfers between devices, on_device(): lax.all_to_all(jnp.einsum('nesh,ehd->nesd', hidden, expert_down, preferre...  70 us
    pallas_call x1, Pallas kernels, local_delta(): pl.pallas_call(delta_kernel, grid=(1,), in_specs=[whole(heads, length, kw...  68.3 us
    ppermute x6, waiting for transfers between devices, shifted(): lax.ppermute(value, axis, [(source, source + steps) for source in range(c...  38.3 us
    ppermute x6, starting transfers between devices, shifted(): lax.ppermute(value, axis, [(source, source + steps) for source in range(c...  30.9 us
    reduce_scatter x1, waiting for transfers between devices, on_device(): lax.psum_scatter(jnp.dot(gated_out, out_weight, preferred_element_type=jn...  30.8 us
    all_gather x1, waiting for transfers between devices, on_device(): piece_rows = lax.all_gather(mixer_in, 'head', axis=0, tiled=True)  28 us
    dot_general x1, matrix products, on_device(): jnp.einsum('nesh,ehd->nesd', hidden, expert_down, preferred_element_type=...  19.6 us
  transfers between devices with their start and end apart: 10, of which 8 were waited for; matrix products, arithmetic and copies ran while one was open for 4% of the time, Pallas kernels for 0%

profile of v5, /device:TPU:1, one launch (start us, length us, event | category | flops | bytes accessed | tf_op | source)
XLA Modules:
  0.0 518.7 jit_solution(9993062843280964095)
XLA Ops:
  17.4 13.0 %copy.130 = bf16[128,2,6,2048]{3,1,2,0:T(2,128)(2,1)S(1)} copy(bf16[128,2,6,2048]{3,0,2,1:T(8,128)(2,1)S(1)} %convolution_convert_fusion) | data formatting | bytes 12582912 | tf_op jit(solution)/shard_map/convert_element_type | solution.py:205
  30.4 87.7 %all_to_all.10 = bf16[128,2,6,2048]{3,1,2,0:T(2,128)(2,1)S(1)} all-to-all(bf16[128,2,6,2048]{3,1,2,0:T(2,128)(2,1)S(1)} %copy.130), channel_id=1, replica_groups=mesh['ctx'=32,'head'=4] {'ctx','head'}, dimensions={0} | all-to-all | bytes 12582912 | tf_op jit(solution)/shard_map/all_to_all | solution.py:206
  120.8 8.6 %fusion.2 = f32[2,128,6,512]{3,1,2,0:T(8,128)} fusion(bf16[128,2,6,2048]{3,1,2,0:T(2,128)(2,1)S(1)} %all_to_all.10, bf16[2,2048,512]{2,1,0:T(8,128)(2,1)S(1)} %copy-done.19), kind=kOutput, calls=%fused_computation.7 | convolution fusion | flops 3221225472 | bytes 13631488 | tf_op jit(solution)/shard_map/nesd,edh->nesh/dot_general | solution.py:210
  129.4 19.6 %convert_bitcast_fusion = bf16[128,2,6,2048]{3,0,2,1:T(8,128)(2,1)} fusion(bf16[2,512,2048]{2,1,0:T(8,128)(2,1)} %param.27, f32[2,128,6,512]{3,1,2,0:T(8,128)} %fusion.2, bf16[2,2048,512]{2,1,0:T(8,128)(2,1)} %param.25, bf16[128,2,6,2048]{3,1,2,0:T(2,128)(2,1)} %copy-done.4), kind=kOutput, calls=%fused_computation.6 | convolution fusion | flops 6450315264 | bytes 24117248 | tf_op jit(solution)/shard_map/nesh,ehd->nesd/dot_general | solution.py:213
  149.0 12.7 %copy.133 = bf16[128,2,6,2048]{3,1,2,0:T(2,128)(2,1)} copy(bf16[128,2,6,2048]{3,0,2,1:T(8,128)(2,1)} %convert_bitcast_fusion) | data formatting | bytes 12582912 | tf_op jit(solution)/shard_map/convert_element_type | solution.py:215
  161.7 4.9 all-to-all-start.1
  173.7 70.0 %all-to-all-done.1 = bf16[128,2,6,2048]{3,1,2,0:T(2,128)(2,1)} async-done(((bf16[128,2,6,2048]{3,1,2,0:T(2,128)(2,1)}), bf16[128,2,6,2048]{3,1,2,0:T(2,128)(2,1)}, u32[]{:S(2)}, u32[]{:S(2)}) %all-to-all-start.1) | async-done | bytes 6291488 | tf_op jit(solution)/shard_map/all_to_all | solution.py:212
  243.7 12.6 %multiply_reduce_fusion.1 = (f32[128]{0:T(128)S(1)}, bf16[128,2048]{1,0:T(8,128)(2,1)S(1)}) fusion(bf16[128,2048]{1,0:T(8,128)(2,1)S(1)} %copy-done.5, bf16[128,2,6,2048]{3,1,2,0:T(2,128)(2,1)} %all-to-all-done.1, f32[128,128,2,6]{0,3,2,1:T(8,128)} %reshape.139), kind=kOutput, calls=%fused_computation.83 | convolution fusion | flops 4833411072 | bytes 8126976 | tf_op jit(solution)/shard_map/tnes,nesd->td/dot_general | solution.py:225
  258.6 28.0 %all-gather.2.cloned.1.call-done = bf16[512,2048]{1,0:T(8,128)(2,1)} async-done(((bf16[128,2048]{1,0:T(8,128)(2,1)}), bf16[512,2048]{1,0:T(8,128)(2,1)}) %all-gather.2.cloned.1.call-update) | async-done | bytes 2097168 | tf_op jit(solution)/shard_map/all_gather | solution.py:232
  286.7 3.7 convolution_convert_fusion.3
  294.2 3.7 collective-permute-start
  303.7 6.5 %divide_multiply_fusion = f32[512,1024]{0,1:T(8,128)S(1)} fusion(f32[512,1024]{0,1:T(8,128)} %get-tuple-element.11, f32[3,1024]{0,1:T(8,128)S(1)} %convert_element_type.74, f32[1024]{0:T(1024)S(1)} %bitcast.124, f32[1024]{0:T(1024)S(1)} %bitcast.125, f32[1024]{0:T(1024)S(1)} %bitcast.126, f32[1024]{0:T(1024)S(1)} %bitcast.123), kind=kLoop, calls=%fused_computation.38 | loop fusion | flops 7340032 | bytes 4222976 | tf_op jit(solution)/shard_map/jit(silu)/mul | solution.py:255
  321.7 68.3 %delta_chunks.1 = (f32[4,512,256]{2,1,0:T(8,128)}, f32[4,128,256]{2,1,0:T(8,128)}) custom-call(f32[4,512,128]{2,1,0:T(8,128)} %bitcast.118, f32[4,512,128]{2,1,0:T(8,128)} %bitcast.119, f32[4,512,128]{2,1,0:T(8,128)} %bitcast.117, f32[4,512,1]{2,1,0:T(8,128)} %copy.139.b_ref, f32[4,512,1]{2,1,0:T(8,128)} %reshape.158.cc_ref, f32[4,8,64]{2,1,0:T(8,128)} %copy-done.8), custom_call_target="tpu_custom_call" | custom-call | tf_op jit(solution)/shard_map/delta_chunks/pallas_call | solution.py:95
  392.0 6.4 %collective-permute-done.1 = f32[4,128,256]{2,1,0:T(8,128)S(1)} collective-permute-done((f32[4,128,256]{2,1,0:T(8,128)}, f32[4,128,256]{2,1,0:T(8,128)S(1)}, u32[]{:S(2)}, u32[]{:S(2)}) %collective-permute-start.1) | collective-permute-done | bytes 524320 | tf_op jit(solution)/shard_map/ppermute | solution.py:115
  400.2 4.0 collective-permute-start.2
  404.2 9.2 %collective-permute-done.2 = f32[4,128,256]{2,1,0:T(8,128)} collective-permute-done((f32[4,128,256]{2,1,0:T(8,128)S(1)}, f32[4,128,256]{2,1,0:T(8,128)}, u32[]{:S(2)}, u32[]{:S(2)}) %collective-permute-start.2) | collective-permute-done | bytes 524320 | tf_op jit(solution)/shard_map/ppermute | solution.py:115
  415.0 8.2 %collective-permute-start.3 = (f32[4,128,256]{2,1,0:T(8,128)S(1)}, f32[4,128,256]{2,1,0:T(8,128)S(1)}, u32[]{:S(2)}, u32[]{:S(2)}) collective-permute-start(f32[4,128,256]{2,1,0:T(8,128)S(1)} %fusion.42), channel_id=1, source_target_pairs={{0,16},{4,20},{8,24},{12,28},{16,32},{20,36},{24,40},{28,44},{32,4... | collective-permute-start | bytes 1572872 | tf_op jit(solution)/shard_map/ppermute | solution.py:115
  423.2 10.8 %collective-permute-done.3 = f32[4,128,256]{2,1,0:T(8,128)S(1)} collective-permute-done((f32[4,128,256]{2,1,0:T(8,128)S(1)}, f32[4,128,256]{2,1,0:T(8,128)S(1)}, u32[]{:S(2)}, u32[]{:S(2)}) %collective-permute-start.3) | collective-permute-done | bytes 524320 | tf_op jit(solution)/shard_map/ppermute | solution.py:115
  435.8 3.9 collective-permute-start.4
  439.7 8.6 %collective-permute-done.4 = f32[4,128,256]{2,1,0:T(8,128)} collective-permute-done((f32[4,128,256]{2,1,0:T(8,128)S(1)}, f32[4,128,256]{2,1,0:T(8,128)}, u32[]{:S(2)}, u32[]{:S(2)}) %collective-permute-start.4) | collective-permute-done | bytes 524320 | tf_op jit(solution)/shard_map/ppermute | solution.py:115
  450.0 4.0 collective-permute-start.5
  458.4 8.9 %collective-permute-start.6 = (f32[4,128,128]{2,1,0:T(8,128)}, f32[4,128,128]{2,1,0:T(8,128)S(1)}, u32[]{:S(2)}, u32[]{:S(2)}) collective-permute-start(f32[4,128,128]{2,1,0:T(8,128)} %fusion.44), channel_id=1, source_target_pairs={{0,4},{4,8},{8,12},{12,16},{16,20},{20,24},{24,28},{28,32},{32,36}... | collective-permute-start | bytes 786440 | tf_op jit(solution)/shard_map/ppermute | solution.py:115
  467.3 4.3 convolution_convert_fusion.2
  480.9 30.8 %reduce-scatter.2.cloned.1.call-done = bf16[128,2048]{1,0:T(8,128)(2,1)} async-done(((bf16[512,2048]{1,0:T(8,128)(2,1)}), bf16[128,2048]{1,0:T(8,128)(2,1)}) %reduce-scatter.2.cloned.1.call-update) | async-done | bytes 524304 | tf_op jit(solution)/shard_map/reduce_scatter | solution.py:286
  (120 shorter events, 65.4 us)
Async XLA Ops:
  7.2 471.1 %copy-start = (bf16[512,2048]{1,0:T(8,128)(2,1)S(1)}, bf16[512,2048]{1,0:T(8,128)(2,1)}, u32[]{:S(2)}) copy-start(bf16[512,2048]{1,0:T(8,128)(2,1)} %param.41) | copy-start | bytes 6291460
  30.4 90.4 %copy-start.19 = (bf16[2,2048,512]{2,1,0:T(8,128)(2,1)S(1)}, bf16[2,2048,512]{2,1,0:T(8,128)(2,1)}, u32[]{:S(2)}) copy-start(bf16[2,2048,512]{2,1,0:T(8,128)(2,1)} %param.26) | copy-start | bytes 12582916
  118.1 2.7 copy-start.4
  161.7 5.0 copy-start.14
  161.7 82.0 %all-to-all-start.1 = ((bf16[128,2,6,2048]{3,1,2,0:T(2,128)(2,1)}), bf16[128,2,6,2048]{3,1,2,0:T(2,128)(2,1)}, u32[]{:S(2)}, u32[]{:S(2)}) async-start(bf16[128,2,6,2048]{3,1,2,0:T(2,128)(2,1)} %copy.133), calls=%async_computation.1 | async-start | bytes 12582912 | tf_op jit(solution)/shard_map/all_to_all | solution.py:212
  166.6 120.0 %all-gather.2.cloned.1.call-start = ((), (), s32[]{:S(2)}) async-start(), calls=%async_computation.3 | async-start | bytes 2621440 | tf_op jit(solution)/shard_map/all_gather | solution.py:232
  173.7 83.4 %copy-start.12 = (f32[2048]{0:T(1024)S(1)}, f32[2048]{0:T(1024)}, u32[]{:S(2)}) copy-start(f32[2048]{0:T(1024)} %param.28) | copy-start | bytes 24580
  258.1 253.6 %reduce-scatter.2.cloned.1.call-start = ((), (), s32[]{:S(2)}) async-start(), calls=%async_computation.4 | async-start | bytes 2621440 | tf_op jit(solution)/shard_map/reduce_scatter | solution.py:286
  286.7 3.7 copy-start.3
  286.7 3.7 copy-start.20
  292.4 5.6 %copy-start.10 = (bf16[2048,4]{0,1:T(4,128)(2,1)S(1)}, bf16[2048,4]{0,1:T(4,128)(2,1)}, u32[]{:S(2)}) copy-start(bf16[2048,4]{0,1:T(4,128)(2,1)} %param.34) | copy-start | bytes 49156
  292.4 5.6 %copy-start.17 = (f32[4]{0:T(128)S(1)}, f32[4]{0:T(128)}, u32[]{:S(2)}) copy-start(f32[4]{0:T(128)} %param.39) | copy-start | bytes 52
  294.0 4.6 copy-start.11
  294.2 9.5 %collective-permute-start = (bf16[3,1024]{0,1:T(8,128)(2,1)S(1)}, bf16[3,1024]{0,1:T(8,128)(2,1)S(1)}, u32[]{:S(2)}, u32[]{:S(2)}) collective-permute-start(bf16[3,1024]{0,1:T(8,128)(2,1)S(1)} %slice.88), channel_id=1, source_target_pairs={{0,4},{4,8},{8,12},{12,16},{16,20},{20,24},{24,28},{28,32},{32,36}... | collective-permute-start | bytes 18440 | tf_op jit(solution)/shard_map/ppermute | solution.py:110
  300.3 10.0 %copy-start.8 = (f32[4,8,64]{2,1,0:T(8,128)}, f32[4,8,64]{2,1,0:T(8,128)S(1)}, u32[]{:S(2)}) copy-start(f32[4,8,64]{2,1,0:T(8,128)S(1)} %reduce_window_sum.25.cr_ref) | copy-start | bytes 24580
  311.9 4.2 slice-start
  390.0 8.4 %collective-permute-start.1 = (f32[4,128,256]{2,1,0:T(8,128)}, f32[4,128,256]{2,1,0:T(8,128)S(1)}, u32[]{:S(2)}, u32[]{:S(2)}) collective-permute-start(f32[4,128,256]{2,1,0:T(8,128)} %get-tuple-element.5), channel_id=1, source_target_pairs={{0,4},{4,8},{8,12},{12,16},{16,20},{20,24},{24,28},{28,32},{32,36}... | collective-permute-start | bytes 1572872 | tf_op jit(solution)/shard_map/ppermute | solution.py:115
  400.2 13.2 %collective-permute-start.2 = (f32[4,128,256]{2,1,0:T(8,128)S(1)}, f32[4,128,256]{2,1,0:T(8,128)}, u32[]{:S(2)}, u32[]{:S(2)}) collective-permute-start(f32[4,128,256]{2,1,0:T(8,128)S(1)} %fusion.43), channel_id=1, source_target_pairs={{0,8},{4,12},{8,16},{12,20},{16,24},{20,28},{24,32},{28,36},{32,40... | collective-permute-start | bytes 1572872 | tf_op jit(solution)/shard_map/ppermute | solution.py:115
  415.0 8.2 %copy-start.6 = (f32[4,128,256]{2,1,0:T(8,128)}, f32[4,128,256]{2,1,0:T(8,128)S(1)}, u32[]{:S(2)}) copy-start(f32[4,128,256]{2,1,0:T(8,128)S(1)} %fusion.42) | copy-start | bytes 1572868
  415.0 19.0 %collective-permute-start.3 = (f32[4,128,256]{2,1,0:T(8,128)S(1)}, f32[4,128,256]{2,1,0:T(8,128)S(1)}, u32[]{:S(2)}, u32[]{:S(2)}) collective-permute-start(f32[4,128,256]{2,1,0:T(8,128)S(1)} %fusion.42), channel_id=1, source_target_pairs={{0,16},{4,20},{8,24},{12,28},{16,32},{20,36},{24,40},{28,44},{32,4... | collective-permute-start | bytes 1572872 | tf_op jit(solution)/shard_map/ppermute | solution.py:115
  435.8 12.5 %collective-permute-start.4 = (f32[4,128,256]{2,1,0:T(8,128)S(1)}, f32[4,128,256]{2,1,0:T(8,128)}, u32[]{:S(2)}, u32[]{:S(2)}) collective-permute-start(f32[4,128,256]{2,1,0:T(8,128)S(1)} %fusion.41), channel_id=1, source_target_pairs={{0,32},{4,36},{8,40},{12,44},{16,48},{20,52},{24,56},{28,60},{32,6... | collective-permute-start | bytes 1572872 | tf_op jit(solution)/shard_map/ppermute | solution.py:115
  450.0 7.3 %collective-permute-start.5 = (f32[4,128,128]{2,1,0:T(8,128)S(1)}, f32[4,128,128]{2,1,0:T(8,128)S(1)}, u32[]{:S(2)}, u32[]{:S(2)}) collective-permute-start(f32[4,128,128]{2,1,0:T(8,128)S(1)} %slice.102), channel_id=1, source_target_pairs={{0,64},{4,68},{8,72},{12,76},{16,80},{20,84},{24,88},{28,92},{32,9... | collective-permute-start | bytes 786440 | tf_op jit(solution)/shard_map/ppermute | solution.py:115
  458.4 14.5 %collective-permute-start.6 = (f32[4,128,128]{2,1,0:T(8,128)}, f32[4,128,128]{2,1,0:T(8,128)S(1)}, u32[]{:S(2)}, u32[]{:S(2)}) collective-permute-start(f32[4,128,128]{2,1,0:T(8,128)} %fusion.44), channel_id=1, source_target_pairs={{0,4},{4,8},{8,12},{12,16},{16,20},{20,24},{24,28},{28,32},{32,36}... | collective-permute-start | bytes 786440 | tf_op jit(solution)/shard_map/ppermute | solution.py:115
  471.6 4.2 copy-start.18
  (10 other events, 17.4 us)
Sparse Core Ops, SparseCore 0:
  258.2 28.4 all-gather.1
  481.0 30.6 reduce-scatter.1

commit v6 on v5

--- a/solution.py
+++ b/solution.py
@@ -11,6 +11,7 @@
 HI = lax.Precision.HIGHEST
 KERNEL_PRECISION = lax.Precision.HIGH
 CHUNK = 64
+GROUP = 256
 epsilon = 1e-06
 
 
@@ -28,60 +29,76 @@
                            preferred_element_type=jnp.float32)
 
 
-def delta_kernel(q_ref, k_ref, v_ref, b_ref, cc_ref, cr_ref, out_ref, carry_ref):
+def delta_kernel(q_ref, k_ref, v_ref, b_ref, cc_ref, cg_ref, last_ref, out_ref, carry_ref,
+                 wv_s, wk_s, qd_s, kd_s, mix_s, change_s, starts_s):
     heads, length, kw = q_ref.shape
     vw = v_ref.shape[2]
     n_chunks = length // CHUNK
-    row = lax.broadcasted_iota(jnp.int32, (CHUNK, CHUNK), 0)
-    col = lax.broadcasted_iota(jnp.int32, (CHUNK, CHUNK), 1)
-    strict = row > col
-    inclusive = row >= col
-    eye_c = jnp.where(row == col, 1.0, 0.0).astype(jnp.float32)
+    n_groups = length // GROUP
+    per_group = GROUP // CHUNK
+    row = lax.broadcasted_iota(jnp.int32, (GROUP, GROUP), 0)
+    col = lax.broadcasted_iota(jnp.int32, (GROUP, GROUP), 1)
+    same = (row // CHUNK) == (col // CHUNK)
+    strict = (row > col) & same
+    inclusive = (row >= col) & same
+    eye_g = jnp.where(row == col, 1.0, 0.0).astype(jnp.float32)
     pairs = ((row // 2) == (col // 2)) & (row != col)
+    for h in range(heads):
+        for g in range(n_groups):
+            rows = pl.ds(g * GROUP, GROUP)
+            q = q_ref[h, rows, :]
+            k = k_ref[h, rows, :]
+            v = v_ref[h, rows, :]
+            beta = b_ref[h, rows, :]
+            cum_c = cc_ref[h, rows, :]
+            cum_r = cg_ref[h, pl.ds(g, 1), :]
+            spread = cum_c - cum_r
+            fall_s = jnp.where(strict, jnp.exp(jnp.where(strict, spread, 0.0)), 0.0)
+            fall_i = jnp.where(inclusive, jnp.exp(jnp.where(inclusive, spread, 0.0)), 0.0)
+            a = beta * fall_s * _mm_nt(k, k)
+            inv = eye_g - jnp.where(pairs, a, 0.0)
+            size = 2
+            while size < CHUNK:
+                band = ((row // (2 * size)) == (col // (2 * size))) & ((row // size) != (col // size))
+                inv = inv - _mm(_mm(inv, jnp.where(band, a, 0.0)), inv)
+                size *= 2
+            ec = jnp.exp(cum_c)
+            solved = _mm(inv, jnp.concatenate([beta * v, (beta * ec) * k], axis=1))
+            wv_s[h, rows, :] = solved[:, :vw]
+            wk_s[h, rows, :] = solved[:, vw:]
+            mix_s[h, rows, :] = fall_i * _mm_nt(q, k)
+            qd_s[h, rows, :] = ec * q
+            kd_s[h, rows, :] = jnp.exp(last_ref[h, rows, :] - cum_c) * k
+
     lane = lax.broadcasted_iota(jnp.int32, (CHUNK, vw + kw), 1)
     value_lanes = lane < vw
     krow = lax.broadcasted_iota(jnp.int32, (kw, vw + kw), 0)
     kcol = lax.broadcasted_iota(jnp.int32, (kw, vw + kw), 1)
     carry0 = jnp.where(kcol - vw == krow, 1.0, 0.0).astype(jnp.float32)
 
-    def one_head(h, c, carry):
+    def step(c, carries):
         rows = pl.ds(pl.multiple_of(c * CHUNK, CHUNK), CHUNK)
-        q = q_ref[h, rows, :]
-        k = k_ref[h, rows, :]
-        v = v_ref[h, rows, :]
-        beta = b_ref[h, rows, :]
-        cum_c = cc_ref[h, rows, :]
-        cum_r = cr_ref[h, pl.ds(c, 1), :]
-        spread = cum_c - cum_r
-        fall_s = jnp.where(strict, jnp.exp(jnp.where(strict, spread, 0.0)), 0.0)
-        fall_i = jnp.where(inclusive, jnp.exp(jnp.where(inclusive, spread, 0.0)), 0.0)
-        a = beta * fall_s * _mm_nt(k, k)
-        inv = eye_c - jnp.where(pairs, a, 0.0)
-        size = 2
-        while size < CHUNK:
-            band = ((row // (2 * size)) == (col // (2 * size))) & ((row // size) != (col // size))
-            e = jnp.where(band, a, 0.0)
-            inv = inv - _mm(_mm(inv, e), inv)
-            size *= 2
-        ec = jnp.exp(cum_c)
-        solved = _mm(inv, jnp.concatenate([beta * v, (beta * ec) * k], axis=1))
-        w_values = jnp.where(value_lanes, solved, 0.0)
-        w_keys = solved[:, vw:]
-        mixing = fall_i * _mm_nt(q, k)
-        q_dec = ec * q
-        last = cum_r[:, CHUNK - 1:CHUNK]
-        k_dec = jnp.exp(last - cum_c) * k
-        closing = jnp.exp(last)
-        change = w_values - _mm(w_keys, carry)
-        out_ref[h, rows, :] = _mm(q_dec, carry) + _mm(mixing, change)
-        return closing * carry + _mm_tn(k_dec, change)
-
-    def body(c, carries):
-        return tuple(one_head(h, c, carries[h]) for h in range(heads))
-
-    carries = lax.fori_loop(0, n_chunks, body, (carry0,) * heads)
+        new = []
+        for h in range(heads):
+            carry = carries[h]
+            starts_s[h, c] = carry
+            w_values = jnp.concatenate([wv_s[h, rows, :], jnp.zeros((CHUNK, kw), jnp.float32)], axis=1)
+            change = w_values - _mm(wk_s[h, rows, :], carry)
+            change_s[h, rows, :] = change
+            closing = jnp.exp(last_ref[h, pl.ds(c * CHUNK, 1), :])
+            new.append(closing * carry + _mm_tn(kd_s[h, rows, :], change))
+        return tuple(new)
+
+    carries = lax.fori_loop(0, n_chunks, step, (carry0,) * heads)
     for h in range(heads):
         carry_ref[h] = carries[h]
+        for g in range(n_groups):
+            rows = pl.ds(g * GROUP, GROUP)
+            mixed = _mm(mix_s[h, rows, :], change_s[h, rows, :])
+            for j in range(per_group):
+                c = g * per_group + j
+                sub = pl.ds(c * CHUNK, CHUNK)
+                out_ref[h, sub, :] = mixed[j * CHUNK:(j + 1) * CHUNK] + _mm(qd_s[h, sub, :], starts_s[h, c])
 
 
 def local_delta(queries, key_rows, values, strength, decays):
@@ -89,19 +106,27 @@
     vw = values.shape[2]
     n_chunks = length // CHUNK
     cum = jnp.cumsum(decays.reshape(heads, n_chunks, CHUNK), axis=-1)
-    cum_col = cum.reshape(heads, length, 1)
-    beta_col = strength.reshape(heads, length, 1)
+    last = jnp.broadcast_to(cum[..., CHUNK - 1:], cum.shape).reshape(heads, length, 1)
     whole = lambda *shape: pl.BlockSpec(shape, lambda i: (0,) * len(shape))
     return pl.pallas_call(
         delta_kernel,
         grid=(1,),
         in_specs=[whole(heads, length, kw), whole(heads, length, kw), whole(heads, length, vw),
-                  whole(heads, length, 1), whole(heads, length, 1), whole(heads, n_chunks, CHUNK)],
+                  whole(heads, length, 1), whole(heads, length, 1),
+                  whole(heads, length // GROUP, GROUP), whole(heads, length, 1)],
         out_specs=[whole(heads, length, vw + kw), whole(heads, kw, vw + kw)],
         out_shape=[jax.ShapeDtypeStruct((heads, length, vw + kw), jnp.float32),
                    jax.ShapeDtypeStruct((heads, kw, vw + kw), jnp.float32)],
+        scratch_shapes=[pltpu.VMEM((heads, length, vw), jnp.float32),
+                        pltpu.VMEM((heads, length, kw), jnp.float32),
+                        pltpu.VMEM((heads, length, kw), jnp.float32),
+                        pltpu.VMEM((heads, length, kw), jnp.float32),
+                        pltpu.VMEM((heads, length, GROUP), jnp.float32),
+                        pltpu.VMEM((heads, length, vw + kw), jnp.float32),
+                        pltpu.VMEM((heads, n_chunks, kw, vw + kw), jnp.float32)],
         name="delta_chunks",
-    )(queries, key_rows, values, beta_col, cum_col, cum)
+    )(queries, key_rows, values, strength.reshape(heads, length, 1), cum.reshape(heads, length, 1),
+      cum.reshape(heads, length // GROUP, GROUP), last)
 
 
 def passed_along(value, axis, steps):

time: 525 us -> 494 us (0.941)
  Pallas kernels: 68.3 us -> 39 us
  waiting for transfers between devices: 167 us -> 160 us
    pallas_call x1, Pallas kernels: 68.3 us -> 39 us  [local_delta(): pl.pallas_call(delta_kernel, grid=(1,), in_specs=[whole(heads, length, kw...]
    ppermute x6, waiting for transfers between devices: 38.3 us -> 32.7 us  [shifted(): lax.ppermute(value, axis, [(source, source + steps) for source in range(c...]
  transfers between devices with their start and end apart: 10 -> 10, of which waited for: 8 -> 8; matrix products, arithmetic and copies ran while one was open for 4% -> 5% of each run, Pallas kernels for 0% -> 0%
where the time goes in v6:
time: 494 us; the launch traced here: 488 us
  waiting for transfers between devices  160 us (32%)
  blocking collectives  87.5 us (18%)
  matrix products  71.1 us (14%)
  local copies, waits for them, and re-layouts  54.9 us (11%)
  starting transfers between devices  41.4 us (8%)
  Pallas kernels  39 us (8%)
  other arithmetic  19.7 us (4%)
  between operations  14.9 us (3%)
    all_to_all x1, blocking collectives, on_device(): lax.all_to_all(outgoing, ('ctx', 'head'), split_axis=0, concat_axis=0, ti...  87.5 us
    all_to_all x1, waiting for transfers between devices, on_device(): lax.all_to_all(jnp.einsum('nesh,ehd->nesd', hidden, expert_down, preferre...  70.1 us
    pallas_call x1, Pallas kernels, local_delta(): pl.pallas_call(delta_kernel, grid=(1,), in_specs=[whole(heads, length, kw...  39 us
    ppermute x6, waiting for transfers between devices, shifted(): lax.ppermute(value, axis, [(source, source + steps) for source in range(c...  32.7 us
    ppermute x6, starting transfers between devices, shifted(): lax.ppermute(value, axis, [(source, source + steps) for source in range(c...  32.4 us
    reduce_scatter x1, waiting for transfers between devices, on_device(): lax.psum_scatter(jnp.dot(gated_out, out_weight, preferred_element_type=jn...  28.8 us
    all_gather x1, waiting for transfers between devices, on_device(): piece_rows = lax.all_gather(mixer_in, 'head', axis=0, tiled=True)  28.2 us
    dot_general x1, matrix products, on_device(): jnp.einsum('nesh,ehd->nesd', hidden, expert_down, preferred_element_type=...  20 us
  transfers between devices with their start and end apart: 10, of which 8 were waited for; matrix products, arithmetic and copies ran while one was open for 5% of the time, Pallas kernels for 0%

profile of v6, /device:TPU:1, one launch (start us, length us, event | category | flops | bytes accessed | tf_op | source)
XLA Modules:
  0.0 488.2 jit_solution(14326066033898964832)
XLA Ops:
  17.4 13.0 %copy.134 = bf16[128,2,6,2048]{3,1,2,0:T(2,128)(2,1)S(1)} copy(bf16[128,2,6,2048]{3,0,2,1:T(8,128)(2,1)S(1)} %convolution_convert_fusion) | data formatting | bytes 12582912 | tf_op jit(solution)/shard_map/convert_element_type | solution.py:230
  30.4 87.5 %all_to_all.10 = bf16[128,2,6,2048]{3,1,2,0:T(2,128)(2,1)S(1)} all-to-all(bf16[128,2,6,2048]{3,1,2,0:T(2,128)(2,1)S(1)} %copy.134), channel_id=1, replica_groups=mesh['ctx'=32,'head'=4] {'ctx','head'}, dimensions={0} | all-to-all | bytes 12582912 | tf_op jit(solution)/shard_map/all_to_all | solution.py:231
  120.5 8.6 %fusion.2 = f32[2,128,6,512]{3,1,2,0:T(8,128)} fusion(bf16[128,2,6,2048]{3,1,2,0:T(2,128)(2,1)S(1)} %all_to_all.10, bf16[2,2048,512]{2,1,0:T(8,128)(2,1)S(1)} %copy-done.18), kind=kOutput, calls=%fused_computation.7 | convolution fusion | flops 3221225472 | bytes 13631488 | tf_op jit(solution)/shard_map/nesd,edh->nesh/dot_general | solution.py:235
  129.1 20.0 %convert_bitcast_fusion = bf16[128,2,6,2048]{3,0,2,1:T(8,128)(2,1)} fusion(bf16[2,512,2048]{2,1,0:T(8,128)(2,1)} %param.27, f32[2,128,6,512]{3,1,2,0:T(8,128)} %fusion.2, bf16[2,2048,512]{2,1,0:T(8,128)(2,1)} %param.25, bf16[128,2,6,2048]{3,1,2,0:T(2,128)(2,1)} %copy-done.4), kind=kOutput, calls=%fused_computation.6 | convolution fusion | flops 6450315264 | bytes 24117248 | tf_op jit(solution)/shard_map/nesh,ehd->nesd/dot_general | solution.py:238
  149.1 12.7 %copy.137 = bf16[128,2,6,2048]{3,1,2,0:T(2,128)(2,1)} copy(bf16[128,2,6,2048]{3,0,2,1:T(8,128)(2,1)} %convert_bitcast_fusion) | data formatting | bytes 12582912 | tf_op jit(solution)/shard_map/convert_element_type | solution.py:240
  161.9 4.9 %all-to-all-start.1 = ((bf16[128,2,6,2048]{3,1,2,0:T(2,128)(2,1)}), bf16[128,2,6,2048]{3,1,2,0:T(2,128)(2,1)}, u32[]{:S(2)}, u32[]{:S(2)}) async-start(bf16[128,2,6,2048]{3,1,2,0:T(2,128)(2,1)} %copy.137), calls=%async_computation.1 | async-start | bytes 12582912 | tf_op jit(solution)/shard_map/all_to_all | solution.py:237
  173.8 70.1 %all-to-all-done.1 = bf16[128,2,6,2048]{3,1,2,0:T(2,128)(2,1)} async-done(((bf16[128,2,6,2048]{3,1,2,0:T(2,128)(2,1)}), bf16[128,2,6,2048]{3,1,2,0:T(2,128)(2,1)}, u32[]{:S(2)}, u32[]{:S(2)}) %all-to-all-start.1) | async-done | bytes 6291488 | tf_op jit(solution)/shard_map/all_to_all | solution.py:237
  243.8 12.6 %multiply_reduce_fusion.1 = (f32[128]{0:T(128)S(1)}, bf16[128,2048]{1,0:T(8,128)(2,1)S(1)}) fusion(bf16[128,2048]{1,0:T(8,128)(2,1)S(1)} %copy-done.5, bf16[128,2,6,2048]{3,1,2,0:T(2,128)(2,1)} %all-to-all-done.1, f32[128,128,2,6]{0,3,2,1:T(8,128)} %reshape.145), kind=kOutput, calls=%fused_computation.83 | convolution fusion | flops 4833411072 | bytes 8126976 | tf_op jit(solution)/shard_map/tnes,nesd->td/dot_general | solution.py:250
  258.6 28.2 %all-gather.2.cloned.1.call-done = bf16[512,2048]{1,0:T(8,128)(2,1)} async-done(((bf16[128,2048]{1,0:T(8,128)(2,1)}), bf16[512,2048]{1,0:T(8,128)(2,1)}) %all-gather.2.cloned.1.call-update) | async-done | bytes 2097168 | tf_op jit(solution)/shard_map/all_gather | solution.py:257
  286.8 3.7 convolution_convert_fusion.3
  294.3 3.7 collective-permute-start
  308.3 7.0 %divide_multiply_fusion = f32[512,1024]{0,1:T(8,128)S(1)} fusion(f32[512,1024]{0,1:T(8,128)} %get-tuple-element.11, f32[3,1024]{0,1:T(8,128)S(1)} %convert_element_type.74, f32[1024]{0:T(1024)S(1)} %bitcast.124, f32[1024]{0:T(1024)S(1)} %bitcast.125, f32[1024]{0:T(1024)S(1)} %bitcast.126, f32[1024]{0:T(1024)S(1)} %bitcast.123), kind=kLoop, calls=%fused_computation.38 | loop fusion | flops 7340032 | bytes 4222976 | tf_op jit(solution)/shard_map/jit(silu)/mul | solution.py:280
  326.7 39.0 %delta_chunks.1 = (f32[4,512,256]{2,1,0:T(8,128)}, f32[4,128,256]{2,1,0:T(8,128)}) custom-call(f32[4,512,128]{2,1,0:T(8,128)} %bitcast.118, f32[4,512,128]{2,1,0:T(8,128)} %bitcast.119, f32[4,512,128]{2,1,0:T(8,128)} %bitcast.117, f32[4,512,1]{2,1,0:T(8,128)} %copy.143.b_ref, f32[4,512,1]{2,1,0:T(8,128)} %reshape.166.cc_ref, f32[4,2,256]{2,1,0:T(2,128)} %reshape.154.cg_ref, ...), custom_call_target="tpu_custom_call" | custom-call | tf_op jit(solution)/shard_map/delta_chunks/pallas_call | solution.py:111
  367.6 6.4 %collective-permute-done.1 = f32[4,128,256]{2,1,0:T(8,128)S(1)} collective-permute-done((f32[4,128,256]{2,1,0:T(8,128)}, f32[4,128,256]{2,1,0:T(8,128)S(1)}, u32[]{:S(2)}, u32[]{:S(2)}) %collective-permute-start.1) | collective-permute-done | bytes 524320 | tf_op jit(solution)/shard_map/ppermute | solution.py:140
  375.8 4.0 collective-permute-start.2
  379.8 9.2 %collective-permute-done.2 = f32[4,128,256]{2,1,0:T(8,128)} collective-permute-done((f32[4,128,256]{2,1,0:T(8,128)S(1)}, f32[4,128,256]{2,1,0:T(8,128)}, u32[]{:S(2)}, u32[]{:S(2)}) %collective-permute-start.2) | collective-permute-done | bytes 524320 | tf_op jit(solution)/shard_map/ppermute | solution.py:140
  390.6 5.5 %collective-permute-start.3 = (f32[4,128,256]{2,1,0:T(8,128)S(1)}, f32[4,128,256]{2,1,0:T(8,128)S(1)}, u32[]{:S(2)}, u32[]{:S(2)}) collective-permute-start(f32[4,128,256]{2,1,0:T(8,128)S(1)} %fusion.42), channel_id=1, source_target_pairs={{0,16},{4,20},{8,24},{12,28},{16,32},{20,36},{24,40},{28,44},{32,4... | collective-permute-start | bytes 1572872 | tf_op jit(solution)/shard_map/ppermute | solution.py:140
  396.1 8.5 %collective-permute-done.3 = f32[4,128,256]{2,1,0:T(8,128)S(1)} collective-permute-done((f32[4,128,256]{2,1,0:T(8,128)S(1)}, f32[4,128,256]{2,1,0:T(8,128)S(1)}, u32[]{:S(2)}, u32[]{:S(2)}) %collective-permute-start.3) | collective-permute-done | bytes 524320 | tf_op jit(solution)/shard_map/ppermute | solution.py:140
  406.4 4.4 collective-permute-start.4
  410.8 5.3 %collective-permute-done.4 = f32[4,128,256]{2,1,0:T(8,128)} collective-permute-done((f32[4,128,256]{2,1,0:T(8,128)S(1)}, f32[4,128,256]{2,1,0:T(8,128)}, u32[]{:S(2)}, u32[]{:S(2)}) %collective-permute-start.4) | collective-permute-done | bytes 524320 | tf_op jit(solution)/shard_map/ppermute | solution.py:140
  417.8 5.4 %collective-permute-start.5 = (f32[4,128,128]{2,1,0:T(8,128)S(1)}, f32[4,128,128]{2,1,0:T(8,128)S(1)}, u32[]{:S(2)}, u32[]{:S(2)}) collective-permute-start(f32[4,128,128]{2,1,0:T(8,128)S(1)} %slice.107), channel_id=1, source_target_pairs={{0,64},{4,68},{8,72},{12,76},{16,80},{20,84},{24,88},{28,92},{32,9... | collective-permute-start | bytes 786440 | tf_op jit(solution)/shard_map/ppermute | solution.py:140
  427.6 11.2 %collective-permute-start.6 = (f32[4,128,128]{2,1,0:T(8,128)}, f32[4,128,128]{2,1,0:T(8,128)S(1)}, u32[]{:S(2)}, u32[]{:S(2)}) collective-permute-start(f32[4,128,128]{2,1,0:T(8,128)} %fusion.44), channel_id=1, source_target_pairs={{0,4},{4,8},{8,12},{12,16},{16,20},{20,24},{24,28},{28,32},{32,36}... | collective-permute-start | bytes 786440 | tf_op jit(solution)/shard_map/ppermute | solution.py:140
  438.8 4.3 convolution_convert_fusion.2
  452.4 28.8 %reduce-scatter.2.cloned.1.call-done = bf16[128,2048]{1,0:T(8,128)(2,1)} async-done(((bf16[512,2048]{1,0:T(8,128)(2,1)}), bf16[128,2048]{1,0:T(8,128)(2,1)}) %reduce-scatter.2.cloned.1.call-update) | async-done | bytes 524304 | tf_op jit(solution)/shard_map/reduce_scatter | solution.py:311
  (122 shorter events, 69.4 us)
Async XLA Ops:
  7.2 442.6 %copy-start = (bf16[512,2048]{1,0:T(8,128)(2,1)S(1)}, bf16[512,2048]{1,0:T(8,128)(2,1)}, u32[]{:S(2)}) copy-start(bf16[512,2048]{1,0:T(8,128)(2,1)} %param.41) | copy-start | bytes 6291460
  30.4 90.2 %copy-start.18 = (bf16[2,2048,512]{2,1,0:T(8,128)(2,1)S(1)}, bf16[2,2048,512]{2,1,0:T(8,128)(2,1)}, u32[]{:S(2)}) copy-start(bf16[2,2048,512]{2,1,0:T(8,128)(2,1)} %param.26) | copy-start | bytes 12582916
  117.9 2.6 copy-start.4
  161.9 5.0 %copy-start.13 = (f32[2048]{0:T(1024)S(1)}, f32[2048]{0:T(1024)}, u32[]{:S(2)}) copy-start(f32[2048]{0:T(1024)} %param.22) | copy-start | bytes 24580
  161.9 82.0 %all-to-all-start.1 = ((bf16[128,2,6,2048]{3,1,2,0:T(2,128)(2,1)}), bf16[128,2,6,2048]{3,1,2,0:T(2,128)(2,1)}, u32[]{:S(2)}, u32[]{:S(2)}) async-start(bf16[128,2,6,2048]{3,1,2,0:T(2,128)(2,1)} %copy.137), calls=%async_computation.1 | async-start | bytes 12582912 | tf_op jit(solution)/shard_map/all_to_all | solution.py:237
  166.8 120.0 %all-gather.2.cloned.1.call-start = ((), (), s32[]{:S(2)}) async-start(), calls=%async_computation.3 | async-start | bytes 2621440 | tf_op jit(solution)/shard_map/all_gather | solution.py:257
  173.7 83.5 %copy-start.11 = (f32[2048]{0:T(1024)S(1)}, f32[2048]{0:T(1024)}, u32[]{:S(2)}) copy-start(f32[2048]{0:T(1024)} %param.28) | copy-start | bytes 24580
  256.4 2.1 copy-start.21
  258.2 222.9 %reduce-scatter.2.cloned.1.call-start = ((), (), s32[]{:S(2)}) async-start(), calls=%async_computation.4 | async-start | bytes 2621440 | tf_op jit(solution)/shard_map/reduce_scatter | solution.py:311
  286.8 3.7 copy-start.3
  286.8 3.7 copy-start.19
  292.5 5.6 %copy-start.9 = (bf16[2048,4]{0,1:T(4,128)(2,1)S(1)}, bf16[2048,4]{0,1:T(4,128)(2,1)}, u32[]{:S(2)}) copy-start(bf16[2048,4]{0,1:T(4,128)(2,1)} %param.34) | copy-start | bytes 49156
  292.5 5.6 %copy-start.16 = (f32[4]{0:T(128)S(1)}, f32[4]{0:T(128)}, u32[]{:S(2)}) copy-start(f32[4]{0:T(128)} %param.39) | copy-start | bytes 52
  294.2 5.5 %copy-start.10 = (bf16[2048,4]{0,1:T(4,128)(2,1)S(1)}, bf16[2048,4]{0,1:T(4,128)(2,1)}, u32[]{:S(2)}) copy-start(bf16[2048,4]{0,1:T(4,128)(2,1)} %param.33) | copy-start | bytes 49156
  294.3 14.0 %collective-permute-start = (bf16[3,1024]{0,1:T(8,128)(2,1)S(1)}, bf16[3,1024]{0,1:T(8,128)(2,1)S(1)}, u32[]{:S(2)}, u32[]{:S(2)}) collective-permute-start(bf16[3,1024]{0,1:T(8,128)(2,1)S(1)} %slice.92), channel_id=1, source_target_pairs={{0,4},{4,8},{8,12},{12,16},{16,20},{20,24},{24,28},{28,32},{32,36}... | collective-permute-start | bytes 18440 | tf_op jit(solution)/shard_map/ppermute | solution.py:135
  317.0 4.2 slice-start
  365.7 8.3 %collective-permute-start.1 = (f32[4,128,256]{2,1,0:T(8,128)}, f32[4,128,256]{2,1,0:T(8,128)S(1)}, u32[]{:S(2)}, u32[]{:S(2)}) collective-permute-start(f32[4,128,256]{2,1,0:T(8,128)} %get-tuple-element.5), channel_id=1, source_target_pairs={{0,4},{4,8},{8,12},{12,16},{16,20},{20,24},{24,28},{28,32},{32,36}... | collective-permute-start | bytes 1572872 | tf_op jit(solution)/shard_map/ppermute | solution.py:140
  375.8 13.2 %collective-permute-start.2 = (f32[4,128,256]{2,1,0:T(8,128)S(1)}, f32[4,128,256]{2,1,0:T(8,128)}, u32[]{:S(2)}, u32[]{:S(2)}) collective-permute-start(f32[4,128,256]{2,1,0:T(8,128)S(1)} %fusion.43), channel_id=1, source_target_pairs={{0,8},{4,12},{8,16},{12,20},{16,24},{20,28},{24,32},{28,36},{32,40... | collective-permute-start | bytes 1572872 | tf_op jit(solution)/shard_map/ppermute | solution.py:140
  390.6 5.5 %copy-start.6 = (f32[4,128,256]{2,1,0:T(8,128)}, f32[4,128,256]{2,1,0:T(8,128)S(1)}, u32[]{:S(2)}) copy-start(f32[4,128,256]{2,1,0:T(8,128)S(1)} %fusion.42) | copy-start | bytes 1572868
  390.6 14.0 %collective-permute-start.3 = (f32[4,128,256]{2,1,0:T(8,128)S(1)}, f32[4,128,256]{2,1,0:T(8,128)S(1)}, u32[]{:S(2)}, u32[]{:S(2)}) collective-permute-start(f32[4,128,256]{2,1,0:T(8,128)S(1)} %fusion.42), channel_id=1, source_target_pairs={{0,16},{4,20},{8,24},{12,28},{16,32},{20,36},{24,40},{28,44},{32,4... | collective-permute-start | bytes 1572872 | tf_op jit(solution)/shard_map/ppermute | solution.py:140
  406.4 9.7 %collective-permute-start.4 = (f32[4,128,256]{2,1,0:T(8,128)S(1)}, f32[4,128,256]{2,1,0:T(8,128)}, u32[]{:S(2)}, u32[]{:S(2)}) collective-permute-start(f32[4,128,256]{2,1,0:T(8,128)S(1)} %fusion.41), channel_id=1, source_target_pairs={{0,32},{4,36},{8,40},{12,44},{16,48},{20,52},{24,56},{28,60},{32,6... | collective-permute-start | bytes 1572872 | tf_op jit(solution)/shard_map/ppermute | solution.py:140
  417.8 8.7 %collective-permute-start.5 = (f32[4,128,128]{2,1,0:T(8,128)S(1)}, f32[4,128,128]{2,1,0:T(8,128)S(1)}, u32[]{:S(2)}, u32[]{:S(2)}) collective-permute-start(f32[4,128,128]{2,1,0:T(8,128)S(1)} %slice.107), channel_id=1, source_target_pairs={{0,64},{4,68},{8,72},{12,76},{16,80},{20,84},{24,88},{28,92},{32,9... | collective-permute-start | bytes 786440 | tf_op jit(solution)/shard_map/ppermute | solution.py:140
  427.6 16.8 %collective-permute-start.6 = (f32[4,128,128]{2,1,0:T(8,128)}, f32[4,128,128]{2,1,0:T(8,128)S(1)}, u32[]{:S(2)}, u32[]{:S(2)}) collective-permute-start(f32[4,128,128]{2,1,0:T(8,128)} %fusion.44), channel_id=1, source_target_pairs={{0,4},{4,8},{8,12},{12,16},{16,20},{20,24},{24,28},{28,32},{32,36}... | collective-permute-start | bytes 786440 | tf_op jit(solution)/shard_map/ppermute | solution.py:140
  443.1 4.2 copy-start.17
  (9 other events, 14.5 us)
Sparse Core Ops, SparseCore 0:
  258.4 28.4 all-gather.1
  452.5 28.6 reduce-scatter.1

commit v7 on v6

--- a/solution.py
+++ b/solution.py
@@ -247,9 +247,15 @@
         jnp.where(place_rows[:, :, None] == slot_ids[None, None, :], weights[:, :, None], 0.0), axis=1
     )
     mix = mix.reshape(tok_rows, sources, local_experts, capacity)
-    moe_out = jnp.einsum(
-        "tnes,nesd->td", mix, returned.astype(jnp.float32), precision=HI
-    ).astype(jnp.bfloat16)
+    mix_high = mix.astype(jnp.bfloat16)
+    mix_low = (mix - mix_high.astype(jnp.float32)).astype(jnp.bfloat16)
+    both = jnp.einsum(
+        "tnes,nesd->td",
+        jnp.concatenate([mix_high, mix_low], axis=0),
+        returned,
+        preferred_element_type=jnp.float32,
+    )
+    moe_out = (both[:tok_rows] + both[tok_rows:]).astype(jnp.bfloat16)
     mixer_in = rms_rows(
         stream.astype(jnp.float32) + moe_out.astype(jnp.float32), mixer_gain
     ).astype(jnp.bfloat16)

time: 494 us -> 490 us (level)
  no operation moved by 1% of the time
where the time goes in v7:
time: 490 us; the launch traced here: 485 us
  waiting for transfers between devices  157 us (32%)
  blocking collectives  87.4 us (18%)
  matrix products  67.1 us (14%)
  local copies, waits for them, and re-layouts  56.4 us (12%)
  starting transfers between devices  41.2 us (8%)
  Pallas kernels  39 us (8%)
  other arithmetic  21.2 us (4%)
  between operations  15.1 us (3%)
    all_to_all x1, blocking collectives, on_device(): lax.all_to_all(outgoing, ('ctx', 'head'), split_axis=0, concat_axis=0, ti...  87.4 us
    all_to_all x1, waiting for transfers between devices, on_device(): lax.all_to_all(jnp.einsum('nesh,ehd->nesd', hidden, expert_down, preferre...  67.2 us
    pallas_call x1, Pallas kernels, local_delta(): pl.pallas_call(delta_kernel, grid=(1,), in_specs=[whole(heads, length, kw...  39 us
    ppermute x6, waiting for transfers between devices, shifted(): lax.ppermute(value, axis, [(source, source + steps) for source in range(c...  32.6 us
    ppermute x6, starting transfers between devices, shifted(): lax.ppermute(value, axis, [(source, source + steps) for source in range(c...  32.5 us
    reduce_scatter x1, waiting for transfers between devices, on_device(): lax.psum_scatter(jnp.dot(gated_out, out_weight, preferred_element_type=jn...  28.8 us
    all_gather x1, waiting for transfers between devices, on_device(): piece_rows = lax.all_gather(mixer_in, 'head', axis=0, tiled=True)  28.4 us
    dot_general x1, matrix products, on_device(): jnp.einsum('nesh,ehd->nesd', hidden, expert_down, preferred_element_type=...  19.7 us
  transfers between devices with their start and end apart: 10, of which 8 were waited for; matrix products, arithmetic and copies ran while one was open for 5% of the time, Pallas kernels for 0%

profile of v7, /device:TPU:1, one launch (start us, length us, event | category | flops | bytes accessed | tf_op | source)
XLA Modules:
  0.0 484.5 jit_solution(8462076974232546184)
XLA Ops:
  17.4 13.0 %copy.140 = bf16[128,2,6,2048]{3,1,2,0:T(2,128)(2,1)S(1)} copy(bf16[128,2,6,2048]{3,0,2,1:T(8,128)(2,1)S(1)} %convolution_convert_fusion) | data formatting | bytes 12582912 | tf_op jit(solution)/shard_map/convert_element_type | solution.py:230
  30.4 87.4 %all_to_all.10 = bf16[128,2,6,2048]{3,1,2,0:T(2,128)(2,1)S(1)} all-to-all(bf16[128,2,6,2048]{3,1,2,0:T(2,128)(2,1)S(1)} %copy.140), channel_id=1, replica_groups=mesh['ctx'=32,'head'=4] {'ctx','head'}, dimensions={0} | all-to-all | bytes 12582912 | tf_op jit(solution)/shard_map/all_to_all | solution.py:231
  120.4 8.6 %fusion.2 = f32[2,128,6,512]{3,1,2,0:T(8,128)} fusion(bf16[128,2,6,2048]{3,1,2,0:T(2,128)(2,1)S(1)} %all_to_all.10, bf16[2,2048,512]{2,1,0:T(8,128)(2,1)S(1)} %copy-done.18), kind=kOutput, calls=%fused_computation.7 | convolution fusion | flops 3221225472 | bytes 13631488 | tf_op jit(solution)/shard_map/nesd,edh->nesh/dot_general | solution.py:235
  129.0 19.7 %convert_bitcast_fusion = bf16[128,2,6,2048]{3,0,2,1:T(8,128)(2,1)} fusion(bf16[2,512,2048]{2,1,0:T(8,128)(2,1)} %param.27, f32[2,128,6,512]{3,1,2,0:T(8,128)} %fusion.2, bf16[2,2048,512]{2,1,0:T(8,128)(2,1)} %param.25, bf16[128,2,6,2048]{3,1,2,0:T(2,128)(2,1)} %copy-done.5), kind=kOutput, calls=%fused_computation.6 | convolution fusion | flops 6450315264 | bytes 24117248 | tf_op jit(solution)/shard_map/nesh,ehd->nesd/dot_general | solution.py:238
  148.7 12.7 %copy.143 = bf16[128,2,6,2048]{3,1,2,0:T(2,128)(2,1)} copy(bf16[128,2,6,2048]{3,0,2,1:T(8,128)(2,1)} %convert_bitcast_fusion) | data formatting | bytes 12582912 | tf_op jit(solution)/shard_map/convert_element_type | solution.py:240
  161.4 4.9 %all-to-all-start.1 = ((bf16[128,2,6,2048]{3,1,2,0:T(2,128)(2,1)}), bf16[128,2,6,2048]{3,1,2,0:T(2,128)(2,1)}, u32[]{:S(2)}, u32[]{:S(2)}) async-start(bf16[128,2,6,2048]{3,1,2,0:T(2,128)(2,1)} %copy.143), calls=%async_computation.1 | async-start | bytes 12582912 | tf_op jit(solution)/shard_map/all_to_all | solution.py:237
  176.2 67.2 %all-to-all-done.1 = bf16[128,2,6,2048]{3,1,2,0:T(2,128)(2,1)} async-done(((bf16[128,2,6,2048]{3,1,2,0:T(2,128)(2,1)}), bf16[128,2,6,2048]{3,1,2,0:T(2,128)(2,1)}, u32[]{:S(2)}, u32[]{:S(2)}) %all-to-all-start.1) | async-done | bytes 6291488 | tf_op jit(solution)/shard_map/all_to_all | solution.py:237
  243.4 8.9 %fusion.13 = f32[256,2048]{1,0:T(8,128)S(1)} fusion(bf16[128,2,6,2048]{3,1,2,0:T(2,128)(2,1)} %all-to-all-done.1, bf16[128,128,2,6]{1,0,3,2:T(8,128)(2,1)} %get-tuple-element.10, bf16[128,128,2,6]{1,0,3,2:T(8,128)(2,1)} %get-tuple-element.11), kind=kOutput, calls=%fused_computation.25 | convolution fusion | flops 1612185600 | bytes 9175040 | tf_op jit(solution)/shard_map/tnes,nesd->td/dot_general | solution.py:252
  254.7 28.4 %all-gather.2.cloned.1.call-done = bf16[512,2048]{1,0:T(8,128)(2,1)} async-done(((bf16[128,2048]{1,0:T(8,128)(2,1)}), bf16[512,2048]{1,0:T(8,128)(2,1)}) %all-gather.2.cloned.1.call-update) | async-done | bytes 2097168 | tf_op jit(solution)/shard_map/all_gather | solution.py:263
  283.1 3.7 convolution_convert_fusion.3
  290.6 3.7 collective-permute-start
  304.6 6.8 %divide_multiply_fusion = f32[512,1024]{0,1:T(8,128)S(1)} fusion(f32[512,1024]{0,1:T(8,128)} %get-tuple-element.15, f32[3,1024]{0,1:T(8,128)S(1)} %convert_element_type.85, f32[1024]{0:T(1024)S(1)} %bitcast.122, f32[1024]{0:T(1024)S(1)} %bitcast.123, f32[1024]{0:T(1024)S(1)} %bitcast.124, f32[1024]{0:T(1024)S(1)} %bitcast.121), kind=kLoop, calls=%fused_computation.37 | loop fusion | flops 7340032 | bytes 4222976 | tf_op jit(solution)/shard_map/jit(silu)/mul | solution.py:286
  322.8 39.0 %delta_chunks.1 = (f32[4,512,256]{2,1,0:T(8,128)}, f32[4,128,256]{2,1,0:T(8,128)}) custom-call(f32[4,512,128]{2,1,0:T(8,128)} %bitcast.116, f32[4,512,128]{2,1,0:T(8,128)} %bitcast.117, f32[4,512,128]{2,1,0:T(8,128)} %bitcast.115, f32[4,512,1]{2,1,0:T(8,128)} %copy.148.b_ref, f32[4,512,1]{2,1,0:T(8,128)} %reshape.166.cc_ref, f32[4,2,256]{2,1,0:T(2,128)} %reshape.154.cg_ref, ...), custom_call_target="tpu_custom_call" | custom-call | tf_op jit(solution)/shard_map/delta_chunks/pallas_call | solution.py:111
  363.7 6.4 %collective-permute-done.1 = f32[4,128,256]{2,1,0:T(8,128)S(1)} collective-permute-done((f32[4,128,256]{2,1,0:T(8,128)}, f32[4,128,256]{2,1,0:T(8,128)S(1)}, u32[]{:S(2)}, u32[]{:S(2)}) %collective-permute-start.1) | collective-permute-done | bytes 524320 | tf_op jit(solution)/shard_map/ppermute | solution.py:140
  371.9 4.0 collective-permute-start.2
  375.9 9.2 %collective-permute-done.2 = f32[4,128,256]{2,1,0:T(8,128)} collective-permute-done((f32[4,128,256]{2,1,0:T(8,128)S(1)}, f32[4,128,256]{2,1,0:T(8,128)}, u32[]{:S(2)}, u32[]{:S(2)}) %collective-permute-start.2) | collective-permute-done | bytes 524320 | tf_op jit(solution)/shard_map/ppermute | solution.py:140
  386.7 5.5 %collective-permute-start.3 = (f32[4,128,256]{2,1,0:T(8,128)S(1)}, f32[4,128,256]{2,1,0:T(8,128)S(1)}, u32[]{:S(2)}, u32[]{:S(2)}) collective-permute-start(f32[4,128,256]{2,1,0:T(8,128)S(1)} %fusion.39), channel_id=1, source_target_pairs={{0,16},{4,20},{8,24},{12,28},{16,32},{20,36},{24,40},{28,44},{32,4... | collective-permute-start | bytes 1572872 | tf_op jit(solution)/shard_map/ppermute | solution.py:140
  392.3 8.5 %collective-permute-done.3 = f32[4,128,256]{2,1,0:T(8,128)S(1)} collective-permute-done((f32[4,128,256]{2,1,0:T(8,128)S(1)}, f32[4,128,256]{2,1,0:T(8,128)S(1)}, u32[]{:S(2)}, u32[]{:S(2)}) %collective-permute-start.3) | collective-permute-done | bytes 524320 | tf_op jit(solution)/shard_map/ppermute | solution.py:140
  402.5 4.4 collective-permute-start.4
  406.9 5.3 %collective-permute-done.4 = f32[4,128,256]{2,1,0:T(8,128)} collective-permute-done((f32[4,128,256]{2,1,0:T(8,128)S(1)}, f32[4,128,256]{2,1,0:T(8,128)}, u32[]{:S(2)}, u32[]{:S(2)}) %collective-permute-start.4) | collective-permute-done | bytes 524320 | tf_op jit(solution)/shard_map/ppermute | solution.py:140
  413.9 5.5 %collective-permute-start.5 = (f32[4,128,128]{2,1,0:T(8,128)S(1)}, f32[4,128,128]{2,1,0:T(8,128)S(1)}, u32[]{:S(2)}, u32[]{:S(2)}) collective-permute-start(f32[4,128,128]{2,1,0:T(8,128)S(1)} %slice.117), channel_id=1, source_target_pairs={{0,64},{4,68},{8,72},{12,76},{16,80},{20,84},{24,88},{28,92},{32,9... | collective-permute-start | bytes 786440 | tf_op jit(solution)/shard_map/ppermute | solution.py:140
  423.7 11.2 %collective-permute-start.6 = (f32[4,128,128]{2,1,0:T(8,128)}, f32[4,128,128]{2,1,0:T(8,128)S(1)}, u32[]{:S(2)}, u32[]{:S(2)}) collective-permute-start(f32[4,128,128]{2,1,0:T(8,128)} %fusion.41), channel_id=1, source_target_pairs={{0,4},{4,8},{8,12},{12,16},{16,20},{20,24},{24,28},{28,32},{32,36}... | collective-permute-start | bytes 786440 | tf_op jit(solution)/shard_map/ppermute | solution.py:140
  434.9 4.3 convolution_convert_fusion.2
  448.5 28.8 %reduce-scatter.2.cloned.1.call-done = bf16[128,2048]{1,0:T(8,128)(2,1)} async-done(((bf16[512,2048]{1,0:T(8,128)(2,1)}), bf16[128,2048]{1,0:T(8,128)(2,1)}) %reduce-scatter.2.cloned.1.call-update) | async-done | bytes 524304 | tf_op jit(solution)/shard_map/reduce_scatter | solution.py:317
  (125 shorter events, 72.4 us)
Async XLA Ops:
  7.2 438.7 %copy-start = (bf16[512,2048]{1,0:T(8,128)(2,1)S(1)}, bf16[512,2048]{1,0:T(8,128)(2,1)}, u32[]{:S(2)}) copy-start(bf16[512,2048]{1,0:T(8,128)(2,1)} %param.41) | copy-start | bytes 6291460
  30.3 90.1 %copy-start.18 = (bf16[2,2048,512]{2,1,0:T(8,128)(2,1)S(1)}, bf16[2,2048,512]{2,1,0:T(8,128)(2,1)}, u32[]{:S(2)}) copy-start(bf16[2,2048,512]{2,1,0:T(8,128)(2,1)} %param.26) | copy-start | bytes 12582916
  117.8 2.6 copy-start.5
  161.4 5.0 %copy-start.13 = (f32[2048]{0:T(1024)S(1)}, f32[2048]{0:T(1024)}, u32[]{:S(2)}) copy-start(f32[2048]{0:T(1024)} %param.22) | copy-start | bytes 24580
  161.4 82.0 %all-to-all-start.1 = ((bf16[128,2,6,2048]{3,1,2,0:T(2,128)(2,1)}), bf16[128,2,6,2048]{3,1,2,0:T(2,128)(2,1)}, u32[]{:S(2)}, u32[]{:S(2)}) async-start(bf16[128,2,6,2048]{3,1,2,0:T(2,128)(2,1)} %copy.143), calls=%async_computation.1 | async-start | bytes 12582912 | tf_op jit(solution)/shard_map/all_to_all | solution.py:237
  166.3 116.8 %all-gather.2.cloned.1.call-start = ((), (), s32[]{:S(2)}) async-start(), calls=%async_computation.3 | async-start | bytes 2621440 | tf_op jit(solution)/shard_map/all_gather | solution.py:263
  252.4 2.3 copy-start.12
  252.4 2.3 copy-start.21
  254.5 222.7 %reduce-scatter.2.cloned.1.call-start = ((), (), s32[]{:S(2)}) async-start(), calls=%async_computation.4 | async-start | bytes 2621440 | tf_op jit(solution)/shard_map/reduce_scatter | solution.py:317
  283.1 3.7 copy-start.3
  283.1 3.7 copy-start.19
  288.8 5.6 %copy-start.9 = (bf16[2048,4]{0,1:T(4,128)(2,1)S(1)}, bf16[2048,4]{0,1:T(4,128)(2,1)}, u32[]{:S(2)}) copy-start(bf16[2048,4]{0,1:T(4,128)(2,1)} %param.34) | copy-start | bytes 49156
  288.8 5.6 %copy-start.16 = (f32[4]{0:T(128)S(1)}, f32[4]{0:T(128)}, u32[]{:S(2)}) copy-start(f32[4]{0:T(128)} %param.39) | copy-start | bytes 52
  290.5 5.6 %copy-start.10 = (bf16[2048,4]{0,1:T(4,128)(2,1)S(1)}, bf16[2048,4]{0,1:T(4,128)(2,1)}, u32[]{:S(2)}) copy-start(bf16[2048,4]{0,1:T(4,128)(2,1)} %param.33) | copy-start | bytes 49156
  290.6 13.9 %collective-permute-start = (bf16[3,1024]{0,1:T(8,128)(2,1)S(1)}, bf16[3,1024]{0,1:T(8,128)(2,1)S(1)}, u32[]{:S(2)}, u32[]{:S(2)}) collective-permute-start(bf16[3,1024]{0,1:T(8,128)(2,1)S(1)} %slice.102), channel_id=1, source_target_pairs={{0,4},{4,8},{8,12},{12,16},{16,20},{20,24},{24,28},{28,32},{32,36}... | collective-permute-start | bytes 18440 | tf_op jit(solution)/shard_map/ppermute | solution.py:135
  313.0 4.2 slice-start
  361.8 8.3 %collective-permute-start.1 = (f32[4,128,256]{2,1,0:T(8,128)}, f32[4,128,256]{2,1,0:T(8,128)S(1)}, u32[]{:S(2)}, u32[]{:S(2)}) collective-permute-start(f32[4,128,256]{2,1,0:T(8,128)} %get-tuple-element.5), channel_id=1, source_target_pairs={{0,4},{4,8},{8,12},{12,16},{16,20},{20,24},{24,28},{28,32},{32,36}... | collective-permute-start | bytes 1572872 | tf_op jit(solution)/shard_map/ppermute | solution.py:140
  371.9 13.2 %collective-permute-start.2 = (f32[4,128,256]{2,1,0:T(8,128)S(1)}, f32[4,128,256]{2,1,0:T(8,128)}, u32[]{:S(2)}, u32[]{:S(2)}) collective-permute-start(f32[4,128,256]{2,1,0:T(8,128)S(1)} %fusion.40), channel_id=1, source_target_pairs={{0,8},{4,12},{8,16},{12,20},{16,24},{20,28},{24,32},{28,36},{32,40... | collective-permute-start | bytes 1572872 | tf_op jit(solution)/shard_map/ppermute | solution.py:140
  386.7 5.5 %copy-start.7 = (f32[4,128,256]{2,1,0:T(8,128)}, f32[4,128,256]{2,1,0:T(8,128)S(1)}, u32[]{:S(2)}) copy-start(f32[4,128,256]{2,1,0:T(8,128)S(1)} %fusion.39) | copy-start | bytes 1572868
  386.7 14.0 %collective-permute-start.3 = (f32[4,128,256]{2,1,0:T(8,128)S(1)}, f32[4,128,256]{2,1,0:T(8,128)S(1)}, u32[]{:S(2)}, u32[]{:S(2)}) collective-permute-start(f32[4,128,256]{2,1,0:T(8,128)S(1)} %fusion.39), channel_id=1, source_target_pairs={{0,16},{4,20},{8,24},{12,28},{16,32},{20,36},{24,40},{28,44},{32,4... | collective-permute-start | bytes 1572872 | tf_op jit(solution)/shard_map/ppermute | solution.py:140
  402.5 9.7 %collective-permute-start.4 = (f32[4,128,256]{2,1,0:T(8,128)S(1)}, f32[4,128,256]{2,1,0:T(8,128)}, u32[]{:S(2)}, u32[]{:S(2)}) collective-permute-start(f32[4,128,256]{2,1,0:T(8,128)S(1)} %fusion.38), channel_id=1, source_target_pairs={{0,32},{4,36},{8,40},{12,44},{16,48},{20,52},{24,56},{28,60},{32,6... | collective-permute-start | bytes 1572872 | tf_op jit(solution)/shard_map/ppermute | solution.py:140
  413.9 8.7 %collective-permute-start.5 = (f32[4,128,128]{2,1,0:T(8,128)S(1)}, f32[4,128,128]{2,1,0:T(8,128)S(1)}, u32[]{:S(2)}, u32[]{:S(2)}) collective-permute-start(f32[4,128,128]{2,1,0:T(8,128)S(1)} %slice.117), channel_id=1, source_target_pairs={{0,64},{4,68},{8,72},{12,76},{16,80},{20,84},{24,88},{28,92},{32,9... | collective-permute-start | bytes 786440 | tf_op jit(solution)/shard_map/ppermute | solution.py:140
  423.7 16.8 %collective-permute-start.6 = (f32[4,128,128]{2,1,0:T(8,128)}, f32[4,128,128]{2,1,0:T(8,128)S(1)}, u32[]{:S(2)}, u32[]{:S(2)}) collective-permute-start(f32[4,128,128]{2,1,0:T(8,128)} %fusion.41), channel_id=1, source_target_pairs={{0,4},{4,8},{8,12},{12,16},{16,20},{20,24},{24,28},{28,32},{32,36}... | collective-permute-start | bytes 786440 | tf_op jit(solution)/shard_map/ppermute | solution.py:140
  439.3 4.2 copy-start.17
  (9 other events, 13.9 us)
Sparse Core Ops, SparseCore 0:
  254.7 28.4 all-gather.1
  448.6 28.6 reduce-scatter.1

commit v8 on v7

--- a/solution.py
+++ b/solution.py
@@ -247,8 +247,9 @@
         jnp.where(place_rows[:, :, None] == slot_ids[None, None, :], weights[:, :, None], 0.0), axis=1
     )
     mix = mix.reshape(tok_rows, sources, local_experts, capacity)
-    mix_high = mix.astype(jnp.bfloat16)
-    mix_low = (mix - mix_high.astype(jnp.float32)).astype(jnp.bfloat16)
+    mix_rounded = lax.reduce_precision(mix, exponent_bits=8, mantissa_bits=7)
+    mix_high = mix_rounded.astype(jnp.bfloat16)
+    mix_low = (mix - mix_rounded).astype(jnp.bfloat16)
     both = jnp.einsum(
         "tnes,nesd->td",
         jnp.concatenate([mix_high, mix_low], axis=0),

time: 490 us -> 490 us (level)
  no operation moved by 1% of the time
where the time goes in v8:
time: 490 us; the launch traced here: 485 us
  waiting for transfers between devices  157 us (32%)
  blocking collectives  87.4 us (18%)
  matrix products  67.1 us (14%)
  local copies, waits for them, and re-layouts  56.4 us (12%)
  starting transfers between devices  41.2 us (8%)
  Pallas kernels  39 us (8%)
  other arithmetic  21.2 us (4%)
  between operations  15.1 us (3%)
    all_to_all x1, blocking collectives, on_device(): lax.all_to_all(outgoing, ('ctx', 'head'), split_axis=0, concat_axis=0, ti...  87.4 us
    all_to_all x1, waiting for transfers between devices, on_device(): lax.all_to_all(jnp.einsum('nesh,ehd->nesd', hidden, expert_down, preferre...  67.2 us
    pallas_call x1, Pallas kernels, local_delta(): pl.pallas_call(delta_kernel, grid=(1,), in_specs=[whole(heads, length, kw...  39 us
    ppermute x6, waiting for transfers between devices, shifted(): lax.ppermute(value, axis, [(source, source + steps) for source in range(c...  32.6 us
    ppermute x6, starting transfers between devices, shifted(): lax.ppermute(value, axis, [(source, source + steps) for source in range(c...  32.5 us
    reduce_scatter x1, waiting for transfers between devices, on_device(): lax.psum_scatter(jnp.dot(gated_out, out_weight, preferred_element_type=jn...  28.8 us
    all_gather x1, waiting for transfers between devices, on_device(): piece_rows = lax.all_gather(mixer_in, 'head', axis=0, tiled=True)  28.4 us
    dot_general x1, matrix products, on_device(): jnp.einsum('nesh,ehd->nesd', hidden, expert_down, preferred_element_type=...  19.7 us
  transfers between devices with their start and end apart: 10, of which 8 were waited for; matrix products, arithmetic and copies ran while one was open for 5% of the time, Pallas kernels for 0%

profile of v8, /device:TPU:1, one launch (start us, length us, event | category | flops | bytes accessed | tf_op | source)
XLA Modules:
  0.0 484.5 jit_solution(11634958608576271872)
XLA Ops:
  17.4 13.0 %copy.140 = bf16[128,2,6,2048]{3,1,2,0:T(2,128)(2,1)S(1)} copy(bf16[128,2,6,2048]{3,0,2,1:T(8,128)(2,1)S(1)} %convolution_convert_fusion) | data formatting | bytes 12582912 | tf_op jit(solution)/shard_map/convert_element_type | solution.py:230
  30.4 87.4 %all_to_all.10 = bf16[128,2,6,2048]{3,1,2,0:T(2,128)(2,1)S(1)} all-to-all(bf16[128,2,6,2048]{3,1,2,0:T(2,128)(2,1)S(1)} %copy.140), channel_id=1, replica_groups=mesh['ctx'=32,'head'=4] {'ctx','head'}, dimensions={0} | all-to-all | bytes 12582912 | tf_op jit(solution)/shard_map/all_to_all | solution.py:231
  120.4 8.6 %fusion.2 = f32[2,128,6,512]{3,1,2,0:T(8,128)} fusion(bf16[128,2,6,2048]{3,1,2,0:T(2,128)(2,1)S(1)} %all_to_all.10, bf16[2,2048,512]{2,1,0:T(8,128)(2,1)S(1)} %copy-done.18), kind=kOutput, calls=%fused_computation.7 | convolution fusion | flops 3221225472 | bytes 13631488 | tf_op jit(solution)/shard_map/nesd,edh->nesh/dot_general | solution.py:235
  129.0 19.7 %convert_bitcast_fusion = bf16[128,2,6,2048]{3,0,2,1:T(8,128)(2,1)} fusion(bf16[2,512,2048]{2,1,0:T(8,128)(2,1)} %param.27, f32[2,128,6,512]{3,1,2,0:T(8,128)} %fusion.2, bf16[2,2048,512]{2,1,0:T(8,128)(2,1)} %param.25, bf16[128,2,6,2048]{3,1,2,0:T(2,128)(2,1)} %copy-done.5), kind=kOutput, calls=%fused_computation.6 | convolution fusion | flops 6450315264 | bytes 24117248 | tf_op jit(solution)/shard_map/nesh,ehd->nesd/dot_general | solution.py:238
  148.7 12.7 %copy.143 = bf16[128,2,6,2048]{3,1,2,0:T(2,128)(2,1)} copy(bf16[128,2,6,2048]{3,0,2,1:T(8,128)(2,1)} %convert_bitcast_fusion) | data formatting | bytes 12582912 | tf_op jit(solution)/shard_map/convert_element_type | solution.py:240
  161.4 4.9 %all-to-all-start.1 = ((bf16[128,2,6,2048]{3,1,2,0:T(2,128)(2,1)}), bf16[128,2,6,2048]{3,1,2,0:T(2,128)(2,1)}, u32[]{:S(2)}, u32[]{:S(2)}) async-start(bf16[128,2,6,2048]{3,1,2,0:T(2,128)(2,1)} %copy.143), calls=%async_computation.1 | async-start | bytes 12582912 | tf_op jit(solution)/shard_map/all_to_all | solution.py:237
  176.2 67.2 %all-to-all-done.1 = bf16[128,2,6,2048]{3,1,2,0:T(2,128)(2,1)} async-done(((bf16[128,2,6,2048]{3,1,2,0:T(2,128)(2,1)}), bf16[128,2,6,2048]{3,1,2,0:T(2,128)(2,1)}, u32[]{:S(2)}, u32[]{:S(2)}) %all-to-all-start.1) | async-done | bytes 6291488 | tf_op jit(solution)/shard_map/all_to_all | solution.py:237
  243.4 8.9 %fusion.13 = f32[256,2048]{1,0:T(8,128)S(1)} fusion(bf16[128,2,6,2048]{3,1,2,0:T(2,128)(2,1)} %all-to-all-done.1, bf16[128,128,2,6]{1,0,3,2:T(8,128)(2,1)} %get-tuple-element.15, bf16[128,128,2,6]{1,0,3,2:T(8,128)(2,1)} %get-tuple-element.14), kind=kOutput, calls=%fused_computation.25 | convolution fusion | flops 1612185600 | bytes 9175040 | tf_op jit(solution)/shard_map/tnes,nesd->td/dot_general | solution.py:253
  254.7 28.4 %all-gather.2.cloned.1.call-done = bf16[512,2048]{1,0:T(8,128)(2,1)} async-done(((bf16[128,2048]{1,0:T(8,128)(2,1)}), bf16[512,2048]{1,0:T(8,128)(2,1)}) %all-gather.2.cloned.1.call-update) | async-done | bytes 2097168 | tf_op jit(solution)/shard_map/all_gather | solution.py:264
  283.1 3.7 convolution_convert_fusion.3
  290.6 3.7 collective-permute-start
  304.6 6.8 %divide_multiply_fusion = f32[512,1024]{0,1:T(8,128)S(1)} fusion(f32[512,1024]{0,1:T(8,128)} %get-tuple-element.13, f32[3,1024]{0,1:T(8,128)S(1)} %convert_element_type.81, f32[1024]{0:T(1024)S(1)} %bitcast.122, f32[1024]{0:T(1024)S(1)} %bitcast.123, f32[1024]{0:T(1024)S(1)} %bitcast.124, f32[1024]{0:T(1024)S(1)} %bitcast.121), kind=kLoop, calls=%fused_computation.37 | loop fusion | flops 7340032 | bytes 4222976 | tf_op jit(solution)/shard_map/jit(silu)/mul | solution.py:287
  322.8 39.0 %delta_chunks.1 = (f32[4,512,256]{2,1,0:T(8,128)}, f32[4,128,256]{2,1,0:T(8,128)}) custom-call(f32[4,512,128]{2,1,0:T(8,128)} %bitcast.116, f32[4,512,128]{2,1,0:T(8,128)} %bitcast.117, f32[4,512,128]{2,1,0:T(8,128)} %bitcast.115, f32[4,512,1]{2,1,0:T(8,128)} %copy.148.b_ref, f32[4,512,1]{2,1,0:T(8,128)} %reshape.166.cc_ref, f32[4,2,256]{2,1,0:T(2,128)} %reshape.154.cg_ref, ...), custom_call_target="tpu_custom_call" | custom-call | tf_op jit(solution)/shard_map/delta_chunks/pallas_call | solution.py:111
  363.7 6.4 %collective-permute-done.1 = f32[4,128,256]{2,1,0:T(8,128)S(1)} collective-permute-done((f32[4,128,256]{2,1,0:T(8,128)}, f32[4,128,256]{2,1,0:T(8,128)S(1)}, u32[]{:S(2)}, u32[]{:S(2)}) %collective-permute-start.1) | collective-permute-done | bytes 524320 | tf_op jit(solution)/shard_map/ppermute | solution.py:140
  371.9 4.0 collective-permute-start.2
  375.9 9.2 %collective-permute-done.2 = f32[4,128,256]{2,1,0:T(8,128)} collective-permute-done((f32[4,128,256]{2,1,0:T(8,128)S(1)}, f32[4,128,256]{2,1,0:T(8,128)}, u32[]{:S(2)}, u32[]{:S(2)}) %collective-permute-start.2) | collective-permute-done | bytes 524320 | tf_op jit(solution)/shard_map/ppermute | solution.py:140
  386.7 5.5 %collective-permute-start.3 = (f32[4,128,256]{2,1,0:T(8,128)S(1)}, f32[4,128,256]{2,1,0:T(8,128)S(1)}, u32[]{:S(2)}, u32[]{:S(2)}) collective-permute-start(f32[4,128,256]{2,1,0:T(8,128)S(1)} %fusion.39), channel_id=1, source_target_pairs={{0,16},{4,20},{8,24},{12,28},{16,32},{20,36},{24,40},{28,44},{32,4... | collective-permute-start | bytes 1572872 | tf_op jit(solution)/shard_map/ppermute | solution.py:140
  392.3 8.5 %collective-permute-done.3 = f32[4,128,256]{2,1,0:T(8,128)S(1)} collective-permute-done((f32[4,128,256]{2,1,0:T(8,128)S(1)}, f32[4,128,256]{2,1,0:T(8,128)S(1)}, u32[]{:S(2)}, u32[]{:S(2)}) %collective-permute-start.3) | collective-permute-done | bytes 524320 | tf_op jit(solution)/shard_map/ppermute | solution.py:140
  402.5 4.4 collective-permute-start.4
  406.9 5.3 %collective-permute-done.4 = f32[4,128,256]{2,1,0:T(8,128)} collective-permute-done((f32[4,128,256]{2,1,0:T(8,128)S(1)}, f32[4,128,256]{2,1,0:T(8,128)}, u32[]{:S(2)}, u32[]{:S(2)}) %collective-permute-start.4) | collective-permute-done | bytes 524320 | tf_op jit(solution)/shard_map/ppermute | solution.py:140
  413.9 5.5 %collective-permute-start.5 = (f32[4,128,128]{2,1,0:T(8,128)S(1)}, f32[4,128,128]{2,1,0:T(8,128)S(1)}, u32[]{:S(2)}, u32[]{:S(2)}) collective-permute-start(f32[4,128,128]{2,1,0:T(8,128)S(1)} %slice.117), channel_id=1, source_target_pairs={{0,64},{4,68},{8,72},{12,76},{16,80},{20,84},{24,88},{28,92},{32,9... | collective-permute-start | bytes 786440 | tf_op jit(solution)/shard_map/ppermute | solution.py:140
  423.7 11.2 %collective-permute-start.6 = (f32[4,128,128]{2,1,0:T(8,128)}, f32[4,128,128]{2,1,0:T(8,128)S(1)}, u32[]{:S(2)}, u32[]{:S(2)}) collective-permute-start(f32[4,128,128]{2,1,0:T(8,128)} %fusion.41), channel_id=1, source_target_pairs={{0,4},{4,8},{8,12},{12,16},{16,20},{20,24},{24,28},{28,32},{32,36}... | collective-permute-start | bytes 786440 | tf_op jit(solution)/shard_map/ppermute | solution.py:140
  434.9 4.3 convolution_convert_fusion.2
  448.5 28.8 %reduce-scatter.2.cloned.1.call-done = bf16[128,2048]{1,0:T(8,128)(2,1)} async-done(((bf16[512,2048]{1,0:T(8,128)(2,1)}), bf16[128,2048]{1,0:T(8,128)(2,1)}) %reduce-scatter.2.cloned.1.call-update) | async-done | bytes 524304 | tf_op jit(solution)/shard_map/reduce_scatter | solution.py:318
  (125 shorter events, 72.4 us)
Async XLA Ops:
  7.2 438.7 %copy-start = (bf16[512,2048]{1,0:T(8,128)(2,1)S(1)}, bf16[512,2048]{1,0:T(8,128)(2,1)}, u32[]{:S(2)}) copy-start(bf16[512,2048]{1,0:T(8,128)(2,1)} %param.41) | copy-start | bytes 6291460
  30.3 90.1 %copy-start.18 = (bf16[2,2048,512]{2,1,0:T(8,128)(2,1)S(1)}, bf16[2,2048,512]{2,1,0:T(8,128)(2,1)}, u32[]{:S(2)}) copy-start(bf16[2,2048,512]{2,1,0:T(8,128)(2,1)} %param.26) | copy-start | bytes 12582916
  117.8 2.6 copy-start.5
  161.4 5.0 %copy-start.13 = (f32[2048]{0:T(1024)S(1)}, f32[2048]{0:T(1024)}, u32[]{:S(2)}) copy-start(f32[2048]{0:T(1024)} %param.22) | copy-start | bytes 24580
  161.4 82.0 %all-to-all-start.1 = ((bf16[128,2,6,2048]{3,1,2,0:T(2,128)(2,1)}), bf16[128,2,6,2048]{3,1,2,0:T(2,128)(2,1)}, u32[]{:S(2)}, u32[]{:S(2)}) async-start(bf16[128,2,6,2048]{3,1,2,0:T(2,128)(2,1)} %copy.143), calls=%async_computation.1 | async-start | bytes 12582912 | tf_op jit(solution)/shard_map/all_to_all | solution.py:237
  166.3 116.8 %all-gather.2.cloned.1.call-start = ((), (), s32[]{:S(2)}) async-start(), calls=%async_computation.3 | async-start | bytes 2621440 | tf_op jit(solution)/shard_map/all_gather | solution.py:264
  252.4 2.3 copy-start.12
  252.4 2.3 copy-start.21
  254.5 222.7 %reduce-scatter.2.cloned.1.call-start = ((), (), s32[]{:S(2)}) async-start(), calls=%async_computation.4 | async-start | bytes 2621440 | tf_op jit(solution)/shard_map/reduce_scatter | solution.py:318
  283.1 3.7 copy-start.3
  283.1 3.7 copy-start.19
  288.8 5.6 %copy-start.9 = (bf16[2048,4]{0,1:T(4,128)(2,1)S(1)}, bf16[2048,4]{0,1:T(4,128)(2,1)}, u32[]{:S(2)}) copy-start(bf16[2048,4]{0,1:T(4,128)(2,1)} %param.34) | copy-start | bytes 49156
  288.8 5.6 %copy-start.16 = (f32[4]{0:T(128)S(1)}, f32[4]{0:T(128)}, u32[]{:S(2)}) copy-start(f32[4]{0:T(128)} %param.39) | copy-start | bytes 52
  290.5 5.6 %copy-start.10 = (bf16[2048,4]{0,1:T(4,128)(2,1)S(1)}, bf16[2048,4]{0,1:T(4,128)(2,1)}, u32[]{:S(2)}) copy-start(bf16[2048,4]{0,1:T(4,128)(2,1)} %param.33) | copy-start | bytes 49156
  290.6 13.9 %collective-permute-start = (bf16[3,1024]{0,1:T(8,128)(2,1)S(1)}, bf16[3,1024]{0,1:T(8,128)(2,1)S(1)}, u32[]{:S(2)}, u32[]{:S(2)}) collective-permute-start(bf16[3,1024]{0,1:T(8,128)(2,1)S(1)} %slice.102), channel_id=1, source_target_pairs={{0,4},{4,8},{8,12},{12,16},{16,20},{20,24},{24,28},{28,32},{32,36}... | collective-permute-start | bytes 18440 | tf_op jit(solution)/shard_map/ppermute | solution.py:135
  313.0 4.2 slice-start
  361.8 8.3 %collective-permute-start.1 = (f32[4,128,256]{2,1,0:T(8,128)}, f32[4,128,256]{2,1,0:T(8,128)S(1)}, u32[]{:S(2)}, u32[]{:S(2)}) collective-permute-start(f32[4,128,256]{2,1,0:T(8,128)} %get-tuple-element.5), channel_id=1, source_target_pairs={{0,4},{4,8},{8,12},{12,16},{16,20},{20,24},{24,28},{28,32},{32,36}... | collective-permute-start | bytes 1572872 | tf_op jit(solution)/shard_map/ppermute | solution.py:140
  371.9 13.2 %collective-permute-start.2 = (f32[4,128,256]{2,1,0:T(8,128)S(1)}, f32[4,128,256]{2,1,0:T(8,128)}, u32[]{:S(2)}, u32[]{:S(2)}) collective-permute-start(f32[4,128,256]{2,1,0:T(8,128)S(1)} %fusion.40), channel_id=1, source_target_pairs={{0,8},{4,12},{8,16},{12,20},{16,24},{20,28},{24,32},{28,36},{32,40... | collective-permute-start | bytes 1572872 | tf_op jit(solution)/shard_map/ppermute | solution.py:140
  386.7 5.5 %copy-start.7 = (f32[4,128,256]{2,1,0:T(8,128)}, f32[4,128,256]{2,1,0:T(8,128)S(1)}, u32[]{:S(2)}) copy-start(f32[4,128,256]{2,1,0:T(8,128)S(1)} %fusion.39) | copy-start | bytes 1572868
  386.7 14.0 %collective-permute-start.3 = (f32[4,128,256]{2,1,0:T(8,128)S(1)}, f32[4,128,256]{2,1,0:T(8,128)S(1)}, u32[]{:S(2)}, u32[]{:S(2)}) collective-permute-start(f32[4,128,256]{2,1,0:T(8,128)S(1)} %fusion.39), channel_id=1, source_target_pairs={{0,16},{4,20},{8,24},{12,28},{16,32},{20,36},{24,40},{28,44},{32,4... | collective-permute-start | bytes 1572872 | tf_op jit(solution)/shard_map/ppermute | solution.py:140
  402.5 9.7 %collective-permute-start.4 = (f32[4,128,256]{2,1,0:T(8,128)S(1)}, f32[4,128,256]{2,1,0:T(8,128)}, u32[]{:S(2)}, u32[]{:S(2)}) collective-permute-start(f32[4,128,256]{2,1,0:T(8,128)S(1)} %fusion.38), channel_id=1, source_target_pairs={{0,32},{4,36},{8,40},{12,44},{16,48},{20,52},{24,56},{28,60},{32,6... | collective-permute-start | bytes 1572872 | tf_op jit(solution)/shard_map/ppermute | solution.py:140
  413.9 8.7 %collective-permute-start.5 = (f32[4,128,128]{2,1,0:T(8,128)S(1)}, f32[4,128,128]{2,1,0:T(8,128)S(1)}, u32[]{:S(2)}, u32[]{:S(2)}) collective-permute-start(f32[4,128,128]{2,1,0:T(8,128)S(1)} %slice.117), channel_id=1, source_target_pairs={{0,64},{4,68},{8,72},{12,76},{16,80},{20,84},{24,88},{28,92},{32,9... | collective-permute-start | bytes 786440 | tf_op jit(solution)/shard_map/ppermute | solution.py:140
  423.7 16.8 %collective-permute-start.6 = (f32[4,128,128]{2,1,0:T(8,128)}, f32[4,128,128]{2,1,0:T(8,128)S(1)}, u32[]{:S(2)}, u32[]{:S(2)}) collective-permute-start(f32[4,128,128]{2,1,0:T(8,128)} %fusion.41), channel_id=1, source_target_pairs={{0,4},{4,8},{8,12},{12,16},{16,20},{20,24},{24,28},{28,32},{32,36}... | collective-permute-start | bytes 786440 | tf_op jit(solution)/shard_map/ppermute | solution.py:140
  439.3 4.2 copy-start.17
  (9 other events, 13.9 us)
Sparse Core Ops, SparseCore 0:
  254.7 28.4 all-gather.1
  448.6 28.6 reduce-scatter.1

commit v9 on v8

--- a/solution.py
+++ b/solution.py
@@ -153,15 +153,15 @@
         reached = place >= steps
         transfer = pair[..., value_width:]
         if 2 * steps < count:
-            far = shifted(pair, axis, steps)
+            far = shifted(pair.astype(jnp.bfloat16), axis, steps).astype(jnp.float32)
             joined = batched_mm(transfer, far) + jnp.where(offset_lanes, pair, 0.0)
             pair = jnp.where(reached, joined, pair)
         else:
-            far = shifted(pair[..., :value_width], axis, steps)
+            far = shifted(pair[..., :value_width].astype(jnp.bfloat16), axis, steps).astype(jnp.float32)
             offset = pair[..., :value_width]
             offset = jnp.where(reached, offset + batched_mm(transfer, far), offset)
         steps *= 2
-    return shifted(offset, axis, 1)
+    return shifted(offset.astype(jnp.bfloat16), axis, 1).astype(jnp.float32)
 
 
 def rms_rows(values, gain):

time: 490 us -> 472 us (0.963)
  waiting for transfers between devices: 157 us -> 144 us
    ppermute x6, waiting for transfers between devices: 32.6 us -> 15.7 us  [shifted(): lax.ppermute(value, axis, [(source, source + steps) for source in range(c...]
where the time goes in v9:
time: 472 us; the launch traced here: 466 us
  waiting for transfers between devices  144 us (31%)
  blocking collectives  87.4 us (19%)
  matrix products  63.6 us (13%)
  local copies, waits for them, and re-layouts  56.4 us (12%)
  Pallas kernels  39 us (8%)
  starting transfers between devices  38.2 us (8%)
  other arithmetic  22.2 us (5%)
  between operations  14.9 us (3%)
    all_to_all x1, blocking collectives, on_device(): lax.all_to_all(outgoing, ('ctx', 'head'), split_axis=0, concat_axis=0, ti...  87.4 us
    all_to_all x1, waiting for transfers between devices, on_device(): lax.all_to_all(jnp.einsum('nesh,ehd->nesd', hidden, expert_down, preferre...  67.3 us
    pallas_call x1, Pallas kernels, local_delta(): pl.pallas_call(delta_kernel, grid=(1,), in_specs=[whole(heads, length, kw...  39 us
    reduce_scatter x1, waiting for transfers between devices, on_device(): lax.psum_scatter(jnp.dot(gated_out, out_weight, preferred_element_type=jn...  32.7 us
    ppermute x6, starting transfers between devices, shifted(): lax.ppermute(value, axis, [(source, source + steps) for source in range(c...  29.4 us
    all_gather x1, waiting for transfers between devices, on_device(): piece_rows = lax.all_gather(mixer_in, 'head', axis=0, tiled=True)  28.4 us
    dot_general x1, matrix products, on_device(): jnp.einsum('nesh,ehd->nesd', hidden, expert_down, preferred_element_type=...  19.6 us
    ppermute x6, waiting for transfers between devices, shifted(): lax.ppermute(value, axis, [(source, source + steps) for source in range(c...  15.7 us
  transfers between devices with their start and end apart: 10, of which 8 were waited for; matrix products, arithmetic and copies ran while one was open for 5% of the time, Pallas kernels for 0%

profile of v9, /device:TPU:1, one launch (start us, length us, event | category | flops | bytes accessed | tf_op | source)
XLA Modules:
  0.0 465.9 jit_solution(13573470390509050833)
XLA Ops:
  17.4 13.0 %copy.140 = bf16[128,2,6,2048]{3,1,2,0:T(2,128)(2,1)S(1)} copy(bf16[128,2,6,2048]{3,0,2,1:T(8,128)(2,1)S(1)} %convolution_convert_fusion) | data formatting | bytes 12582912 | tf_op jit(solution)/shard_map/convert_element_type | solution.py:230
  30.4 87.4 %all_to_all.10 = bf16[128,2,6,2048]{3,1,2,0:T(2,128)(2,1)S(1)} all-to-all(bf16[128,2,6,2048]{3,1,2,0:T(2,128)(2,1)S(1)} %copy.140), channel_id=1, replica_groups=mesh['ctx'=32,'head'=4] {'ctx','head'}, dimensions={0} | all-to-all | bytes 12582912 | tf_op jit(solution)/shard_map/all_to_all | solution.py:231
  120.4 8.6 %fusion.2 = f32[2,128,6,512]{3,1,2,0:T(8,128)} fusion(bf16[128,2,6,2048]{3,1,2,0:T(2,128)(2,1)S(1)} %all_to_all.10, bf16[2,2048,512]{2,1,0:T(8,128)(2,1)S(1)} %copy-done.17), kind=kOutput, calls=%fused_computation.7 | convolution fusion | flops 3221225472 | bytes 13631488 | tf_op jit(solution)/shard_map/nesd,edh->nesh/dot_general | solution.py:235
  129.0 19.6 %convert_bitcast_fusion = bf16[128,2,6,2048]{3,0,2,1:T(8,128)(2,1)} fusion(bf16[2,512,2048]{2,1,0:T(8,128)(2,1)} %param.27, f32[2,128,6,512]{3,1,2,0:T(8,128)} %fusion.2, bf16[2,2048,512]{2,1,0:T(8,128)(2,1)} %param.25, bf16[128,2,6,2048]{3,1,2,0:T(2,128)(2,1)} %copy-done.5), kind=kOutput, calls=%fused_computation.6 | convolution fusion | flops 6450315264 | bytes 24117248 | tf_op jit(solution)/shard_map/nesh,ehd->nesd/dot_general | solution.py:238
  148.6 12.7 %copy.143 = bf16[128,2,6,2048]{3,1,2,0:T(2,128)(2,1)} copy(bf16[128,2,6,2048]{3,0,2,1:T(8,128)(2,1)} %convert_bitcast_fusion) | data formatting | bytes 12582912 | tf_op jit(solution)/shard_map/convert_element_type | solution.py:240
  161.4 4.9 %all-to-all-start.1 = ((bf16[128,2,6,2048]{3,1,2,0:T(2,128)(2,1)}), bf16[128,2,6,2048]{3,1,2,0:T(2,128)(2,1)}, u32[]{:S(2)}, u32[]{:S(2)}) async-start(bf16[128,2,6,2048]{3,1,2,0:T(2,128)(2,1)} %copy.143), calls=%async_computation.1 | async-start | bytes 12582912 | tf_op jit(solution)/shard_map/all_to_all | solution.py:237
  176.1 67.3 %all-to-all-done.1 = bf16[128,2,6,2048]{3,1,2,0:T(2,128)(2,1)} async-done(((bf16[128,2,6,2048]{3,1,2,0:T(2,128)(2,1)}), bf16[128,2,6,2048]{3,1,2,0:T(2,128)(2,1)}, u32[]{:S(2)}, u32[]{:S(2)}) %all-to-all-start.1) | async-done | bytes 6291488 | tf_op jit(solution)/shard_map/all_to_all | solution.py:237
  243.3 8.9 %fusion.13 = f32[256,2048]{1,0:T(8,128)S(1)} fusion(bf16[128,2,6,2048]{3,1,2,0:T(2,128)(2,1)} %all-to-all-done.1, bf16[128,128,2,6]{1,0,3,2:T(8,128)(2,1)} %get-tuple-element.15, bf16[128,128,2,6]{1,0,3,2:T(8,128)(2,1)} %get-tuple-element.14), kind=kOutput, calls=%fused_computation.25 | convolution fusion | flops 1612185600 | bytes 9175040 | tf_op jit(solution)/shard_map/tnes,nesd->td/dot_general | solution.py:253
  254.7 28.4 %all-gather.2.cloned.1.call-done = bf16[512,2048]{1,0:T(8,128)(2,1)} async-done(((bf16[128,2048]{1,0:T(8,128)(2,1)}), bf16[512,2048]{1,0:T(8,128)(2,1)}) %all-gather.2.cloned.1.call-update) | async-done | bytes 2097168 | tf_op jit(solution)/shard_map/all_gather | solution.py:264
  283.1 3.7 convolution_convert_fusion.3
  290.6 3.7 collective-permute-start
  304.6 6.8 %divide_multiply_fusion = f32[512,1024]{0,1:T(8,128)S(1)} fusion(f32[512,1024]{0,1:T(8,128)} %get-tuple-element.13, f32[3,1024]{0,1:T(8,128)S(1)} %convert_element_type.105, f32[1024]{0:T(1024)S(1)} %bitcast.122, f32[1024]{0:T(1024)S(1)} %bitcast.123, f32[1024]{0:T(1024)S(1)} %bitcast.124, f32[1024]{0:T(1024)S(1)} %bitcast.121), kind=kLoop, calls=%fused_computation.37 | loop fusion | flops 7340032 | bytes 4222976 | tf_op jit(solution)/shard_map/jit(silu)/mul | solution.py:287
  322.8 39.0 %delta_chunks.1 = (f32[4,512,256]{2,1,0:T(8,128)}, f32[4,128,256]{2,1,0:T(8,128)}) custom-call(f32[4,512,128]{2,1,0:T(8,128)} %bitcast.116, f32[4,512,128]{2,1,0:T(8,128)} %bitcast.117, f32[4,512,128]{2,1,0:T(8,128)} %bitcast.115, f32[4,512,1]{2,1,0:T(8,128)} %copy.148.b_ref, f32[4,512,1]{2,1,0:T(8,128)} %reshape.166.cc_ref, f32[4,2,256]{2,1,0:T(2,128)} %reshape.154.cg_ref, ...), custom_call_target="tpu_custom_call" | custom-call | tf_op jit(solution)/shard_map/delta_chunks/pallas_call | solution.py:111
  364.8 3.3 collective-permute-done.1
  369.6 3.2 collective-permute-start.2
  372.8 4.2 collective-permute-done.2
  378.2 5.2 %collective-permute-start.3 = (bf16[4,128,256]{2,1,0:T(8,128)(2,1)S(1)}, bf16[4,128,256]{2,1,0:T(8,128)(2,1)S(1)}, u32[]{:S(2)}, u32[]{:S(2)}) collective-permute-start(bf16[4,128,256]{2,1,0:T(8,128)(2,1)S(1)} %get-tuple-element.22), channel_id=1, source_target_pairs={{0,16},{4,20},{8,24},{12,28},{16,32},{20,36},{24,40},{28,44},{32,4... | collective-permute-start | bytes 786440 | tf_op jit(solution)/shard_map/ppermute | solution.py:140
  383.4 3.3 collective-permute-done.3
  388.2 6.0 %collective-permute-start.4 = (bf16[4,128,256]{2,1,0:T(8,128)(2,1)S(1)}, bf16[4,128,256]{2,1,0:T(8,128)(2,1)S(1)}, u32[]{:S(2)}, u32[]{:S(2)}) collective-permute-start(bf16[4,128,256]{2,1,0:T(8,128)(2,1)S(1)} %get-tuple-element.24), channel_id=1, source_target_pairs={{0,32},{4,36},{8,40},{12,44},{16,48},{20,52},{24,56},{28,60},{32,6... | collective-permute-start | bytes 786440 | tf_op jit(solution)/shard_map/ppermute | solution.py:140
  394.2 3.3 collective-permute-done.4
  397.9 5.6 %collective-permute-start.5 = (bf16[4,128,128]{2,1,0:T(8,128)(2,1)S(1)}, bf16[4,128,128]{2,1,0:T(8,128)(2,1)S(1)}, u32[]{:S(2)}, u32[]{:S(2)}) collective-permute-start(bf16[4,128,128]{2,1,0:T(8,128)(2,1)S(1)} %slice.176), channel_id=1, source_target_pairs={{0,64},{4,68},{8,72},{12,76},{16,80},{20,84},{24,88},{28,92},{32,9... | collective-permute-start | bytes 393224 | tf_op jit(solution)/shard_map/ppermute | solution.py:140
  405.4 7.6 %collective-permute-start.6 = (bf16[4,128,128]{2,1,0:T(8,128)(2,1)S(1)}, bf16[4,128,128]{2,1,0:T(8,128)(2,1)S(1)}, u32[]{:S(2)}, u32[]{:S(2)}) collective-permute-start(bf16[4,128,128]{2,1,0:T(8,128)(2,1)S(1)} %fusion.42), channel_id=1, source_target_pairs={{0,4},{4,8},{8,12},{12,16},{16,20},{20,24},{24,28},{28,32},{32,36}... | collective-permute-start | bytes 393224 | tf_op jit(solution)/shard_map/ppermute | solution.py:140
  413.1 4.3 convolution_convert_fusion.2
  426.2 32.7 %reduce-scatter.2.cloned.1.call-done = bf16[128,2048]{1,0:T(8,128)(2,1)} async-done(((bf16[512,2048]{1,0:T(8,128)(2,1)}), bf16[128,2048]{1,0:T(8,128)(2,1)}) %reduce-scatter.2.cloned.1.call-update) | async-done | bytes 524304 | tf_op jit(solution)/shard_map/reduce_scatter | solution.py:318
  (124 shorter events, 68.4 us)
Async XLA Ops:
  7.2 416.4 %copy-start = (bf16[512,2048]{1,0:T(8,128)(2,1)S(1)}, bf16[512,2048]{1,0:T(8,128)(2,1)}, u32[]{:S(2)}) copy-start(bf16[512,2048]{1,0:T(8,128)(2,1)} %param.41) | copy-start | bytes 6291460
  30.4 90.1 %copy-start.17 = (bf16[2,2048,512]{2,1,0:T(8,128)(2,1)S(1)}, bf16[2,2048,512]{2,1,0:T(8,128)(2,1)}, u32[]{:S(2)}) copy-start(bf16[2,2048,512]{2,1,0:T(8,128)(2,1)} %param.26) | copy-start | bytes 12582916
  117.8 2.6 copy-start.5
  161.4 5.0 %copy-start.12 = (f32[2048]{0:T(1024)S(1)}, f32[2048]{0:T(1024)}, u32[]{:S(2)}) copy-start(f32[2048]{0:T(1024)} %param.22) | copy-start | bytes 24580
  161.4 82.0 %all-to-all-start.1 = ((bf16[128,2,6,2048]{3,1,2,0:T(2,128)(2,1)}), bf16[128,2,6,2048]{3,1,2,0:T(2,128)(2,1)}, u32[]{:S(2)}, u32[]{:S(2)}) async-start(bf16[128,2,6,2048]{3,1,2,0:T(2,128)(2,1)} %copy.143), calls=%async_computation.1 | async-start | bytes 12582912 | tf_op jit(solution)/shard_map/all_to_all | solution.py:237
  166.3 116.8 %all-gather.2.cloned.1.call-start = ((), (), s32[]{:S(2)}) async-start(), calls=%async_computation.3 | async-start | bytes 2621440 | tf_op jit(solution)/shard_map/all_gather | solution.py:264
  252.3 2.3 copy-start.14
  252.3 2.3 copy-start.11
  252.3 2.3 copy-start.20
  254.5 204.3 %reduce-scatter.2.cloned.1.call-start = ((), (), s32[]{:S(2)}) async-start(), calls=%async_computation.4 | async-start | bytes 2621440 | tf_op jit(solution)/shard_map/reduce_scatter | solution.py:318
  283.1 3.7 copy-start.3
  283.1 3.7 copy-start.18
  288.8 5.6 %copy-start.8 = (bf16[2048,4]{0,1:T(4,128)(2,1)S(1)}, bf16[2048,4]{0,1:T(4,128)(2,1)}, u32[]{:S(2)}) copy-start(bf16[2048,4]{0,1:T(4,128)(2,1)} %param.34) | copy-start | bytes 49156
  288.8 5.6 %copy-start.15 = (f32[4]{0:T(128)S(1)}, f32[4]{0:T(128)}, u32[]{:S(2)}) copy-start(f32[4]{0:T(128)} %param.39) | copy-start | bytes 52
  290.4 5.5 %copy-start.9 = (bf16[2048,4]{0,1:T(4,128)(2,1)S(1)}, bf16[2048,4]{0,1:T(4,128)(2,1)}, u32[]{:S(2)}) copy-start(bf16[2048,4]{0,1:T(4,128)(2,1)} %param.33) | copy-start | bytes 49156
  290.6 13.9 %collective-permute-start = (bf16[3,1024]{0,1:T(8,128)(2,1)S(1)}, bf16[3,1024]{0,1:T(8,128)(2,1)S(1)}, u32[]{:S(2)}, u32[]{:S(2)}) collective-permute-start(bf16[3,1024]{0,1:T(8,128)(2,1)S(1)} %slice.102), channel_id=1, source_target_pairs={{0,4},{4,8},{8,12},{12,16},{16,20},{20,24},{24,28},{28,32},{32,36}... | collective-permute-start | bytes 18440 | tf_op jit(solution)/shard_map/ppermute | solution.py:135
  313.0 4.2 slice-start
  362.9 5.2 %collective-permute-start.1 = (bf16[4,128,256]{2,1,0:T(8,128)(2,1)S(1)}, bf16[4,128,256]{2,1,0:T(8,128)(2,1)S(1)}, u32[]{:S(2)}, u32[]{:S(2)}) collective-permute-start(bf16[4,128,256]{2,1,0:T(8,128)(2,1)S(1)} %convert_element_type.107), channel_id=1, source_target_pairs={{0,4},{4,8},{8,12},{12,16},{16,20},{20,24},{24,28},{28,32},{32,36}... | collective-permute-start | bytes 786440 | tf_op jit(solution)/shard_map/ppermute | solution.py:140
  369.6 7.4 %collective-permute-start.2 = (bf16[4,128,256]{2,1,0:T(8,128)(2,1)S(1)}, bf16[4,128,256]{2,1,0:T(8,128)(2,1)S(1)}, u32[]{:S(2)}, u32[]{:S(2)}) collective-permute-start(bf16[4,128,256]{2,1,0:T(8,128)(2,1)S(1)} %get-tuple-element.20), channel_id=1, source_target_pairs={{0,8},{4,12},{8,16},{12,20},{16,24},{20,28},{24,32},{28,36},{32,40... | collective-permute-start | bytes 786440 | tf_op jit(solution)/shard_map/ppermute | solution.py:140
  378.2 8.4 %collective-permute-start.3 = (bf16[4,128,256]{2,1,0:T(8,128)(2,1)S(1)}, bf16[4,128,256]{2,1,0:T(8,128)(2,1)S(1)}, u32[]{:S(2)}, u32[]{:S(2)}) collective-permute-start(bf16[4,128,256]{2,1,0:T(8,128)(2,1)S(1)} %get-tuple-element.22), channel_id=1, source_target_pairs={{0,16},{4,20},{8,24},{12,28},{16,32},{20,36},{24,40},{28,44},{32,4... | collective-permute-start | bytes 786440 | tf_op jit(solution)/shard_map/ppermute | solution.py:140
  388.2 9.3 %collective-permute-start.4 = (bf16[4,128,256]{2,1,0:T(8,128)(2,1)S(1)}, bf16[4,128,256]{2,1,0:T(8,128)(2,1)S(1)}, u32[]{:S(2)}, u32[]{:S(2)}) collective-permute-start(bf16[4,128,256]{2,1,0:T(8,128)(2,1)S(1)} %get-tuple-element.24), channel_id=1, source_target_pairs={{0,32},{4,36},{8,40},{12,44},{16,48},{20,52},{24,56},{28,60},{32,6... | collective-permute-start | bytes 786440 | tf_op jit(solution)/shard_map/ppermute | solution.py:140
  397.9 7.3 %collective-permute-start.5 = (bf16[4,128,128]{2,1,0:T(8,128)(2,1)S(1)}, bf16[4,128,128]{2,1,0:T(8,128)(2,1)S(1)}, u32[]{:S(2)}, u32[]{:S(2)}) collective-permute-start(bf16[4,128,128]{2,1,0:T(8,128)(2,1)S(1)} %slice.176), channel_id=1, source_target_pairs={{0,64},{4,68},{8,72},{12,76},{16,80},{20,84},{24,88},{28,92},{32,9... | collective-permute-start | bytes 393224 | tf_op jit(solution)/shard_map/ppermute | solution.py:140
  405.4 13.2 %collective-permute-start.6 = (bf16[4,128,128]{2,1,0:T(8,128)(2,1)S(1)}, bf16[4,128,128]{2,1,0:T(8,128)(2,1)S(1)}, u32[]{:S(2)}, u32[]{:S(2)}) collective-permute-start(bf16[4,128,128]{2,1,0:T(8,128)(2,1)S(1)} %fusion.42), channel_id=1, source_target_pairs={{0,4},{4,8},{8,12},{12,16},{16,20},{20,24},{24,28},{28,32},{32,36}... | collective-permute-start | bytes 393224 | tf_op jit(solution)/shard_map/ppermute | solution.py:140
  417.4 3.7 copy-start.16
  (8 other events, 11.7 us)
Sparse Core Ops, SparseCore 0:
  254.6 28.4 all-gather.1
  426.3 32.5 reduce-scatter.1
